TPU v7x, 32 devices: a whole 2x2x4 slice. The times are simulated.
32 devices in a mesh: fsdp: 8 (over z, x), tp: 4 (over y, core).
Axes of the slice: x: 2, y: 2, z: 4, core: 2. Of those that a mesh axis runs over, the one named last changes fastest.
Arguments:
- inputs: bfloat16 [32768, 512], P(('fsdp', 'tp')), may hold values from -6 to 6
- segments: int32 [8, 4096], P('fsdp', 'tp'), may hold values from 0 to 20, as said below
- out_grad: bfloat16 [32768, 512], P(('fsdp', 'tp')), may hold values from -6 to 6
- first_gain: bfloat16 [512], replicated, may hold values from 0.5 to 1.5
- first_shift: bfloat16 [512], replicated, may hold values from -3 to 3
- qkv_weight: bfloat16 [512, 3, 512], P('fsdp', None, 'tp'), may hold values from -0.375 to 0.375
- qv_bias: bfloat16 [2, 512], replicated, may hold values from -3 to 3
- out_weight: bfloat16 [512, 512], P('tp', 'fsdp'), may hold values from -1 to 1
- out_bias: bfloat16 [512], replicated, may hold values from -3 to 3
- second_gain: bfloat16 [512], replicated, may hold values from 0.5 to 1.5
- second_shift: bfloat16 [512], replicated, may hold values from -3 to 3
- fc_weight: bfloat16 [512, 2048], P('fsdp', 'tp'), may hold values from -0.25 to 0.25
- fc_bias: bfloat16 [2048], replicated, may hold values from -3 to 3
- proj_weight: bfloat16 [2048, 512], P('tp', 'fsdp'), may hold values from -0.125 to 0.125
- proj_bias: bfloat16 [512], replicated, may hold values from -3 to 3
Outputs:
- layer_out: bfloat16 [32768, 512], P(('fsdp', 'tp'))
- input_grad: bfloat16 [32768, 512], P(('fsdp', 'tp'))
- first_gain_grad: float32 [512], replicated
- first_shift_grad: float32 [512], replicated
- qkv_weight_grad: float32 [512, 3, 512], P('fsdp', None, 'tp')
- qv_bias_grad: float32 [2, 512], replicated
- out_weight_grad: float32 [512, 512], P('tp', 'fsdp')
- out_bias_grad: float32 [512], replicated
- second_gain_grad: float32 [512], replicated
- second_shift_grad: float32 [512], replicated
- fc_weight_grad: float32 [512, 2048], P('fsdp', 'tp')
- fc_bias_grad: float32 [2048], replicated
- proj_weight_grad: float32 [2048, 512], P('tp', 'fsdp')
- proj_bias_grad: float32 [512], replicated
Inputs may be any that keep to these rules, and one draw needn't show every extreme that they name: `segments`: along each sequence the numbers start at 1 and rise by one from document to document; each document has 200 to 2000 tokens, and in one sequence every document has exactly 200; 0 marks padding, which only follows the last whole document of a sequence.
All inputs are finite; a program needn't handle non-finite values.
Results may differ from a plain program's by a relative error of at most 0.018.
The roundings to bfloat16 on the way count: a program that leaves them out, or rounds other values in their place, can miss the bound.
Values may be sent and summed in bfloat16 or wider, within the bound.
A program may use at most 128 MiB of HBM per device.

v0:
```python
import jax
import jax.numpy as jnp
from jax import lax
from jax.sharding import PartitionSpec as P

HD = 64
FF = 2048


epsilon = 1e-05
gelu_slope = 1.702
masked_score = -1e30


def split_up(value, dim, peers):
    dims = value.shape
    pieces = value.reshape(*dims[:dim], peers, dims[dim] // peers, *dims[dim + 1 :])
    return jnp.moveaxis(pieces, dim, 0)


def sent_and_summed(value, axis, dim):
    pieces = split_up(value, dim, lax.axis_size(axis))
    arrived = lax.all_to_all(pieces, axis, split_axis=0, concat_axis=0, tiled=True)
    return arrived.astype(jnp.float32).sum(axis=0)


def layer_norm(values_in, gain_vec, shift_vec):
    mean_row = jnp.mean(values_in, axis=-1, keepdims=True)
    centred = values_in - mean_row
    inverse = lax.rsqrt(jnp.mean(centred * centred, axis=-1, keepdims=True) + epsilon)
    normed = centred * inverse
    return (normed * gain_vec + shift_vec, normed, inverse)


def norm_back(grad_out, normed, inverse, gain_vec):
    scaled = grad_out * gain_vec
    grad_in = inverse * (
        scaled
        - jnp.mean(scaled, axis=-1, keepdims=True)
        - normed * jnp.mean(scaled * normed, axis=-1, keepdims=True)
    )
    return (grad_in, jnp.sum(grad_out * normed, axis=0), jnp.sum(grad_out, axis=0))


def allowed(seg_query, pos_query, seg_key, pos_key):
    same_doc = seg_query[:, None] == seg_key[None, :]
    causal = pos_key[None, :] <= pos_query[:, None]
    living = (seg_query[:, None] != 0) | (pos_key[None, :] == pos_query[:, None])
    return same_doc & causal & living


def attend(queries, keys_all, values_all, seg_all, block_rows):
    seq_rows, heads_here, head_size = queries.shape
    blocks = seq_rows // block_rows
    positions = jnp.arange(seq_rows, dtype=jnp.int32)
    scale_factor = head_size ** (-0.5)

    def one_block(pieces):
        q_blk, seg_blk, pos_blk = pieces
        scores = (
            jnp.einsum("qhe,khe->hqk", q_blk, keys_all, preferred_element_type=jnp.float32)
            * scale_factor
        )
        allowed_mask = allowed(seg_blk, pos_blk, seg_all, positions)
        scores = jnp.where(allowed_mask[None], scores, masked_score)
        row_max = jnp.max(scores, axis=-1, keepdims=True)
        exp_scores = jnp.exp(scores - row_max)
        row_sum = jnp.sum(exp_scores, axis=-1, keepdims=True)
        softmax_w = (exp_scores / row_sum).astype(jnp.bfloat16)
        block_out = jnp.einsum(
            "hqk,khe->qhe", softmax_w, values_all, preferred_element_type=jnp.float32
        )
        return (block_out, (row_max + jnp.log(row_sum))[..., 0])

    block_outs, log_norm = lax.map(
        one_block,
        (
            queries.reshape(blocks, block_rows, heads_here, head_size),
            seg_all.reshape(blocks, block_rows),
            positions.reshape(blocks, block_rows),
        ),
    )
    return (block_outs.reshape(seq_rows, heads_here, head_size), log_norm)


def attend_back(queries, keys_all, values_all, grad_out, raw_out, log_norm, seg_all, block_rows):
    seq_rows, heads_here, head_size = queries.shape
    blocks = seq_rows // block_rows
    positions = jnp.arange(seq_rows, dtype=jnp.int32)
    scale_factor = head_size ** (-0.5)
    row_dot = jnp.sum(grad_out.astype(jnp.float32) * raw_out, axis=-1)

    def one_block(running, pieces):
        grad_keys, grad_values = running
        q_blk, g_blk, dot_blk, norm_blk, seg_blk, pos_blk = pieces
        scores = (
            jnp.einsum("qhe,khe->hqk", q_blk, keys_all, preferred_element_type=jnp.float32)
            * scale_factor
        )
        allowed_mask = allowed(seg_blk, pos_blk, seg_all, positions)
        scores = jnp.where(allowed_mask[None], scores, masked_score)
        softmax_f = jnp.exp(scores - norm_blk[..., None])
        grad_soft = jnp.einsum(
            "qhe,khe->hqk", g_blk, values_all, preferred_element_type=jnp.float32
        )
        grad_scores = (softmax_f * (grad_soft - dot_blk.T[..., None]) * scale_factor).astype(
            jnp.bfloat16
        )
        grad_q = jnp.einsum(
            "hqk,khe->qhe", grad_scores, keys_all, preferred_element_type=jnp.float32
        )
        grad_keys = grad_keys + jnp.einsum(
            "hqk,qhe->khe", grad_scores, q_blk, preferred_element_type=jnp.float32
        )
        grad_values = grad_values + jnp.einsum(
            "hqk,qhe->khe",
            softmax_f.astype(jnp.bfloat16),
            g_blk,
            preferred_element_type=jnp.float32,
        )
        return ((grad_keys, grad_values), grad_q)

    zero_state = jnp.zeros((seq_rows, heads_here, head_size), jnp.float32)
    (grad_keys, grad_values), grad_queries = lax.scan(
        one_block,
        (zero_state, zero_state),
        (
            queries.reshape(blocks, block_rows, heads_here, head_size),
            grad_out.reshape(blocks, block_rows, heads_here, head_size),
            row_dot.reshape(blocks, block_rows, heads_here),
            log_norm,
            seg_all.reshape(blocks, block_rows),
            positions.reshape(blocks, block_rows),
        ),
    )
    return (grad_queries.reshape(seq_rows, heads_here, head_size), grad_keys, grad_values)


def local(
    inputs,
    segments,
    out_grad,
    first_gain,
    first_shift,
    qkv_weight,
    qv_bias,
    out_weight,
    out_bias,
    second_gain,
    second_shift,
    fc_weight,
    fc_bias,
    proj_weight,
    proj_bias,
):
    tp_index = lax.axis_index("tp")
    qkv_full, out_full, fc_full, proj_full = (
        lax.all_gather(qkv_weight, "fsdp", axis=0, tiled=True),
        lax.all_gather(out_weight, "fsdp", axis=1, tiled=True),
        lax.all_gather(fc_weight, "fsdp", axis=0, tiled=True),
        lax.all_gather(proj_weight, "fsdp", axis=1, tiled=True),
    )
    model_width = inputs.shape[1]
    head_cols = qkv_full.shape[2]
    hidden_cols = fc_full.shape[1]
    heads_here = head_cols // HD
    resid_in = inputs.astype(jnp.float32)
    normed_one, hat_one, inv_one = layer_norm(
        resid_in, first_gain.astype(jnp.float32), first_shift.astype(jnp.float32)
    )
    lowered_one = normed_one.astype(jnp.bfloat16)
    seq_normed, seg_rows = (
        lax.all_gather(lowered_one, "tp", axis=0, tiled=True),
        lax.all_gather(segments, "tp", axis=1, tiled=True),
    )
    seg_all = seg_rows[0]
    seq_rows = seq_normed.shape[0]
    block_rows = min(512, seq_rows)
    projected = jnp.einsum("sd,dje->sje", seq_normed, qkv_full, preferred_element_type=jnp.float32)
    bias_here = lax.dynamic_slice_in_dim(qv_bias, tp_index * head_cols, head_cols, 1).astype(
        jnp.float32
    )
    queries = (
        (projected[:, 0] + bias_here[0]).astype(jnp.bfloat16).reshape(seq_rows, heads_here, HD)
    )
    keys_all = projected[:, 1].astype(jnp.bfloat16).reshape(seq_rows, heads_here, HD)
    values_all = (
        (projected[:, 2] + bias_here[1]).astype(jnp.bfloat16).reshape(seq_rows, heads_here, HD)
    )
    live_rows = (seg_all != 0).astype(jnp.float32)
    raw_out, log_norm = attend(queries, keys_all, values_all, seg_all, block_rows)
    attn_low = (
        (raw_out * live_rows[:, None, None]).astype(jnp.bfloat16).reshape(seq_rows, head_cols)
    )
    attn_sum = lax.psum_scatter(
        jnp.dot(attn_low, out_full, preferred_element_type=jnp.float32).astype(jnp.bfloat16),
        "tp",
        scatter_dimension=0,
        tiled=True,
    ).astype(jnp.float32)
    hidden = resid_in + attn_sum + out_bias.astype(jnp.float32)
    normed_two, hat_two, inv_two = layer_norm(
        hidden, second_gain.astype(jnp.float32), second_shift.astype(jnp.float32)
    )
    lowered_two = normed_two.astype(jnp.bfloat16)
    mlp_in = lax.all_gather(lowered_two, "tp", axis=0, tiled=True)
    fc_bias_here = lax.dynamic_slice_in_dim(fc_bias, tp_index * hidden_cols, hidden_cols, 0)
    pre_act = jnp.dot(mlp_in, fc_full, preferred_element_type=jnp.float32) + fc_bias_here.astype(
        jnp.float32
    )
    sigmoid_pre = jax.nn.sigmoid(gelu_slope * pre_act)
    act_low = (pre_act * sigmoid_pre).astype(jnp.bfloat16)
    mlp_sum = lax.psum_scatter(
        jnp.dot(act_low, proj_full, preferred_element_type=jnp.float32).astype(jnp.bfloat16),
        "tp",
        scatter_dimension=0,
        tiled=True,
    ).astype(jnp.float32)
    grad_rows = lax.all_gather(out_grad, "tp", axis=0, tiled=True)
    layer_out = (hidden + mlp_sum + proj_bias.astype(jnp.float32)).astype(jnp.bfloat16)
    proj_grad = jnp.einsum("sf,sd->fd", act_low, grad_rows, preferred_element_type=jnp.float32)
    grad_act = jnp.einsum("sd,fd->sf", grad_rows, proj_full, preferred_element_type=jnp.float32)
    grad_pre = grad_act * (sigmoid_pre + gelu_slope * pre_act * sigmoid_pre * (1.0 - sigmoid_pre))
    grad_pre_low = grad_pre.astype(jnp.bfloat16)
    fc_grad = jnp.einsum("sd,sf->df", mlp_in, grad_pre_low, preferred_element_type=jnp.float32)
    fc_bias_part = jnp.sum(grad_pre_low.astype(jnp.float32), axis=0)
    grad_normed_two = lax.psum_scatter(
        jnp.einsum("sf,df->sd", grad_pre_low, fc_full, preferred_element_type=jnp.float32).astype(
            jnp.bfloat16
        ),
        "tp",
        scatter_dimension=0,
        tiled=True,
    ).astype(jnp.float32)
    fc_bias_full = lax.dynamic_update_slice_in_dim(
        jnp.zeros((FF,), jnp.float32), fc_bias_part, tp_index * hidden_cols, 0
    )
    resid_grad = out_grad.astype(jnp.float32)
    grad_hidden_ln, second_gain_part, second_shift_part = norm_back(
        grad_normed_two, hat_two, inv_two, second_gain.astype(jnp.float32)
    )
    grad_hidden = resid_grad + grad_hidden_ln
    grad_hidden_low = grad_hidden.astype(jnp.bfloat16)
    out_bias_part = jnp.sum(grad_hidden_low.astype(jnp.float32), axis=0)
    proj_bias_part = jnp.sum(resid_grad, axis=0)
    seq_grad = lax.all_gather(grad_hidden_low, "tp", axis=0, tiled=True)
    out_w_grad = jnp.einsum("sc,sd->cd", attn_low, seq_grad, preferred_element_type=jnp.float32)
    grad_attn = jnp.einsum("sd,cd->sc", seq_grad, out_full, preferred_element_type=jnp.float32)
    grad_attn_low = (
        grad_attn.astype(jnp.bfloat16).reshape(seq_rows, heads_here, HD)
        * live_rows.astype(jnp.bfloat16)[:, None, None]
    )
    grad_q, grad_k, grad_v = attend_back(
        queries, keys_all, values_all, grad_attn_low, raw_out, log_norm, seg_all, block_rows
    )
    grad_qkv = (
        jnp.stack([grad_q, grad_k, grad_v], axis=1)
        .astype(jnp.bfloat16)
        .reshape(seq_rows, 3, head_cols)
    )
    qkv_w_grad = jnp.einsum("sd,sje->dje", seq_normed, grad_qkv, preferred_element_type=jnp.float32)
    qv_part = jnp.sum(grad_qkv[:, 0::2].astype(jnp.float32), axis=0)
    grad_normed_one = lax.psum_scatter(
        jnp.einsum("sje,dje->sd", grad_qkv, qkv_full, preferred_element_type=jnp.float32).astype(
            jnp.bfloat16
        ),
        "tp",
        scatter_dimension=0,
        tiled=True,
    ).astype(jnp.float32)
    qv_full = lax.dynamic_update_slice_in_dim(
        jnp.zeros((2, model_width), jnp.float32), qv_part, tp_index * head_cols, 1
    )
    grad_in_ln, first_gain_part, first_shift_part = norm_back(
        grad_normed_one, hat_one, inv_one, first_gain.astype(jnp.float32)
    )
    input_grad = (grad_hidden + grad_in_ln).astype(jnp.bfloat16)
    qkv_w_grad, out_w_grad, fc_grad, proj_grad = (
        sent_and_summed(qkv_w_grad.astype(jnp.bfloat16), "fsdp", 0),
        sent_and_summed(out_w_grad.astype(jnp.bfloat16), "fsdp", 1),
        sent_and_summed(fc_grad.astype(jnp.bfloat16), "fsdp", 0),
        sent_and_summed(proj_grad.astype(jnp.bfloat16), "fsdp", 1),
    )
    (
        first_gain_grad,
        first_shift_grad,
        qv_bias_grad,
        out_bias_grad,
        second_gain_grad,
        second_shift_grad,
        fc_bias_grad,
        proj_bias_grad,
    ) = lax.psum(
        (
            first_gain_part,
            first_shift_part,
            qv_full,
            out_bias_part,
            second_gain_part,
            second_shift_part,
            fc_bias_full,
            proj_bias_part,
        ),
        ("fsdp", "tp"),
    )
    return (
        layer_out,
        input_grad,
        first_gain_grad,
        first_shift_grad,
        qkv_w_grad,
        qv_bias_grad,
        out_w_grad,
        out_bias_grad,
        second_gain_grad,
        second_shift_grad,
        fc_grad,
        fc_bias_grad,
        proj_grad,
        proj_bias_grad,
    )


def solution(mesh):
    return jax.shard_map(
        local,
        mesh=mesh,
        in_specs=(
            P(("fsdp", "tp"), None),
            P("fsdp", "tp"),
            P(("fsdp", "tp"), None),
            P(),
            P(),
            P("fsdp", None, "tp"),
            P(),
            P("tp", "fsdp"),
            P(),
            P(),
            P(),
            P("fsdp", "tp"),
            P(),
            P("tp", "fsdp"),
            P(),
        ),
        out_specs=(
            P(("fsdp", "tp"), None),
            P(("fsdp", "tp"), None),
            P(),
            P(),
            P("fsdp", None, "tp"),
            P(),
            P("tp", "fsdp"),
            P(),
            P(),
            P(),
            P("fsdp", "tp"),
            P(),
            P("tp", "fsdp"),
            P(),
        ),
        check_vma=False,
    )
```

profile of v0, /device:TPU:0, one launch (start us, length us, event | category | flops | bytes accessed | tf_op | source)
XLA Modules:
  0.0 1055.4 jit_solution(14751792335652611730)
XLA Ops:
  23.5 33.3 %all_gather.30 = bf16[128,512]{0,1:T(8,128)(2,1)} all-gather(bf16[128,64]{0,1:T(8,128)(2,1)S(1)} %copy-done.28), channel_id=1, replica_groups=mesh['fsdp'=8,'tp'=4] {'fsdp'}, dimensions={1}, use_global_device_ids=true | all-gather | bytes 147456 | tf_op jit(solution)/shard_map/all_gather | solution.py:159
  56.8 31.0 %all_gather.29 = bf16[512,3,128]{2,0,1:T(8,128)(2,1)S(1)} all-gather(bf16[64,3,128]{2,0,1:T(8,128)(2,1)S(1)} %copy-done.26), channel_id=1, replica_groups=mesh['fsdp'=8,'tp'=4] {'fsdp'}, dimensions={0}, use_global_device_ids=true | all-gather | bytes 442368 | tf_op jit(solution)/shard_map/all_gather | solution.py:158
  97.2 209.7 %while.30 = (s32[]{:T(128)}, f32[8,512,2,64]{1,0,3,2:T(8,128)}, f32[8,2,512]{2,1,0:T(2,128)S(1)}, s32[8,512]{1,0:T(8,128)S(1)}, s32[1,4096]{1,0:T(1,128)S(1)}, /...) while((s32[]{:T(128)}, f32[8,512,2,64]{1,0,3,2:T(8,128)}, ...), condition=%wide.region_5.6_spmd.clone.clone, body=%wide.region_2.5_spmd.clone.clone.sunk | while | flops 1136655872 | bytes 62323844 | solution.py:75
  315.8 45.1 %reduce-scatter.5.cloned.1.call-done = bf16[1024,512]{1,0:T(8,128)(2,1)} async-done(((bf16[4096,512]{1,0:T(8,128)(2,1)}), bf16[1024,512]{1,0:T(8,128)(2,1)}) %reduce-scatter.5.cloned.1.call-update) | async-done | bytes 1048592 | tf_op jit(solution)/shard_map/reduce_scatter | solution.py:195
  367.5 33.6 %all_gather.32 = bf16[512,512]{1,0:T(8,128)(2,1)} all-gather(bf16[64,512]{1,0:T(8,128)(2,1)S(1)} %copy-done.24), channel_id=1, replica_groups=mesh['fsdp'=8,'tp'=4] {'fsdp'}, dimensions={0}, use_global_device_ids=true | all-gather | bytes 589824 | tf_op jit(solution)/shard_map/all_gather | solution.py:160
  401.1 33.5 %all_gather.33 = bf16[512,512]{0,1:T(8,128)(2,1)} all-gather(bf16[512,64]{0,1:T(8,128)(2,1)S(1)} %copy-done.25), channel_id=1, replica_groups=mesh['fsdp'=8,'tp'=4] {'fsdp'}, dimensions={1}, use_global_device_ids=true | all-gather | bytes 589824 | tf_op jit(solution)/shard_map/all_gather | solution.py:161
  434.6 10.4 multiply_convert_fusion.2
  445.0 9.5 convert_reduce_fusion
  468.5 37.4 %reduce-scatter.9.cloned.1.call-done = bf16[1024,512]{1,0:T(8,128)(2,1)} async-done(((bf16[4096,512]{1,0:T(8,128)(2,1)}), bf16[1024,512]{1,0:T(8,128)(2,1)}) %reduce-scatter.9.cloned.1.call-update) | async-done | bytes 1048592 | tf_op jit(solution)/shard_map/reduce_scatter | solution.py:227
  509.2 43.7 %reduce-scatter.7.cloned.1.call-done = bf16[1024,512]{1,0:T(8,128)(2,1)} async-done(((bf16[4096,512]{1,0:T(8,128)(2,1)}), bf16[1024,512]{1,0:T(8,128)(2,1)}) %reduce-scatter.7.cloned.1.call-update) | async-done | bytes 1048592 | tf_op jit(solution)/shard_map/reduce_scatter | solution.py:213
  557.9 34.5 %all-gather.11.cloned.1.call-done = bf16[4096,512]{1,0:T(8,128)(2,1)} async-done(((bf16[1024,512]{1,0:T(8,128)(2,1)}), bf16[4096,512]{1,0:T(8,128)(2,1)}) %all-gather.11.cloned.1.call-update) | async-done | bytes 4194320 | tf_op jit(solution)/shard_map/all_gather | solution.py:246
  602.7 301.0 %while.31 = (s32[]{:T(128)}, f32[4096,2,64]{0,2,1:T(8,128)S(1)}, f32[4096,2,64]{0,2,1:T(8,128)}, bf16[8,512,2,64]{1,3,2,0:T(8,128)(2,1)}, bf16[8,512,2,64]{1,3,2...) while((s32[]{:T(128)}, f32[4096,2,64]{0,2,1:T(8,128)S(1)}, ...), condition=%wide.region_15.16_spmd.clone.clone, body=%wide.region_14.15_spmd.clone.clone.sunk | while | flops 2745172480 | bytes 161287376 | solution.py:124
  623.7 10.5 multiply_convert_fusion.7
  661.3 10.5 multiply_convert_fusion.7
  698.9 10.5 multiply_convert_fusion.7
  736.5 10.5 multiply_convert_fusion.7
  774.1 10.5 multiply_convert_fusion.7
  811.7 10.5 multiply_convert_fusion.7
  849.3 10.5 multiply_convert_fusion.7
  886.9 10.5 multiply_convert_fusion.7
  943.1 8.3 all-to-all-done.3
  957.6 12.2 %all-to-all-done.2 = bf16[8,64,512]{2,1,0:T(8,128)(2,1)} async-done(((bf16[8,64,512]{2,1,0:T(8,128)(2,1)}), bf16[8,64,512]{2,1,0:T(8,128)(2,1)}, u32[]{:S(2)}, u32[]{:S(2)}) %all-to-all-start.2) | async-done | bytes 524320 | tf_op jit(solution)/shard_map/all_to_all | solution.py:23
  995.3 7.6 all-to-all-done
  1006.2 39.5 %all-reduce = (f32[512]{0:T(512)}, f32[512]{0:T(512)}, f32[2,512]{1,0:T(2,128)}, f32[512]{0:T(512)}, f32[512]{0:T(512)}, /*index=5*/f32[512]{0:T(512)}, f32[2048]{0:T(1024)}, f32[512]{0:T(512)}) all-reduce(f32[512]{0:T(512)S(1)} %get-tuple-element.300, ...), channel_id=1, replica_groups=mesh['fsdp'=8,'tp'=4] {'fsdp','tp'}, use_global_device_ids=true, to_apply=%region_20.21 | all-reduce | flops 6144 | bytes 49152 | tf_op jit(solution)/shard_map/psum | solution.py:293
  (343 shorter events, 574.5 us)
Async XLA Ops:
  7.2 16.3 %copy-start.28 = (bf16[128,64]{0,1:T(8,128)(2,1)S(1)}, bf16[128,64]{0,1:T(8,128)(2,1)}, u32[]{:S(2)}) copy-start(bf16[128,64]{0,1:T(8,128)(2,1)} %param.26) | copy-start | bytes 49156
  7.2 49.6 %copy-start.26 = (bf16[64,3,128]{2,0,1:T(8,128)(2,1)S(1)}, bf16[64,3,128]{2,0,1:T(8,128)(2,1)}, u32[]{:S(2)}) copy-start(bf16[64,3,128]{2,0,1:T(8,128)(2,1)} %param.24) | copy-start | bytes 147460
  7.2 81.2 %all-gather.5.cloned.1.call-start = ((), (), s32[]{:S(2)}) async-start(), calls=%async_computation.8 | async-start | bytes 5242880 | tf_op jit(solution)/shard_map/all_gather | solution.py:173
  15.1 345.9 %reduce-scatter.5.cloned.1.call-start = ((), (), s32[]{:S(2)}) async-start(), calls=%async_computation.9 | async-start | bytes 5242880 | tf_op jit(solution)/shard_map/reduce_scatter | solution.py:195
  315.1 45.9 %copy-start.1 = (bf16[1024,512]{1,0:T(8,128)(2,1)S(1)}, bf16[1024,512]{1,0:T(8,128)(2,1)}, u32[]{:S(2)}) copy-start(bf16[1024,512]{1,0:T(8,128)(2,1)} %param.19) | copy-start | bytes 3145732
  315.1 119.4 %all-gather.7.cloned.1.call-start = ((), (), s32[]{:S(2)}) async-start(), calls=%async_computation.10 | async-start | bytes 5242880 | tf_op jit(solution)/shard_map/all_gather | solution.py:206
  364.5 36.6 %copy-start.25 = (bf16[512,64]{0,1:T(8,128)(2,1)S(1)}, bf16[512,64]{0,1:T(8,128)(2,1)}, u32[]{:S(2)}) copy-start(bf16[512,64]{0,1:T(8,128)(2,1)} %param.32) | copy-start | bytes 196612
  366.1 78.9 %all-gather.9.cloned.1.call-start = ((), (), s32[]{:S(2)}) async-start(), calls=%async_computation.12 | async-start | bytes 5242880 | tf_op jit(solution)/shard_map/all_gather | solution.py:219
  366.7 139.2 %reduce-scatter.9.cloned.1.call-start = ((), (), s32[]{:S(2)}) async-start(), calls=%async_computation.13 | async-start | bytes 5242880 | tf_op jit(solution)/shard_map/reduce_scatter | solution.py:227
  461.0 91.9 %reduce-scatter.7.cloned.1.call-start = ((), (), s32[]{:S(2)}) async-start(), calls=%async_computation.11 | async-start | bytes 5242880 | tf_op jit(solution)/shard_map/reduce_scatter | solution.py:213
  467.8 124.6 %all-gather.11.cloned.1.call-start = ((), (), s32[]{:S(2)}) async-start(), calls=%async_computation.14 | async-start | bytes 5242880 | tf_op jit(solution)/shard_map/all_gather | solution.py:246
  557.8 445.8 %reduce-scatter.11.cloned.1.call-start = ((), (), s32[]{:S(2)}) async-start(), calls=%async_computation.15 | async-start | bytes 5242880 | tf_op jit(solution)/shard_map/reduce_scatter | solution.py:263
  930.8 20.5 %all-to-all-start.3 = ((bf16[8,512,64]{1,2,0:T(8,128)(2,1)}), bf16[8,512,64]{1,2,0:T(8,128)(2,1)}, u32[]{:S(2)}, u32[]{:S(2)}) async-start(bf16[8,512,64]{1,2,0:T(8,128)(2,1)} %bitcast.13), calls=%async_computation.7 | async-start | bytes 1048576 | tf_op jit(solution)/shard_map/all_to_all | solution.py:23
  936.3 19.2 %copy-start.31 = (f32[512]{0:T(512)S(1)}, f32[512]{0:T(512)}, u32[]{:S(2)}) copy-start(f32[512]{0:T(512)} %get-tuple-element.377) | copy-start | bytes 6148
  936.4 35.2 %copy-start.19 = (f32[1,4096]{1,0:T(1,128)S(1)}, f32[1,4096]{1,0:T(1,128)}, u32[]{:S(2)}) copy-start(f32[1,4096]{1,0:T(1,128)} %compare_convert_fusion) | copy-start | bytes 49156
  943.1 28.5 %copy-start.4 = (f32[16,8,8,512]{3,1,2,0:T(8,128)S(1)}, f32[16,8,8,512]{3,1,2,0:T(8,128)}, u32[]{:S(2)}) copy-start(f32[16,8,8,512]{3,1,2,0:T(8,128)} %copy-done.3) | copy-start | bytes 6291460
  951.3 18.4 %all-to-all-start.2 = ((bf16[8,64,512]{2,1,0:T(8,128)(2,1)}), bf16[8,64,512]{2,1,0:T(8,128)(2,1)}, u32[]{:S(2)}, u32[]{:S(2)}) async-start(bf16[8,64,512]{2,1,0:T(8,128)(2,1)} %bitcast.175), calls=%async_computation.6 | async-start | bytes 1048576 | tf_op jit(solution)/shard_map/all_to_all | solution.py:23
  975.2 11.0 %all-to-all-start.1 = ((bf16[8,128,64]{1,2,0:T(8,128)(2,1)}), bf16[8,128,64]{1,2,0:T(8,128)(2,1)S(1)}, u32[]{:S(2)}, u32[]{:S(2)}) async-start(bf16[8,128,64]{1,2,0:T(8,128)(2,1)} %bitcast.10), calls=%async_computation.5 | async-start | bytes 262144 | tf_op jit(solution)/shard_map/all_to_all | solution.py:23
  978.8 12.9 %copy-start.11 = (bf16[4096,1,128]{2,0,1:T(8,128)(2,1)S(1)}, bf16[4096,1,128]{2,0,1:T(8,128)(2,1)}, u32[]{:S(2)}) copy-start(bf16[4096,1,128]{2,0,1:T(8,128)(2,1)} %copy-done.10) | copy-start | bytes 3145732
  986.8 16.1 %all-to-all-start = ((bf16[8,64,3,128]{3,1,2,0:T(8,128)(2,1)}), bf16[8,64,3,128]{3,1,2,0:T(8,128)(2,1)S(1)}, u32[]{:S(2)}, u32[]{:S(2)}) async-start(bf16[8,64,3,128]{3,1,2,0:T(8,128)(2,1)} %copy.57), calls=%async_computation.4 | async-start | bytes 786432 | tf_op jit(solution)/shard_map/all_to_all | solution.py:23
  991.8 11.8 %copy-start.2 = (bf16[1024,512]{1,0:T(8,128)(2,1)S(1)}, bf16[1024,512]{1,0:T(8,128)(2,1)}, u32[]{:S(2)}) copy-start(bf16[1024,512]{1,0:T(8,128)(2,1)} %param.19) | copy-start | bytes 3145732
  991.8 11.8 %copy-start.21 = (f32[1024]{0:T(1024)S(1)}, f32[1024]{0:T(1024)}, u32[]{:S(2)}) copy-start(f32[1024]{0:T(1024)} %copy-done.20) | copy-start | bytes 12292
  991.8 11.8 %copy-start.23 = (f32[1024]{0:T(1024)S(1)}, f32[1024]{0:T(1024)}, u32[]{:S(2)}) copy-start(f32[1024]{0:T(1024)} %copy-done.22) | copy-start | bytes 12292
  993.5 52.1 %copy-start.6 = (f32[1024,512]{1,0:T(8,128)S(1)}, f32[1024,512]{1,0:T(8,128)}, u32[]{:S(2)}) copy-start(f32[1024,512]{1,0:T(8,128)} %get-tuple-element.362) | copy-start | bytes 6291460
  (32 other events, 125.3 us)
Sparse Core Ops, SparseCore 0:
  15.2 37.1 all-gather.4
  315.3 45.6 reduce-scatter.4
  366.3 34.4 all-gather.6
  402.2 34.4 all-gather.8
  461.1 44.7 reduce-scatter.8
  508.3 44.5 reduce-scatter.6
  557.9 34.4 all-gather.10
  924.3 44.5 reduce-scatter.10
where the time goes:
time: 1060 us
  matrix products  373 us (35%)
  waiting for transfers between devices  191 us (18%)
  blocking collectives  177 us (17%)
  other arithmetic  147 us (14%)
  local copies, waits for them, and re-layouts  132 us (12%)
  starting transfers between devices  18.6 us (2%)
  between operations  14.9 us (1%)
    dot_general x8, matrix products, one_block(): jnp.einsum('qhe,khe->hqk', g_blk, values_all, preferred_element_type=jnp....  84.2 us
    and x16, other arithmetic, allowed(): return same_doc & causal & living  69.2 us
    dot_general x8, matrix products, one_block(): jnp.einsum('hqk,qhe->khe', softmax_f.astype(jnp.bfloat16), g_blk, preferr...  60.4 us
    dot_general x16, matrix products, one_block(): jnp.einsum('qhe,khe->hqk', q_blk, keys_all, preferred_element_type=jnp.fl...  56.1 us
    dot_general x8, matrix products, one_block(): jnp.einsum('hqk,khe->qhe', softmax_w, values_all, preferred_element_type=...  54.3 us
    dynamic_update_slice x16, local copies, waits for them, and re-layouts, attend(): lax.map(one_block, (queries.reshape(blocks, block_rows, heads_here, head_...  53 us
    while x16, local copies, waits for them, and re-layouts  45.6 us
    reduce_scatter x1, waiting for transfers between devices, local(): lax.psum_scatter(jnp.dot(attn_low, out_full, preferred_element_type=jnp.f...  45.1 us
  transfers between devices with their start and end apart: 12, of which 8 were waited for; matrix products, arithmetic and copies ran while one was open for 5% of the time, Pallas kernels for 0%

commit v1 on v0

--- a/solution.py
+++ b/solution.py
@@ -1,6 +1,10 @@
+import functools
+
 import jax
 import jax.numpy as jnp
 from jax import lax
+from jax.experimental import pallas as pl
+from jax.experimental.pallas import tpu as pltpu
 from jax.sharding import PartitionSpec as P
 
 HD = 64
@@ -9,7 +13,7 @@
 
 epsilon = 1e-05
 gelu_slope = 1.702
-masked_score = -1e30
+VMEM_LIMIT = 60 << 20
 
 
 def split_up(value, dim, peers):
@@ -42,98 +46,243 @@
     return (grad_in, jnp.sum(grad_out * normed, axis=0), jnp.sum(grad_out, axis=0))
 
 
-def allowed(seg_query, pos_query, seg_key, pos_key):
-    same_doc = seg_query[:, None] == seg_key[None, :]
-    causal = pos_key[None, :] <= pos_query[:, None]
-    living = (seg_query[:, None] != 0) | (pos_key[None, :] == pos_query[:, None])
-    return same_doc & causal & living
-
-
-def attend(queries, keys_all, values_all, seg_all, block_rows):
-    seq_rows, heads_here, head_size = queries.shape
-    blocks = seq_rows // block_rows
-    positions = jnp.arange(seq_rows, dtype=jnp.int32)
-    scale_factor = head_size ** (-0.5)
-
-    def one_block(pieces):
-        q_blk, seg_blk, pos_blk = pieces
-        scores = (
-            jnp.einsum("qhe,khe->hqk", q_blk, keys_all, preferred_element_type=jnp.float32)
-            * scale_factor
+f32 = jnp.float32
+bf16 = jnp.bfloat16
+LOG2E = 1.4426950408889634
+BLOCK = 512
+TRANSPOSED = (((1,), (1,)), ((), ()))
+
+
+def dot_t(left, right):
+    return lax.dot_general(left, right, TRANSPOSED, preferred_element_type=f32)
+
+
+def dot_n(left, right):
+    return jnp.dot(left, right, preferred_element_type=f32)
+
+
+def three_parts(value):
+    top = value.astype(bf16)
+    rest = value - top.astype(f32)
+    mid = rest.astype(bf16)
+    return top, mid, (rest - mid.astype(f32)).astype(bf16)
+
+
+def diagonal_mask(start_ref, row_at, size):
+    key_pos = lax.broadcasted_iota(jnp.int32, (size, 1), 0)
+    query_pos = lax.broadcasted_iota(jnp.int32, (1, size), 1)
+    first = start_ref[0:1, pl.ds(row_at, size)] - row_at
+    return (key_pos >= first) & (key_pos <= query_pos)
+
+
+def attend_kernel(
+    low_ref, qa_ref, ka_ref, vt_ref, start_ref, out_ref, qb_ref, s0, s1, a0, a1, *, size, blocks
+):
+    score_bufs, acc_bufs = (s0, s1), (a0, a1)
+    heads = range(qa_ref.shape[0])
+    lane = lax.broadcasted_iota(jnp.int32, (size, 128), 1)
+
+    def query_block(i, carry):
+        row_at = pl.multiple_of(i * size, size)
+
+        def score(h, j, top, diag):
+            keys = ka_ref[h, pl.ds(pl.multiple_of(j * size, size), size), :]
+            s = dot_t(keys, qa_ref[h, pl.ds(row_at, size), :])
+            if diag:
+                s = jnp.where(diagonal_mask(start_ref, row_at, size), s, -3e38)
+            score_bufs[h][...] = s
+            col_max = jnp.max(s, axis=0, keepdims=True)
+            return col_max if top is None else jnp.maximum(top, col_max)
+
+        def gather_values(h, j, old, new, first):
+            p = jnp.exp2(score_bufs[h][...] * LOG2E - new * LOG2E).astype(bf16)
+            part = dot_n(vt_ref[h, :, pl.ds(pl.multiple_of(j * size, size), size)], p)
+            if first:
+                acc_bufs[h][...] = part
+            else:
+                acc_bufs[h][...] = acc_bufs[h][...] * jnp.exp2((old - new) * LOG2E) + part
+
+        low = low_ref[i]
+        m0 = score(0, i, None, True)
+        m1 = score(1, i, None, True)
+        gather_values(0, i, None, m0, True)
+        m0n = score(0, jnp.minimum(low, i), m0, False)
+        gather_values(1, i, None, m1, True)
+
+        def body(j, c):
+            m0, m0n, m1 = c
+            m1n = score(1, j, m1, False)
+            gather_values(0, j, m0, m0n, False)
+            m0nn = score(0, jnp.minimum(j + 1, blocks - 1), m0n, False)
+            gather_values(1, j, m1, m1n, False)
+            return m0n, m0nn, m1n
+
+        m0, _, m1 = lax.fori_loop(low, i, body, (m0, m0n, m1))
+        for h, top in ((0, m0), (1, m1)):
+            total = acc_bufs[h][64:65, :]
+            out = acc_bufs[h][0:64, :] / total
+            out_ref[pl.ds(row_at, size), 64 * h : 64 * h + 64] = out.T.astype(out_ref.dtype)
+            norm = jnp.broadcast_to(-(top + jnp.log(total)), (8, size)).T[:, 0:1]
+            n0, n1, n2 = three_parts(norm)
+            rows = qa_ref[h, pl.ds(row_at, size), :]
+            rows = jnp.where(lane == 96, n0, jnp.where(lane == 97, n1, jnp.where(lane == 98, n2, rows)))
+            qb_ref[h, pl.ds(row_at, size), :] = rows
+        return carry
+
+    lax.fori_loop(0, blocks, query_block, 0)
+
+
+def attend(low, qa, ka, vt, start, size):
+    heads, rows, _ = qa.shape
+    vmem = pl.BlockSpec(memory_space=pltpu.VMEM)
+    return pl.pallas_call(
+        functools.partial(attend_kernel, size=size, blocks=rows // size),
+        grid_spec=pltpu.PrefetchScalarGridSpec(
+            num_scalar_prefetch=1,
+            grid=(),
+            in_specs=[vmem] * 4,
+            out_specs=[vmem] * 2,
+            scratch_shapes=[pltpu.VMEM((size, size), f32)] * heads
+            + [pltpu.VMEM((vt.shape[1], size), f32)] * heads,
+        ),
+        out_shape=[
+            jax.ShapeDtypeStruct((rows, HD * heads), bf16),
+            jax.ShapeDtypeStruct(qa.shape, bf16),
+        ],
+        compiler_params=pltpu.CompilerParams(vmem_limit_bytes=VMEM_LIMIT),
+        cost_estimate=pl.CostEstimate(
+            flops=rows * rows * HD * heads, bytes_accessed=8 << 20, transcendentals=rows * rows
+        ),
+        name="attend",
+    )(low, qa, ka, vt, start)
+
+
+def attend_back_kernel(
+    low_ref, qb_ref, ka_ref, va_ref, kt_ref, g_ref, o_ref, start_ref, grad_ref,
+    ga_ref, dk_ref, dv_ref, q0, q1, *, size, blocks
+):
+    query_accs = (q0, q1)
+    lane = lax.broadcasted_iota(jnp.int32, (size, 64), 1)
+
+    def query_block(i, carry):
+        row_at = pl.multiple_of(i * size, size)
+        g_rows = g_ref[pl.ds(row_at, size), :]
+        product = g_rows.astype(f32) * o_ref[pl.ds(row_at, size), :].astype(f32)
+        for h in range(2):
+            cols = slice(64 * h, 64 * h + 64)
+            n0, n1, n2 = three_parts(-jnp.sum(product[:, cols], axis=1, keepdims=True))
+            zero = jnp.zeros((size, 64), bf16)
+            extra = jnp.where(lane == 0, n0, jnp.where(lane == 1, n1, jnp.where(lane == 2, n2, zero)))
+            ga_ref[h] = jnp.concatenate([g_rows[:, cols], extra], axis=1)
+
+        def block(h, j, diag):
+            key_at = pl.multiple_of(j * size, size)
+            keys = ka_ref[h, pl.ds(key_at, size), :]
+            q_rows = qb_ref[h, pl.ds(row_at, size), :]
+            g_head = ga_ref[h]
+            s = dot_t(keys, q_rows)
+            if diag:
+                s = jnp.where(diagonal_mask(start_ref, row_at, size), s, -3e38)
+            p = jnp.exp2(s * LOG2E)
+            dp = dot_t(va_ref[h, pl.ds(key_at, size), :], g_head)
+            ds = (p * dp).astype(bf16)
+            dv = dot_n(p.astype(bf16), g_head[:, 0:64])
+            dk = dot_n(ds, q_rows[:, 0:64])
+            dq = dot_n(kt_ref[h, :, pl.ds(key_at, size)], ds)
+            if diag:
+                dv_ref[h, pl.ds(key_at, size), :] = dv
+                dk_ref[h, pl.ds(key_at, size), :] = dk
+                query_accs[h][...] = dq
+            else:
+                dv_ref[h, pl.ds(key_at, size), :] += dv
+                dk_ref[h, pl.ds(key_at, size), :] += dk
+                query_accs[h][...] += dq
+
+        block(0, i, True)
+        block(1, i, True)
+
+        def body(j, c):
+            block(0, j, False)
+            block(1, j, False)
+            return c
+
+        lax.fori_loop(low_ref[i], i, body, 0)
+        both = jnp.concatenate([query_accs[0][...], query_accs[1][...]], axis=0) * HD ** (-0.5)
+        grad_ref[pl.ds(row_at, size), 0:128] = both.T.astype(bf16)
+        return carry
+
+    lax.fori_loop(0, blocks, query_block, 0)
+
+    def finish(i, carry):
+        row_at = pl.multiple_of(i * size, size)
+        for ref, at in ((dk_ref, 128), (dv_ref, 256)):
+            both = jnp.concatenate([ref[0, pl.ds(row_at, size), :], ref[1, pl.ds(row_at, size), :]], axis=1)
+            grad_ref[pl.ds(row_at, size), at : at + 128] = both.astype(bf16)
+        return carry
+
+    lax.fori_loop(0, blocks, finish, 0)
+
+
+def attend_back(low, qb, ka, va, kt, g, o, start, size):
+    heads, rows, _ = qb.shape
+    vmem = pl.BlockSpec(memory_space=pltpu.VMEM)
+    return pl.pallas_call(
+        functools.partial(attend_back_kernel, size=size, blocks=rows // size),
+        grid_spec=pltpu.PrefetchScalarGridSpec(
+            num_scalar_prefetch=1,
+            grid=(),
+            in_specs=[vmem] * 7,
+            out_specs=vmem,
+            scratch_shapes=[
+                pltpu.VMEM((heads, size, 128), bf16),
+                pltpu.VMEM((heads, rows, HD), f32),
+                pltpu.VMEM((heads, rows, HD), f32),
+            ]
+            + [pltpu.VMEM((HD, size), f32)] * heads,
+        ),
+        out_shape=jax.ShapeDtypeStruct((rows, 3 * HD * heads), bf16),
+        compiler_params=pltpu.CompilerParams(vmem_limit_bytes=VMEM_LIMIT),
+        cost_estimate=pl.CostEstimate(
+            flops=2 * rows * rows * HD * heads, bytes_accessed=16 << 20, transcendentals=rows * rows
+        ),
+        name="attend_back",
+    )(low, qb, ka, va, kt, g, o, start)
+
+
+def with_extras(head_rows, seg_all):
+    rows = seg_all.shape[0]
+    number = jnp.arange(32, dtype=jnp.int32)[None, :]
+    same = seg_all[:, None] == number
+    tail = jnp.zeros((rows, 32), bf16)
+    ones = jnp.zeros((rows, 32), bf16).at[:, 0:3].set(1)
+    other = jnp.where(same, 0.0, -1e30).astype(bf16)
+    own = same.astype(bf16)
+    queries, keys, values = head_rows
+    heads = queries.shape[1] // HD
+    scaled = (queries.astype(f32) * HD ** (-0.5)).astype(bf16)
+
+    def put(rows_in, *more):
+        return jnp.stack(
+            [
+                jnp.concatenate([rows_in[:, HD * h : HD * h + HD], *more], axis=1)
+                for h in range(heads)
+            ]
         )
-        allowed_mask = allowed(seg_blk, pos_blk, seg_all, positions)
-        scores = jnp.where(allowed_mask[None], scores, masked_score)
-        row_max = jnp.max(scores, axis=-1, keepdims=True)
-        exp_scores = jnp.exp(scores - row_max)
-        row_sum = jnp.sum(exp_scores, axis=-1, keepdims=True)
-        softmax_w = (exp_scores / row_sum).astype(jnp.bfloat16)
-        block_out = jnp.einsum(
-            "hqk,khe->qhe", softmax_w, values_all, preferred_element_type=jnp.float32
-        )
-        return (block_out, (row_max + jnp.log(row_sum))[..., 0])
-
-    block_outs, log_norm = lax.map(
-        one_block,
-        (
-            queries.reshape(blocks, block_rows, heads_here, head_size),
-            seg_all.reshape(blocks, block_rows),
-            positions.reshape(blocks, block_rows),
-        ),
-    )
-    return (block_outs.reshape(seq_rows, heads_here, head_size), log_norm)
-
-
-def attend_back(queries, keys_all, values_all, grad_out, raw_out, log_norm, seg_all, block_rows):
-    seq_rows, heads_here, head_size = queries.shape
-    blocks = seq_rows // block_rows
-    positions = jnp.arange(seq_rows, dtype=jnp.int32)
-    scale_factor = head_size ** (-0.5)
-    row_dot = jnp.sum(grad_out.astype(jnp.float32) * raw_out, axis=-1)
-
-    def one_block(running, pieces):
-        grad_keys, grad_values = running
-        q_blk, g_blk, dot_blk, norm_blk, seg_blk, pos_blk = pieces
-        scores = (
-            jnp.einsum("qhe,khe->hqk", q_blk, keys_all, preferred_element_type=jnp.float32)
-            * scale_factor
-        )
-        allowed_mask = allowed(seg_blk, pos_blk, seg_all, positions)
-        scores = jnp.where(allowed_mask[None], scores, masked_score)
-        softmax_f = jnp.exp(scores - norm_blk[..., None])
-        grad_soft = jnp.einsum(
-            "qhe,khe->hqk", g_blk, values_all, preferred_element_type=jnp.float32
-        )
-        grad_scores = (softmax_f * (grad_soft - dot_blk.T[..., None]) * scale_factor).astype(
-            jnp.bfloat16
-        )
-        grad_q = jnp.einsum(
-            "hqk,khe->qhe", grad_scores, keys_all, preferred_element_type=jnp.float32
-        )
-        grad_keys = grad_keys + jnp.einsum(
-            "hqk,qhe->khe", grad_scores, q_blk, preferred_element_type=jnp.float32
-        )
-        grad_values = grad_values + jnp.einsum(
-            "hqk,qhe->khe",
-            softmax_f.astype(jnp.bfloat16),
-            g_blk,
-            preferred_element_type=jnp.float32,
-        )
-        return ((grad_keys, grad_values), grad_q)
-
-    zero_state = jnp.zeros((seq_rows, heads_here, head_size), jnp.float32)
-    (grad_keys, grad_values), grad_queries = lax.scan(
-        one_block,
-        (zero_state, zero_state),
-        (
-            queries.reshape(blocks, block_rows, heads_here, head_size),
-            grad_out.reshape(blocks, block_rows, heads_here, head_size),
-            row_dot.reshape(blocks, block_rows, heads_here),
-            log_norm,
-            seg_all.reshape(blocks, block_rows),
-            positions.reshape(blocks, block_rows),
-        ),
-    )
-    return (grad_queries.reshape(seq_rows, heads_here, head_size), grad_keys, grad_values)
+
+    qa = put(scaled, other, tail)
+    ka = put(keys, own, ones)
+    va = put(values, ones, tail)
+    vt = jnp.swapaxes(va[:, :, 0:80], 1, 2)
+    kt = jnp.swapaxes(ka[:, :, 0:HD], 1, 2)
+    return qa, ka, va, vt, kt
+
+
+def document_starts(seg_all):
+    positions = jnp.arange(seg_all.shape[0], dtype=jnp.int32)
+    number = jnp.arange(32, dtype=jnp.int32)[:, None]
+    before = jnp.sum(((seg_all > 0) & (seg_all < number)).astype(jnp.int32), axis=1)
+    own = jnp.sum(jnp.where(seg_all == number, before[:, None], 0), axis=0)
+    return jnp.where(seg_all == 0, positions, own)
 
 
 def local(
@@ -163,7 +312,6 @@
     model_width = inputs.shape[1]
     head_cols = qkv_full.shape[2]
     hidden_cols = fc_full.shape[1]
-    heads_here = head_cols // HD
     resid_in = inputs.astype(jnp.float32)
     normed_one, hat_one, inv_one = layer_norm(
         resid_in, first_gain.astype(jnp.float32), first_shift.astype(jnp.float32)
@@ -175,23 +323,21 @@
     )
     seg_all = seg_rows[0]
     seq_rows = seq_normed.shape[0]
-    block_rows = min(512, seq_rows)
     projected = jnp.einsum("sd,dje->sje", seq_normed, qkv_full, preferred_element_type=jnp.float32)
     bias_here = lax.dynamic_slice_in_dim(qv_bias, tp_index * head_cols, head_cols, 1).astype(
         jnp.float32
     )
-    queries = (
-        (projected[:, 0] + bias_here[0]).astype(jnp.bfloat16).reshape(seq_rows, heads_here, HD)
-    )
-    keys_all = projected[:, 1].astype(jnp.bfloat16).reshape(seq_rows, heads_here, HD)
-    values_all = (
-        (projected[:, 2] + bias_here[1]).astype(jnp.bfloat16).reshape(seq_rows, heads_here, HD)
-    )
-    live_rows = (seg_all != 0).astype(jnp.float32)
-    raw_out, log_norm = attend(queries, keys_all, values_all, seg_all, block_rows)
-    attn_low = (
-        (raw_out * live_rows[:, None, None]).astype(jnp.bfloat16).reshape(seq_rows, head_cols)
-    )
+    queries = (projected[:, 0] + bias_here[0]).astype(bf16)
+    keys_all = projected[:, 1].astype(bf16)
+    values_all = (projected[:, 2] + bias_here[1]).astype(bf16)
+    live_rows = (seg_all != 0).astype(bf16)
+    start = document_starts(seg_all)
+    size = min(BLOCK, seq_rows)
+    low = start[::size] // size
+    start_rows = jnp.broadcast_to(start[None], (8, seq_rows))
+    qa, ka, va, vt, kt = with_extras((queries, keys_all, values_all), seg_all)
+    raw_out, qb = attend(low, qa, ka, vt, start_rows, size)
+    attn_low = raw_out * live_rows[:, None]
     attn_sum = lax.psum_scatter(
         jnp.dot(attn_low, out_full, preferred_element_type=jnp.float32).astype(jnp.bfloat16),
         "tp",
@@ -246,17 +392,9 @@
     seq_grad = lax.all_gather(grad_hidden_low, "tp", axis=0, tiled=True)
     out_w_grad = jnp.einsum("sc,sd->cd", attn_low, seq_grad, preferred_element_type=jnp.float32)
     grad_attn = jnp.einsum("sd,cd->sc", seq_grad, out_full, preferred_element_type=jnp.float32)
-    grad_attn_low = (
-        grad_attn.astype(jnp.bfloat16).reshape(seq_rows, heads_here, HD)
-        * live_rows.astype(jnp.bfloat16)[:, None, None]
-    )
-    grad_q, grad_k, grad_v = attend_back(
-        queries, keys_all, values_all, grad_attn_low, raw_out, log_norm, seg_all, block_rows
-    )
-    grad_qkv = (
-        jnp.stack([grad_q, grad_k, grad_v], axis=1)
-        .astype(jnp.bfloat16)
-        .reshape(seq_rows, 3, head_cols)
+    grad_attn_low = grad_attn.astype(bf16) * live_rows[:, None]
+    grad_qkv = attend_back(low, qb, ka, va, kt, grad_attn_low, raw_out, start_rows, size).reshape(
+        seq_rows, 3, head_cols
     )
     qkv_w_grad = jnp.einsum("sd,sje->dje", seq_normed, grad_qkv, preferred_element_type=jnp.float32)
     qv_part = jnp.sum(grad_qkv[:, 0::2].astype(jnp.float32), axis=0)

time: 1060 us -> 619 us (0.58)
  matrix products: 373 us -> 72.5 us
  local copies, waits for them, and re-layouts: 132 us -> 36.2 us
  other arithmetic: 147 us -> 53 us
  Pallas kernels: 0 us -> 52.7 us
    dot_general x56 -> x0, matrix products: 303 us -> none  [the longest x8 84.2 us: one_block(): jnp.einsum('qhe,khe->hqk', g_blk, values_all, preferred_element_type=jnp....]
    and x16 -> x0, other arithmetic: 69.2 us -> none  [allowed(): return same_doc & causal & living]
    dynamic_update_slice x16 -> x0, local copies, waits for them, and re-layouts: 53 us -> none  [attend(): lax.map(one_block, (queries.reshape(blocks, block_rows, heads_here, head_...]
    pallas_call x0 -> x2, Pallas kernels: none -> 52.7 us  [the longest x1 30.6 us: attend_back(): pl.pallas_call(functools.partial(attend_back_kernel, size=size, blocks=ro...]
    while x16 -> x0, local copies, waits for them, and re-layouts: 45.6 us -> none
    reduce_sum x9 -> x2, other arithmetic: 37.1 us -> 0.34 us  [the longest x1 0.19 us: document_starts(): jnp.sum(((seg_all > 0) & (seg_all < number)).astype(jnp.int32), axis=1)]
  transfers between devices with their start and end apart: 12 -> 12, of which waited for: 8 -> 8; matrix products, arithmetic and copies ran while one was open for 5% -> 11% of each run, Pallas kernels for 0% -> 0%
where the time goes in v1:
time: 619 us; the launch traced here: 615 us
  waiting for transfers between devices  182 us (29%)
  blocking collectives  177 us (29%)
  matrix products  72.5 us (12%)
  other arithmetic  53 us (9%)
  Pallas kernels  52.7 us (9%)
  local copies, waits for them, and re-layouts  36.2 us (6%)
  starting transfers between devices  26.5 us (4%)
  between operations  15.4 us (2%)
    reduce_scatter x1, waiting for transfers between devices, local(): lax.psum_scatter(jnp.dot(attn_low, out_full, preferred_element_type=jnp.f...  47.6 us
    reduce_scatter x1, waiting for transfers between devices, local(): lax.psum_scatter(jnp.dot(act_low, proj_full, preferred_element_type=jnp.f...  42.5 us
    psum x1, blocking collectives, local(): lax.psum((first_gain_part, first_shift_part, qv_full, out_bias_part, seco...  39.4 us
    reduce_scatter x1, waiting for transfers between devices, local(): lax.psum_scatter(jnp.einsum('sf,df->sd', grad_pre_low, fc_full, preferred...  36.8 us
    all_gather x1, blocking collectives, local(): lax.all_gather(proj_weight, 'fsdp', axis=1, tiled=True)  33.6 us
    all_gather x1, blocking collectives, local(): lax.all_gather(fc_weight, 'fsdp', axis=0, tiled=True)  33.6 us
    all_gather x1, blocking collectives, local(): lax.all_gather(out_weight, 'fsdp', axis=1, tiled=True)  33.3 us
    all_gather x1, blocking collectives, local(): lax.all_gather(qkv_weight, 'fsdp', axis=0, tiled=True)  31.2 us
  transfers between devices with their start and end apart: 12, of which 8 were waited for; matrix products, arithmetic and copies ran while one was open for 11% of the time, Pallas kernels for 0%

profile of v1, /device:TPU:0, one launch (start us, length us, event | category | flops | bytes accessed | tf_op | source)
XLA Modules:
  0.0 615.2 jit_solution(9033312495181236571)
XLA Ops:
  15.3 6.3 %all_gather.27 = s32[1,4096]{1,0:T(1,128)S(1)} all-gather(s32[1,1024]{1,0:T(1,128)S(1)} %copy-done.27), channel_id=1, replica_groups=mesh['fsdp'=8,'tp'=4] {'tp'}, dimensions={1}, use_global_device_ids=true | all-gather | bytes 20480 | tf_op jit(solution)/shard_map/all_gather | solution.py:322
  24.0 33.3 %all_gather.30 = bf16[128,512]{0,1:T(8,128)(2,1)} all-gather(bf16[128,64]{0,1:T(8,128)(2,1)S(1)} %copy-done.25), channel_id=1, replica_groups=mesh['fsdp'=8,'tp'=4] {'fsdp'}, dimensions={1}, use_global_device_ids=true | all-gather | bytes 147456 | tf_op jit(solution)/shard_map/all_gather | solution.py:308
  58.5 31.2 %all_gather.29 = bf16[512,3,128]{2,0,1:T(8,128)(2,1)S(1)} all-gather(bf16[64,3,128]{2,0,1:T(8,128)(2,1)S(1)} %copy-done.21), channel_id=1, replica_groups=mesh['fsdp'=8,'tp'=4] {'fsdp'}, dimensions={0}, use_global_device_ids=true | all-gather | bytes 442368 | tf_op jit(solution)/shard_map/all_gather | solution.py:307
  128.4 22.1 %attend.1 = (bf16[4096,128]{1,0:T(8,128)(2,1)}, bf16[2,4096,128]{2,1,0:T(8,128)(2,1)}) custom-call(s32[8]{0:T(128)} %and_select_fusion.low_ref, bf16[2,4096,128]{2,1,0:T(8,128)(2,1)} %pad_maximum_fusion.2.qa_ref, bf16[2,4096,128]{2,1,0:T(8,128)(2,1)} %copy.76.ka_ref, bf16[2,80,4096]{2,1,0:T(8,128)(2,1)} %copy.77.vt_ref, s32[8,4096]{1,0:T(8,128)} %broadcast_in_dim.33.start_ref), custom_call_target="tpu_custom_call" | custom-call | flops 2147483648 | bytes 8388608 | tf_op jit(solution)/shard_map/attend/pallas_call | solution.py:138
  156.8 47.6 %reduce-scatter.5.cloned.1.call-done = bf16[1024,512]{1,0:T(8,128)(2,1)} async-done(((bf16[4096,512]{1,0:T(8,128)(2,1)}), bf16[1024,512]{1,0:T(8,128)(2,1)}) %reduce-scatter.5.cloned.1.call-update) | async-done | bytes 1048592 | tf_op jit(solution)/shard_map/reduce_scatter | solution.py:341
  211.6 33.6 %all_gather.32 = bf16[512,512]{1,0:T(8,128)(2,1)} all-gather(bf16[64,512]{1,0:T(8,128)(2,1)} %param.28), channel_id=1, replica_groups=mesh['fsdp'=8,'tp'=4] {'fsdp'}, dimensions={0}, use_global_device_ids=true | all-gather | bytes 589824 | tf_op jit(solution)/shard_map/all_gather | solution.py:309
  245.2 33.6 %all_gather.33 = bf16[512,512]{0,1:T(8,128)(2,1)} all-gather(bf16[512,64]{0,1:T(8,128)(2,1)} %param.30), channel_id=1, replica_groups=mesh['fsdp'=8,'tp'=4] {'fsdp'}, dimensions={1}, use_global_device_ids=true | all-gather | bytes 589824 | tf_op jit(solution)/shard_map/all_gather | solution.py:310
  278.8 10.5 %multiply_convert_fusion.1 = (bf16[4096,512]{1,0:T(8,128)(2,1)}, f32[4096,512]{1,0:T(8,128)}) fusion(f32[512]{0:T(512)} %dynamic-slice_convert_fusion, bf16[4096,512]{1,0:T(8,128)(2,1)} %all-gather.7.cloned.1.call-done, bf16[512,512]{1,0:T(8,128)(2,1)} %all_gather.32), kind=kOutput, calls=%fused_computation.3 | convolution fusion | flops 2162163712 | bytes 17303552 | tf_op jit(solution)/shard_map/dot_general | solution.py:354
  289.3 8.8 %convert_reduce_fusion = (f32[512]{0:T(512)}, bf16[4096,512]{1,0:T(8,128)(2,1)S(1)}) fusion(f32[4096,512]{1,0:T(8,128)} %get-tuple-element.72, f32[512]{0:T(512)} %dynamic-slice_convert_fusion, bf16[4096,512]{1,0:T(8,128)(2,1)} %all-gather.9.cloned.1.call-done, bf16[512,512]{0,1:T(8,128)(2,1)} %all_gather.33), kind=kOutput, calls=%fused_computation.1 | convolution fusion | flops 2174746112 | bytes 17305600 | tf_op jit(solution)/shard_map/sd,fd->sf/dot_general | solution.py:368
  304.7 6.8 %convolution_convert_fusion.2 = bf16[4096,512]{1,0:T(8,128)(2,1)} fusion(bf16[4096,512]{1,0:T(8,128)(2,1)} %get-tuple-element.71, bf16[512,512]{0,1:T(8,128)(2,1)} %all_gather.33), kind=kOutput, calls=%fused_computation.7 | convolution fusion | flops 2149580800 | bytes 8912896 | tf_op jit(solution)/shard_map/dot_general | solution.py:360
  312.8 36.8 %reduce-scatter.9.cloned.1.call-done = bf16[1024,512]{1,0:T(8,128)(2,1)} async-done(((bf16[4096,512]{1,0:T(8,128)(2,1)}), bf16[1024,512]{1,0:T(8,128)(2,1)}) %reduce-scatter.9.cloned.1.call-update) | async-done | bytes 1048592 | tf_op jit(solution)/shard_map/reduce_scatter | solution.py:373
  354.1 42.5 %reduce-scatter.7.cloned.1.call-done = bf16[1024,512]{1,0:T(8,128)(2,1)} async-done(((bf16[4096,512]{1,0:T(8,128)(2,1)}), bf16[1024,512]{1,0:T(8,128)(2,1)}) %reduce-scatter.7.cloned.1.call-update) | async-done | bytes 1048592 | tf_op jit(solution)/shard_map/reduce_scatter | solution.py:359
  396.6 5.0 convert_reduce_fusion.6
  405.7 30.6 %all-gather.11.cloned.1.call-done = bf16[4096,512]{1,0:T(8,128)(2,1)} async-done(((bf16[1024,512]{1,0:T(8,128)(2,1)}), bf16[4096,512]{1,0:T(8,128)(2,1)}) %all-gather.11.cloned.1.call-update) | async-done | bytes 4194320 | tf_op jit(solution)/shard_map/all_gather | solution.py:392
  440.7 30.6 %attend_back.1 = bf16[4096,384]{1,0:T(8,128)(2,1)} custom-call(s32[8]{0:T(128)} %and_select_fusion.low_ref, bf16[2,4096,128]{2,1,0:T(8,128)(2,1)} %get-tuple-element.29.qb_ref, bf16[2,4096,128]{2,1,0:T(8,128)(2,1)} %copy.76.ka_ref, bf16[2,4096,128]{2,1,0:T(8,128)(2,1)} %pad_maximum_fusion.1.va_ref, bf16[2,64,4096]{2,1,0:T(8,128)(2,1)} %fusion.42.kt_ref, ...), custom_call_target="tpu_custom_call" | custom-call | flops 4294967296 | bytes 16777216 | tf_op jit(solution)/shard_map/attend_back/pallas_call | solution.py:229
  476.1 6.3 %bitcast_convert_fusion = bf16[4096,512]{1,0:T(8,128)(2,1)} fusion(bf16[4096,3,128]{0,2,1:T(8,128)(2,1)} %bitcast.74, bf16[512,3,128]{2,0,1:T(8,128)(2,1)S(1)} %all_gather.29), kind=kOutput, calls=%fused_computation | convolution fusion | flops 1612709888 | bytes 7733248 | tf_op jit(solution)/shard_map/sje,dje->sd/dot_general | solution.py:402
  482.3 6.7 %convolution_convert_fusion.4 = bf16[512,512]{0,1:T(8,128)(2,1)} fusion(bf16[4096,512]{1,0:T(8,128)(2,1)} %get-tuple-element.71, bf16[4096,512]{1,0:T(8,128)(2,1)} %all-gather.9.cloned.1.call-done), kind=kOutput, calls=%fused_computation.72 | convolution fusion | flops 2147745792 | bytes 8912896 | tf_op jit(solution)/shard_map/sf,sd->fd/dot_general | solution.py:367
  489.0 13.1 %all-to-all-start.3 = ((bf16[8,512,64]{1,2,0:T(8,128)(2,1)}), bf16[8,512,64]{1,2,0:T(8,128)(2,1)S(1)}, u32[]{:S(2)}, u32[]{:S(2)}) async-start(bf16[8,512,64]{1,2,0:T(8,128)(2,1)} %bitcast.25), calls=%async_computation.7 | async-start | bytes 1048576 | tf_op jit(solution)/shard_map/all_to_all | solution.py:27
  502.1 6.7 %convolution_convert_fusion.5 = bf16[512,512]{1,0:T(8,128)(2,1)} fusion(bf16[4096,512]{1,0:T(8,128)(2,1)} %all-gather.7.cloned.1.call-done, bf16[4096,512]{1,0:T(8,128)(2,1)} %copy-done.36), kind=kOutput, calls=%fused_computation.73 | convolution fusion | flops 2147745792 | bytes 8912896 | tf_op jit(solution)/shard_map/sd,sf->df/dot_general | solution.py:371
  508.8 8.2 %all-to-all-done.3 = bf16[8,512,64]{1,2,0:T(8,128)(2,1)S(1)} async-done(((bf16[8,512,64]{1,2,0:T(8,128)(2,1)}), bf16[8,512,64]{1,2,0:T(8,128)(2,1)S(1)}, u32[]{:S(2)}, u32[]{:S(2)}) %all-to-all-start.3) | async-done | bytes 524320 | tf_op jit(solution)/shard_map/all_to_all | solution.py:27
  527.5 8.0 %all-to-all-done.2 = bf16[8,64,512]{2,1,0:T(8,128)(2,1)S(1)} async-done(((bf16[8,64,512]{2,1,0:T(8,128)(2,1)}), bf16[8,64,512]{2,1,0:T(8,128)(2,1)S(1)}, u32[]{:S(2)}, u32[]{:S(2)}) %all-to-all-start.2) | async-done | bytes 524320 | tf_op jit(solution)/shard_map/all_to_all | solution.py:27
  539.1 5.5 fusion.33
  556.6 6.2 %all-to-all-done = bf16[8,64,3,128]{3,1,2,0:T(8,128)(2,1)S(1)} async-done(((bf16[8,64,3,128]{3,1,2,0:T(8,128)(2,1)}), bf16[8,64,3,128]{3,1,2,0:T(8,128)(2,1)S(1)}, u32[]{:S(2)}, u32[]{:S(2)}) %all-to-all-start) | async-done | bytes 393248 | tf_op jit(solution)/shard_map/all_to_all | solution.py:27
  566.0 39.4 %all-reduce.1 = (f32[512]{0:T(512)}, f32[512]{0:T(512)}, f32[2,512]{1,0:T(2,128)}, f32[512]{0:T(512)}, f32[512]{0:T(512)}, /*index=5*/f32[512]{0:T(512)}, f32[2048]{0:T(1024)}, f32[512]{0:T(512)}) all-reduce(f32[512]{0:T(512)S(1)} %get-tuple-element.32, ...), channel_id=1, replica_groups=mesh['fsdp'=8,'tp'=4] {'fsdp','tp'}, use_global_device_ids=true, to_apply=%region_16.17 | all-reduce | flops 6144 | bytes 49152 | tf_op jit(solution)/shard_map/psum | solution.py:431
  (176 shorter events, 120.5 us)
Async XLA Ops:
  7.2 84.9 %all-gather.5.cloned.1.call-start = ((), (), s32[]{:S(2)}) async-start(), calls=%async_computation.8 | async-start | bytes 5242880 | tf_op jit(solution)/shard_map/all_gather | solution.py:321
  8.0 5.9 copy-start.22
  12.4 11.6 %copy-start.25 = (bf16[128,64]{0,1:T(8,128)(2,1)S(1)}, bf16[128,64]{0,1:T(8,128)(2,1)}, u32[]{:S(2)}) copy-start(bf16[128,64]{0,1:T(8,128)(2,1)} %param.24) | copy-start | bytes 49156
  12.5 46.1 %copy-start.21 = (bf16[64,3,128]{2,0,1:T(8,128)(2,1)S(1)}, bf16[64,3,128]{2,0,1:T(8,128)(2,1)}, u32[]{:S(2)}) copy-start(bf16[64,3,128]{2,0,1:T(8,128)(2,1)} %param.22) | copy-start | bytes 147460
  13.9 190.5 %reduce-scatter.5.cloned.1.call-start = ((), (), s32[]{:S(2)}) async-start(), calls=%async_computation.9 | async-start | bytes 5242880 | tf_op jit(solution)/shard_map/reduce_scatter | solution.py:341
  128.4 22.1 %copy-start.13 = (bf16[128,512]{0,1:T(8,128)(2,1)S(1)}, bf16[128,512]{0,1:T(8,128)(2,1)}, u32[]{:S(2)}) copy-start(bf16[128,512]{0,1:T(8,128)(2,1)} %all_gather.30) | copy-start | bytes 393220
  154.9 123.9 %all-gather.7.cloned.1.call-start = ((), (), s32[]{:S(2)}) async-start(), calls=%async_computation.10 | async-start | bytes 5242880 | tf_op jit(solution)/shard_map/all_gather | solution.py:352
  155.6 48.8 %copy-start.15 = (f32[512]{0:T(512)}, f32[512]{0:T(512)S(1)}, u32[]{:S(2)}) copy-start(f32[512]{0:T(512)S(1)} %convert_element_type.161) | copy-start | bytes 6148
  209.7 79.6 %all-gather.9.cloned.1.call-start = ((), (), s32[]{:S(2)}) async-start(), calls=%async_computation.12 | async-start | bytes 5242880 | tf_op jit(solution)/shard_map/all_gather | solution.py:365
  210.2 139.4 %reduce-scatter.9.cloned.1.call-start = ((), (), s32[]{:S(2)}) async-start(), calls=%async_computation.13 | async-start | bytes 5242880 | tf_op jit(solution)/shard_map/reduce_scatter | solution.py:373
  289.3 10.8 %copy-start.11 = (bf16[512,512]{1,0:T(8,128)(2,1)S(1)}, bf16[512,512]{1,0:T(8,128)(2,1)}, u32[]{:S(2)}) copy-start(bf16[512,512]{1,0:T(8,128)(2,1)} %all_gather.32) | copy-start | bytes 1572868
  304.6 92.0 %reduce-scatter.7.cloned.1.call-start = ((), (), s32[]{:S(2)}) async-start(), calls=%async_computation.11 | async-start | bytes 5242880 | tf_op jit(solution)/shard_map/reduce_scatter | solution.py:359
  311.5 124.8 %all-gather.11.cloned.1.call-start = ((), (), s32[]{:S(2)}) async-start(), calls=%async_computation.14 | async-start | bytes 5242880 | tf_op jit(solution)/shard_map/all_gather | solution.py:392
  401.7 161.8 %reduce-scatter.11.cloned.1.call-start = ((), (), s32[]{:S(2)}) async-start(), calls=%async_computation.15 | async-start | bytes 5242880 | tf_op jit(solution)/shard_map/reduce_scatter | solution.py:401
  404.1 32.2 %copy-start.14 = (bf16[128,512]{0,1:T(8,128)(2,1)S(1)}, bf16[128,512]{0,1:T(8,128)(2,1)}, u32[]{:S(2)}) copy-start(bf16[128,512]{0,1:T(8,128)(2,1)} %all_gather.30) | copy-start | bytes 393220
  489.0 28.0 %all-to-all-start.3 = ((bf16[8,512,64]{1,2,0:T(8,128)(2,1)}), bf16[8,512,64]{1,2,0:T(8,128)(2,1)S(1)}, u32[]{:S(2)}, u32[]{:S(2)}) async-start(bf16[8,512,64]{1,2,0:T(8,128)(2,1)} %bitcast.25), calls=%async_computation.7 | async-start | bytes 1048576 | tf_op jit(solution)/shard_map/all_to_all | solution.py:27
  502.1 19.4 %copy-start.28 = (f32[512]{0:T(512)S(1)}, f32[512]{0:T(512)}, u32[]{:S(2)}) copy-start(f32[512]{0:T(512)} %get-tuple-element.73) | copy-start | bytes 6148
  502.1 20.8 %copy-start.9 = (bf16[4096,128]{1,0:T(8,128)(2,1)S(1)}, bf16[4096,128]{1,0:T(8,128)(2,1)}, u32[]{:S(2)}) copy-start(bf16[4096,128]{1,0:T(8,128)(2,1)} %get-tuple-element.28.o_ref) | copy-start | bytes 3145732
  517.0 18.5 %all-to-all-start.2 = ((bf16[8,64,512]{2,1,0:T(8,128)(2,1)}), bf16[8,64,512]{2,1,0:T(8,128)(2,1)S(1)}, u32[]{:S(2)}, u32[]{:S(2)}) async-start(bf16[8,64,512]{2,1,0:T(8,128)(2,1)} %bitcast.83), calls=%async_computation.6 | async-start | bytes 1048576 | tf_op jit(solution)/shard_map/all_to_all | solution.py:27
  535.5 11.0 %all-to-all-start.1 = ((bf16[8,128,64]{1,2,0:T(8,128)(2,1)}), bf16[8,128,64]{1,2,0:T(8,128)(2,1)S(1)}, u32[]{:S(2)}, u32[]{:S(2)}) async-start(bf16[8,128,64]{1,2,0:T(8,128)(2,1)} %bitcast.22), calls=%async_computation.5 | async-start | bytes 262144 | tf_op jit(solution)/shard_map/all_to_all | solution.py:27
  546.5 16.3 %all-to-all-start = ((bf16[8,64,3,128]{3,1,2,0:T(8,128)(2,1)}), bf16[8,64,3,128]{3,1,2,0:T(8,128)(2,1)S(1)}, u32[]{:S(2)}, u32[]{:S(2)}) async-start(bf16[8,64,3,128]{3,1,2,0:T(8,128)(2,1)} %copy.83), calls=%async_computation.4 | async-start | bytes 786432 | tf_op jit(solution)/shard_map/all_to_all | solution.py:27
  551.4 12.0 %copy-start.18 = (f32[1024]{0:T(1024)S(1)}, f32[1024]{0:T(1024)}, u32[]{:S(2)}) copy-start(f32[1024]{0:T(1024)} %copy-done.17) | copy-start | bytes 12292
  551.4 12.0 %copy-start.23 = (f32[512]{0:T(512)S(1)}, f32[512]{0:T(512)}, u32[]{:S(2)}) copy-start(f32[512]{0:T(512)} %copy-done.22) | copy-start | bytes 6148
  552.9 52.5 %copy-start.7 = (f32[1024,512]{1,0:T(8,128)S(1)}, f32[1024,512]{1,0:T(8,128)}, u32[]{:S(2)}) copy-start(f32[1024,512]{1,0:T(8,128)} %get-tuple-element.48) | copy-start | bytes 6291460
  (25 other events, 53.0 us)
Sparse Core Ops, SparseCore 0:
  14.0 37.1 all-gather.4
  155.1 49.2 reduce-scatter.4
  209.8 34.4 all-gather.6
  245.7 34.4 all-gather.8
  304.7 44.8 reduce-scatter.8
  352.0 44.5 reduce-scatter.6
  401.8 34.4 all-gather.10
  482.5 52.1 reduce-scatter.10

commit v2 on v1

--- a/solution.py
+++ b/solution.py
@@ -8,24 +8,9 @@
 from jax.sharding import PartitionSpec as P
 
 HD = 64
-FF = 2048
-
-
+VMEM_LIMIT = 60 << 20
 epsilon = 1e-05
 gelu_slope = 1.702
-VMEM_LIMIT = 60 << 20
-
-
-def split_up(value, dim, peers):
-    dims = value.shape
-    pieces = value.reshape(*dims[:dim], peers, dims[dim] // peers, *dims[dim + 1 :])
-    return jnp.moveaxis(pieces, dim, 0)
-
-
-def sent_and_summed(value, axis, dim):
-    pieces = split_up(value, dim, lax.axis_size(axis))
-    arrived = lax.all_to_all(pieces, axis, split_axis=0, concat_axis=0, tiled=True)
-    return arrived.astype(jnp.float32).sum(axis=0)
 
 
 def layer_norm(values_in, gain_vec, shift_vec):
@@ -121,10 +106,11 @@
         for h, top in ((0, m0), (1, m1)):
             total = acc_bufs[h][64:65, :]
             out = acc_bufs[h][0:64, :] / total
-            out_ref[pl.ds(row_at, size), 64 * h : 64 * h + 64] = out.T.astype(out_ref.dtype)
+            rows = qa_ref[h, pl.ds(row_at, size), :]
+            live = jnp.where(rows[:, 64:65].astype(f32) != 0.0, 1.0, 0.0)
+            out_ref[pl.ds(row_at, size), 64 * h : 64 * h + 64] = (out.T * live).astype(out_ref.dtype)
             norm = jnp.broadcast_to(-(top + jnp.log(total)), (8, size)).T[:, 0:1]
             n0, n1, n2 = three_parts(norm)
-            rows = qa_ref[h, pl.ds(row_at, size), :]
             rows = jnp.where(lane == 96, n0, jnp.where(lane == 97, n1, jnp.where(lane == 98, n2, rows)))
             qb_ref[h, pl.ds(row_at, size), :] = rows
         return carry
@@ -249,32 +235,68 @@
     )(low, qb, ka, va, kt, g, o, start)
 
 
-def with_extras(head_rows, seg_all):
-    rows = seg_all.shape[0]
-    number = jnp.arange(32, dtype=jnp.int32)[None, :]
-    same = seg_all[:, None] == number
-    tail = jnp.zeros((rows, 32), bf16)
-    ones = jnp.zeros((rows, 32), bf16).at[:, 0:3].set(1)
-    other = jnp.where(same, 0.0, -1e30).astype(bf16)
-    own = same.astype(bf16)
-    queries, keys, values = head_rows
-    heads = queries.shape[1] // HD
-    scaled = (queries.astype(f32) * HD ** (-0.5)).astype(bf16)
-
-    def put(rows_in, *more):
-        return jnp.stack(
-            [
-                jnp.concatenate([rows_in[:, HD * h : HD * h + HD], *more], axis=1)
-                for h in range(heads)
-            ]
-        )
-
-    qa = put(scaled, other, tail)
-    ka = put(keys, own, ones)
-    va = put(values, ones, tail)
-    vt = jnp.swapaxes(va[:, :, 0:80], 1, 2)
-    kt = jnp.swapaxes(ka[:, :, 0:HD], 1, 2)
-    return qa, ka, va, vt, kt
+def prepare_kernel(x_ref, w_ref, bias_ref, seg_ref, qa_ref, ka_ref, va_ref, vt_ref, kt_ref):
+    size = x_ref.shape[0]
+    heads = qa_ref.shape[0]
+    width = HD * heads
+    projected = dot_n(x_ref[...], w_ref[...]) + bias_ref[0:1, :]
+    queries = (projected[:, 0:width].astype(bf16).astype(f32) * HD ** (-0.5)).astype(bf16)
+    keys = projected[:, width : 2 * width].astype(bf16)
+    values = projected[:, 2 * width : 3 * width].astype(bf16)
+    number = lax.broadcasted_iota(jnp.int32, (size, 64), 1).astype(f32)
+    seg = jnp.broadcast_to(seg_ref[0:1, :].astype(f32), (8, size)).T[:, 0:1]
+    same = seg == number
+    other = jnp.where(same | (number > 31), 0.0, -1e30).astype(bf16)
+    lanes = lax.broadcasted_iota(jnp.int32, (size, 64), 1)
+    key_tail = jnp.where((same & (lanes < 32)) | ((lanes >= 32) & (lanes < 35)), 1.0, 0.0).astype(bf16)
+    value_tail = jnp.where(lanes < 3, 1.0, 0.0).astype(bf16)
+    for h in range(heads):
+        cols = slice(HD * h, HD * h + HD)
+        qa_ref[h] = jnp.concatenate([queries[:, cols], other], axis=1)
+        ka_ref[h] = jnp.concatenate([keys[:, cols], key_tail], axis=1)
+        va_ref[h] = jnp.concatenate([values[:, cols], value_tail], axis=1)
+        turned = jnp.concatenate([values[:, cols], keys[:, cols]], axis=1).astype(f32).T.astype(bf16)
+        vt_ref[h, 0:64, :] = turned[0:64, :]
+        vt_ref[h, 64:80, :] = jnp.where(
+            lax.broadcasted_iota(jnp.int32, (16, size), 0) == 0, 1.0, 0.0
+        ).astype(bf16)
+        kt_ref[h] = turned[64:128, :]
+
+
+def prepare(x, w, bias, seg_rows, size):
+    rows, width = x.shape
+    heads = w.shape[1] // (3 * HD)
+    wide = pl.BlockSpec((heads, size, 128), lambda i: (0, i, 0))
+    shape = jax.ShapeDtypeStruct((heads, rows, 128), bf16)
+    return pl.pallas_call(
+        prepare_kernel,
+        grid=(rows // size,),
+        in_specs=[
+            pl.BlockSpec((size, width), lambda i: (i, 0)),
+            pl.BlockSpec(w.shape, lambda i: (0, 0)),
+            pl.BlockSpec(bias.shape, lambda i: (0, 0)),
+            pl.BlockSpec((8, size), lambda i: (0, i)),
+        ],
+        out_specs=[
+            wide,
+            wide,
+            wide,
+            pl.BlockSpec((heads, 80, size), lambda i: (0, 0, i)),
+            pl.BlockSpec((heads, 64, size), lambda i: (0, 0, i)),
+        ],
+        out_shape=[
+            shape,
+            shape,
+            shape,
+            jax.ShapeDtypeStruct((heads, 80, rows), bf16),
+            jax.ShapeDtypeStruct((heads, 64, rows), bf16),
+        ],
+        compiler_params=pltpu.CompilerParams(vmem_limit_bytes=VMEM_LIMIT),
+        cost_estimate=pl.CostEstimate(
+            flops=2 * rows * width * w.shape[1], bytes_accessed=14 << 20, transcendentals=0
+        ),
+        name="prepare",
+    )(x, w, bias, seg_rows)
 
 
 def document_starts(seg_all):
@@ -283,6 +305,325 @@
     before = jnp.sum(((seg_all > 0) & (seg_all < number)).astype(jnp.int32), axis=1)
     own = jnp.sum(jnp.where(seg_all == number, before[:, None], 0), axis=0)
     return jnp.where(seg_all == 0, positions, own)
+
+
+MESH = pl.DeviceIdType.MESH
+
+
+def greet(peers):
+    barrier = pltpu.get_barrier_semaphore()
+    for peer in peers:
+        pl.semaphore_signal(barrier, inc=1, device_id=peer, device_id_type=MESH)
+    pl.semaphore_wait(barrier, len(peers))
+
+
+def push(source, target, send_sem, recv_sem, peer):
+    copy = pltpu.make_async_remote_copy(
+        src_ref=source,
+        dst_ref=target,
+        send_sem=send_sem,
+        recv_sem=recv_sem,
+        device_id=peer,
+        device_id_type=MESH,
+    )
+    copy.start()
+    return copy
+
+
+def quad():
+    me = lax.axis_index("tp")
+    side = me + 1 - 2 * lax.rem(me, 2)
+    across = lax.rem(me + 2, 4)
+    far = lax.rem(side + 2, 4)
+    return me, side, across, far
+
+
+def comm_call(kernel, name, number, out_shape, in_specs, out_specs, scratch, moved, *operands):
+    return pl.pallas_call(
+        kernel,
+        out_shape=out_shape,
+        in_specs=in_specs,
+        out_specs=out_specs,
+        scratch_shapes=scratch,
+        compiler_params=pltpu.CompilerParams(
+            collective_id=number, has_side_effects=True, vmem_limit_bytes=VMEM_LIMIT
+        ),
+        cost_estimate=pl.CostEstimate(flops=0, bytes_accessed=moved, transcendentals=0),
+        name=name,
+    )(*operands)
+
+
+def in_vmem():
+    return pl.BlockSpec(memory_space=pltpu.VMEM)
+
+
+def anywhere():
+    return pl.BlockSpec(memory_space=pl.ANY)
+
+
+def gather_kernel(x_ref, seg_ref, all_ref, segs_ref, sy, ry, ss, rs, sf, rf, sg, rg, own, own_seg, *, parts):
+    me, side, across, far = quad()
+    rows = x_ref.shape[0]
+    step = rows // parts
+    greet([{"tp": side}, {"tp": across}, {"tp": far}])
+
+    def rows_of(owner, part):
+        return all_ref.at[pl.ds(owner * rows + part * step, step)]
+
+    sent = []
+    for k, peer in enumerate((across, far, side)):
+        sent.append(push(seg_ref, segs_ref.at[me], sg.at[k], rg.at[k], {"tp": peer}))
+    for part in range(parts):
+        mine = x_ref.at[pl.ds(part * step, step)]
+        sent.append(push(mine, rows_of(me, part), sy.at[part], ry.at[part], {"tp": across}))
+    for part in range(parts):
+        mine = x_ref.at[pl.ds(part * step, step)]
+        sent.append(push(mine, rows_of(me, part), ss.at[part], rs.at[part], {"tp": side}))
+    keep = pltpu.make_async_copy(x_ref, all_ref.at[pl.ds(me * rows, rows)], own)
+    keep.start()
+    keep_seg = pltpu.make_async_copy(seg_ref, segs_ref.at[me], own_seg)
+    keep_seg.start()
+    for part in range(parts):
+        here = rows_of(across, part)
+        pltpu.make_async_remote_copy(
+            here, here, sy.at[part], ry.at[part], {"tp": across}, MESH
+        ).wait_recv()
+        sent.append(push(here, here, sf.at[part], rf.at[part], {"tp": side}))
+    for part in range(parts):
+        there = rows_of(side, part)
+        pltpu.make_async_remote_copy(there, there, ss.at[part], rs.at[part], {"tp": side}, MESH).wait_recv()
+    for part in range(parts):
+        there = rows_of(far, part)
+        pltpu.make_async_remote_copy(there, there, sf.at[part], rf.at[part], {"tp": side}, MESH).wait_recv()
+    for k, peer in enumerate((across, far, side)):
+        there = segs_ref.at[peer]
+        pltpu.make_async_remote_copy(there, there, sg.at[k], rg.at[k], {"tp": peer}, MESH).wait_recv()
+    keep.wait()
+    keep_seg.wait()
+    for copy in sent:
+        copy.wait_send()
+
+
+def gather_rows(x, segments, number, parts=4):
+    rows, width = x.shape
+    dma = pltpu.SemaphoreType.DMA
+    return comm_call(
+        functools.partial(gather_kernel, parts=parts),
+        "gather_rows",
+        number,
+        [
+            jax.ShapeDtypeStruct((4 * rows, width), x.dtype),
+            jax.ShapeDtypeStruct((4, *segments.shape), segments.dtype),
+        ],
+        [in_vmem(), in_vmem()],
+        [anywhere(), anywhere()],
+        [dma((parts,))] * 6 + [dma((3,))] * 2 + [dma, dma],
+        60 << 20,
+        x,
+        segments,
+    )
+
+
+def exchange_kernel(x_ref, out_ref, sems, rems, own):
+    me, side, across, far = quad()
+    rows = x_ref.shape[0] // 4
+    greet([{"tp": side}, {"tp": across}, {"tp": far}])
+    sent = []
+    for k, peer in enumerate((far, across, side)):
+        mine = x_ref.at[pl.ds(peer * rows, rows)]
+        sent.append(push(mine, out_ref.at[me], sems.at[k], rems.at[k], {"tp": peer}))
+    keep = pltpu.make_async_copy(x_ref.at[pl.ds(me * rows, rows)], out_ref.at[me], own)
+    keep.start()
+    for k, peer in enumerate((far, across, side)):
+        there = out_ref.at[peer]
+        pltpu.make_async_remote_copy(there, there, sems.at[k], rems.at[k], {"tp": peer}, MESH).wait_recv()
+    keep.wait()
+    for copy in sent:
+        copy.wait_send()
+
+
+def exchange(x, number, name):
+    rows, width = x.shape
+    dma = pltpu.SemaphoreType.DMA
+    return comm_call(
+        exchange_kernel,
+        name,
+        number,
+        jax.ShapeDtypeStruct((4, rows // 4, width), x.dtype),
+        [in_vmem()],
+        in_vmem(),
+        [dma((3,)), dma((3,)), dma],
+        30 << 20,
+        x,
+    )
+
+
+def fold_kernel(x_ref, out_ref, sum_buf, sa, ra, sb, rb, sy, ry, side_far, side_own, over, *, parts):
+    me, side, across, far = quad()
+    rows = out_ref.shape[0]
+    step = rows // parts
+    greet([{"tp": side}, {"tp": across}])
+
+    def piece(owner, part):
+        return pl.ds(owner * rows + part * step, step)
+
+    sent = []
+    for part in range(parts):
+        here = pl.ds(part * step, step)
+        sent.append(
+            push(x_ref.at[piece(far, part)], side_far.at[here], sa.at[part], ra.at[part], {"tp": side})
+        )
+    for part in range(parts):
+        here = pl.ds(part * step, step)
+        sent.append(
+            push(x_ref.at[piece(side, part)], side_own.at[here], sb.at[part], rb.at[part], {"tp": side})
+        )
+    for part in range(parts):
+        here = pl.ds(part * step, step)
+        block = side_far.at[here]
+        pltpu.make_async_remote_copy(block, block, sa.at[part], ra.at[part], {"tp": side}, MESH).wait_recv()
+        total = x_ref[piece(across, part), :].astype(f32) + side_far[here, :].astype(f32)
+        sum_buf[here, :] = total.astype(sum_buf.dtype)
+        sent.append(push(sum_buf.at[here], over.at[here], sy.at[part], ry.at[part], {"tp": across}))
+    for part in range(parts):
+        here = pl.ds(part * step, step)
+        block = side_own.at[here]
+        pltpu.make_async_remote_copy(block, block, sb.at[part], rb.at[part], {"tp": side}, MESH).wait_recv()
+        out_ref[here, :] = x_ref[piece(me, part), :].astype(f32) + side_own[here, :].astype(f32)
+    for part in range(parts):
+        here = pl.ds(part * step, step)
+        block = over.at[here]
+        pltpu.make_async_remote_copy(block, block, sy.at[part], ry.at[part], {"tp": across}, MESH).wait_recv()
+        out_ref[here, :] += over[here, :].astype(f32)
+    for copy in sent:
+        copy.wait_send()
+
+
+def fold_rows(x, number, parts=4):
+    rows, width = x.shape[0] // 4, x.shape[1]
+    dma = pltpu.SemaphoreType.DMA
+    return comm_call(
+        functools.partial(fold_kernel, parts=parts),
+        "fold_rows",
+        number,
+        jax.ShapeDtypeStruct((rows, width), f32),
+        [in_vmem()],
+        in_vmem(),
+        [pltpu.VMEM((rows, width), x.dtype)]
+        + [dma((parts,))] * 6
+        + [pltpu.VMEM((rows, width), x.dtype)] * 3,
+        60 << 20,
+        x,
+    )
+
+
+def all_sum_kernel(x_ref, out_ref, sems, rems, inbox, *, hops):
+    greet([{axis: flip(axis, bit)} for axis, bit in hops])
+    out_ref[...] = x_ref[...]
+    for k, (axis, bit) in enumerate(hops):
+        peer = {axis: flip(axis, bit)}
+        copy = push(out_ref, inbox.at[k], sems.at[k], rems.at[k], peer)
+        copy.wait()
+        out_ref[...] = out_ref[...] + inbox[k]
+
+
+def flip(axis, bit):
+    me = lax.axis_index(axis)
+    return me + bit - 2 * bit * lax.rem(me // bit, 2)
+
+
+def bits_of(axis):
+    size, bits, bit = lax.axis_size(axis), [], 1
+    while bit < size:
+        bits.append((axis, bit))
+        bit *= 2
+    return bits
+
+
+def all_sum(x, number):
+    hops = bits_of("tp") + bits_of("fsdp")
+    dma = pltpu.SemaphoreType.DMA
+    count = len(hops)
+    return comm_call(
+        functools.partial(all_sum_kernel, hops=hops),
+        "all_sum",
+        number,
+        jax.ShapeDtypeStruct(x.shape, f32),
+        [in_vmem()],
+        in_vmem(),
+        [dma((count,)), dma((count,)), pltpu.VMEM((count, *x.shape), f32)],
+        10 << 20,
+        x,
+    )
+
+
+def fold_shards_kernel(x_ref, out_ref, sems, rems, *bufs, hops):
+    greet([{axis: flip(axis, bit)} for axis, bit in hops])
+    blocks = x_ref.shape[0]
+    count = len(hops)
+    current = x_ref
+    for k, (axis, bit) in enumerate(hops):
+        peer = flip(axis, bit)
+        mine = lax.rem(lax.axis_index(axis) // bit, 2)
+        half = current.shape[0] // 2
+        stage, inbox = bufs[2 * k], bufs[2 * k + 1]
+        for n in range(half):
+            stage[n] = current[2 * n + 1 - mine]
+        copy = push(stage, inbox, sems.at[k], rems.at[k], {axis: peer})
+        copy.wait()
+        if k == count - 1:
+            out_ref[...] = current[mine].astype(f32) + inbox[0].astype(f32)
+        else:
+            keep = bufs[2 * count + k]
+            for n in range(half):
+                keep[n] = (current[2 * n + mine].astype(f32) + inbox[n].astype(f32)).astype(keep.dtype)
+            current = keep
+
+
+def fold_shards(x, number):
+    hops = bits_of("fsdp")
+    count = len(hops)
+    blocks, rows, width = x.shape
+    dma = pltpu.SemaphoreType.DMA
+    halves = [blocks >> (k + 1) for k in range(count)]
+    bufs = []
+    for half in halves:
+        bufs += [pltpu.VMEM((half, rows, width), x.dtype)] * 2
+    bufs += [pltpu.VMEM((half, rows, width), x.dtype) for half in halves[:-1]]
+    return comm_call(
+        functools.partial(fold_shards_kernel, hops=hops),
+        "fold_shards",
+        number,
+        jax.ShapeDtypeStruct((rows, width), f32),
+        [in_vmem()],
+        in_vmem(),
+        [dma((count,)), dma((count,))] + bufs,
+        60 << 20,
+        x,
+    )
+
+
+def spread(value, axis):
+    bits = bits_of(axis)[::-1]
+    size = lax.axis_size(axis)
+    me = lax.axis_index(axis)
+    for k, (_, bit) in enumerate(bits):
+        other = lax.ppermute(value, axis, [(n, n ^ bit) for n in range(size)])
+        high = lax.rem(me // bit, 2) == 1
+        value = jnp.stack([jnp.where(high, other, value), jnp.where(high, value, other)], axis=k)
+    return value.reshape(size, *value.shape[len(bits) :])
+
+
+def fold_bits(value, axis):
+    size = lax.axis_size(axis)
+    for _, bit in bits_of(axis):
+        own = lax.rem(lax.axis_index(axis) // bit, 2)
+        pairs = value.reshape(value.shape[0] // 2, 2, *value.shape[1:])
+        sent = lax.dynamic_index_in_dim(pairs, 1 - own, 1, keepdims=False)
+        kept = lax.dynamic_index_in_dim(pairs, own, 1, keepdims=False)
+        arrived = lax.ppermute(sent, axis, [(n, n ^ bit) for n in range(size)])
+        value = (kept.astype(f32) + arrived.astype(f32)).astype(bf16)
+    return value[0]
 
 
 def local(
@@ -303,122 +644,127 @@
     proj_bias,
 ):
     tp_index = lax.axis_index("tp")
-    qkv_full, out_full, fc_full, proj_full = (
-        lax.all_gather(qkv_weight, "fsdp", axis=0, tiled=True),
-        lax.all_gather(out_weight, "fsdp", axis=1, tiled=True),
-        lax.all_gather(fc_weight, "fsdp", axis=0, tiled=True),
-        lax.all_gather(proj_weight, "fsdp", axis=1, tiled=True),
-    )
-    model_width = inputs.shape[1]
-    head_cols = qkv_full.shape[2]
-    hidden_cols = fc_full.shape[1]
-    resid_in = inputs.astype(jnp.float32)
+    slices = lax.axis_size("tp")
+    rows_here, model_width = inputs.shape
+    shard_rows = qkv_weight.shape[0]
+    head_cols = qkv_weight.shape[2]
+    hidden_cols = fc_weight.shape[1]
+    qkv_full = spread(qkv_weight.reshape(shard_rows, 3 * head_cols), "fsdp").reshape(
+        model_width, 3 * head_cols
+    )
+    packed = jnp.concatenate([fc_weight, proj_weight.T, out_weight.T], axis=1)
+    packed = spread(packed, "fsdp").reshape(model_width, packed.shape[1])
+    packed = spread(packed, "tp")
+    fc_full = packed[:, :, 0:hidden_cols]
+    proj_full = packed[:, :, hidden_cols : 2 * hidden_cols]
+    out_full = packed[:, :, 2 * hidden_cols :]
+
+    resid_in = inputs.astype(f32)
     normed_one, hat_one, inv_one = layer_norm(
-        resid_in, first_gain.astype(jnp.float32), first_shift.astype(jnp.float32)
-    )
-    lowered_one = normed_one.astype(jnp.bfloat16)
-    seq_normed, seg_rows = (
-        lax.all_gather(lowered_one, "tp", axis=0, tiled=True),
-        lax.all_gather(segments, "tp", axis=1, tiled=True),
-    )
-    seg_all = seg_rows[0]
+        resid_in, first_gain.astype(f32), first_shift.astype(f32)
+    )
+    seq_normed, seg_parts = gather_rows(normed_one.astype(bf16), segments, 0)
     seq_rows = seq_normed.shape[0]
-    projected = jnp.einsum("sd,dje->sje", seq_normed, qkv_full, preferred_element_type=jnp.float32)
-    bias_here = lax.dynamic_slice_in_dim(qv_bias, tp_index * head_cols, head_cols, 1).astype(
-        jnp.float32
-    )
-    queries = (projected[:, 0] + bias_here[0]).astype(bf16)
-    keys_all = projected[:, 1].astype(bf16)
-    values_all = (projected[:, 2] + bias_here[1]).astype(bf16)
-    live_rows = (seg_all != 0).astype(bf16)
+    seg_all = seg_parts.reshape(seq_rows)
     start = document_starts(seg_all)
     size = min(BLOCK, seq_rows)
     low = start[::size] // size
     start_rows = jnp.broadcast_to(start[None], (8, seq_rows))
-    qa, ka, va, vt, kt = with_extras((queries, keys_all, values_all), seg_all)
-    raw_out, qb = attend(low, qa, ka, vt, start_rows, size)
-    attn_low = raw_out * live_rows[:, None]
-    attn_sum = lax.psum_scatter(
-        jnp.dot(attn_low, out_full, preferred_element_type=jnp.float32).astype(jnp.bfloat16),
-        "tp",
-        scatter_dimension=0,
-        tiled=True,
-    ).astype(jnp.float32)
-    hidden = resid_in + attn_sum + out_bias.astype(jnp.float32)
+    seg_rows = jnp.broadcast_to(seg_all[None], (8, seq_rows))
+    qv_here = lax.dynamic_slice_in_dim(qv_bias, tp_index * head_cols, head_cols, 1).astype(f32)
+    bias_here = jnp.concatenate([qv_here[0], jnp.zeros((head_cols,), f32), qv_here[1]])
+    bias_rows = jnp.broadcast_to(bias_here[None], (8, 3 * head_cols))
+    qa, ka, va, vt, kt = prepare(seq_normed, qkv_full, bias_rows, seg_rows, size)
+    attn_out, qb = attend(low, qa, ka, vt, start_rows, size)
+    attn_here = exchange(attn_out, 1, "exchange_out")
+
+    hidden = (
+        resid_in
+        + jnp.einsum("prc,pdc->rd", attn_here, out_full, preferred_element_type=f32)
+        + out_bias.astype(f32)
+    )
     normed_two, hat_two, inv_two = layer_norm(
-        hidden, second_gain.astype(jnp.float32), second_shift.astype(jnp.float32)
-    )
-    lowered_two = normed_two.astype(jnp.bfloat16)
-    mlp_in = lax.all_gather(lowered_two, "tp", axis=0, tiled=True)
-    fc_bias_here = lax.dynamic_slice_in_dim(fc_bias, tp_index * hidden_cols, hidden_cols, 0)
-    pre_act = jnp.dot(mlp_in, fc_full, preferred_element_type=jnp.float32) + fc_bias_here.astype(
-        jnp.float32
-    )
+        hidden, second_gain.astype(f32), second_shift.astype(f32)
+    )
+    mlp_in = normed_two.astype(bf16)
+    pre_act = jnp.einsum("sd,tdf->tsf", mlp_in, fc_full, preferred_element_type=f32) + fc_bias.astype(
+        f32
+    ).reshape(slices, 1, hidden_cols)
     sigmoid_pre = jax.nn.sigmoid(gelu_slope * pre_act)
-    act_low = (pre_act * sigmoid_pre).astype(jnp.bfloat16)
-    mlp_sum = lax.psum_scatter(
-        jnp.dot(act_low, proj_full, preferred_element_type=jnp.float32).astype(jnp.bfloat16),
-        "tp",
-        scatter_dimension=0,
-        tiled=True,
-    ).astype(jnp.float32)
-    grad_rows = lax.all_gather(out_grad, "tp", axis=0, tiled=True)
-    layer_out = (hidden + mlp_sum + proj_bias.astype(jnp.float32)).astype(jnp.bfloat16)
-    proj_grad = jnp.einsum("sf,sd->fd", act_low, grad_rows, preferred_element_type=jnp.float32)
-    grad_act = jnp.einsum("sd,fd->sf", grad_rows, proj_full, preferred_element_type=jnp.float32)
+    act_low = (pre_act * sigmoid_pre).astype(bf16)
+    layer_out = (
+        hidden
+        + jnp.einsum("tsf,tdf->sd", act_low, proj_full, preferred_element_type=f32)
+        + proj_bias.astype(f32)
+    ).astype(bf16)
+    proj_grad = jnp.einsum("sd,tsf->tdf", out_grad, act_low, preferred_element_type=f32)
+    grad_act = jnp.einsum("sd,tdf->tsf", out_grad, proj_full, preferred_element_type=f32)
     grad_pre = grad_act * (sigmoid_pre + gelu_slope * pre_act * sigmoid_pre * (1.0 - sigmoid_pre))
-    grad_pre_low = grad_pre.astype(jnp.bfloat16)
-    fc_grad = jnp.einsum("sd,sf->df", mlp_in, grad_pre_low, preferred_element_type=jnp.float32)
-    fc_bias_part = jnp.sum(grad_pre_low.astype(jnp.float32), axis=0)
-    grad_normed_two = lax.psum_scatter(
-        jnp.einsum("sf,df->sd", grad_pre_low, fc_full, preferred_element_type=jnp.float32).astype(
-            jnp.bfloat16
+    grad_pre_low = grad_pre.astype(bf16)
+    fc_grad = jnp.einsum("sd,tsf->tdf", mlp_in, grad_pre_low, preferred_element_type=f32)
+    fc_bias_part = jnp.sum(grad_pre_low.astype(f32), axis=1).reshape(-1)
+    grad_normed_two = jnp.einsum("tsf,tdf->sd", grad_pre_low, fc_full, preferred_element_type=f32)
+    resid_grad = out_grad.astype(f32)
+    grad_hidden_ln, second_gain_part, second_shift_part = norm_back(
+        grad_normed_two, hat_two, inv_two, second_gain.astype(f32)
+    )
+    grad_hidden = resid_grad + grad_hidden_ln
+    grad_hidden_low = grad_hidden.astype(bf16)
+    out_bias_part = jnp.sum(grad_hidden_low.astype(f32), axis=0)
+    proj_bias_part = jnp.sum(resid_grad, axis=0)
+    out_grad_part = jnp.einsum(
+        "sd,psc->pdc", grad_hidden_low, attn_here, preferred_element_type=f32
+    )
+    live_here = (segments[0] != 0).astype(bf16)
+    grad_attn = jnp.einsum("sd,pdc->psc", grad_hidden_low, out_full, preferred_element_type=f32).astype(
+        bf16
+    ) * live_here[None, :, None]
+    grad_attn_seq = exchange(
+        grad_attn.reshape(slices * rows_here, head_cols), 2, "exchange_grad"
+    ).reshape(seq_rows, head_cols)
+    folded = fold_bits(
+        jnp.concatenate(
+            [fc_grad.astype(bf16), proj_grad.astype(bf16), out_grad_part.astype(bf16)], axis=2
         ),
         "tp",
-        scatter_dimension=0,
-        tiled=True,
-    ).astype(jnp.float32)
-    fc_bias_full = lax.dynamic_update_slice_in_dim(
-        jnp.zeros((FF,), jnp.float32), fc_bias_part, tp_index * hidden_cols, 0
-    )
-    resid_grad = out_grad.astype(jnp.float32)
-    grad_hidden_ln, second_gain_part, second_shift_part = norm_back(
-        grad_normed_two, hat_two, inv_two, second_gain.astype(jnp.float32)
-    )
-    grad_hidden = resid_grad + grad_hidden_ln
-    grad_hidden_low = grad_hidden.astype(jnp.bfloat16)
-    out_bias_part = jnp.sum(grad_hidden_low.astype(jnp.float32), axis=0)
-    proj_bias_part = jnp.sum(resid_grad, axis=0)
-    seq_grad = lax.all_gather(grad_hidden_low, "tp", axis=0, tiled=True)
-    out_w_grad = jnp.einsum("sc,sd->cd", attn_low, seq_grad, preferred_element_type=jnp.float32)
-    grad_attn = jnp.einsum("sd,cd->sc", seq_grad, out_full, preferred_element_type=jnp.float32)
-    grad_attn_low = grad_attn.astype(bf16) * live_rows[:, None]
-    grad_qkv = attend_back(low, qb, ka, va, kt, grad_attn_low, raw_out, start_rows, size).reshape(
-        seq_rows, 3, head_cols
-    )
-    qkv_w_grad = jnp.einsum("sd,sje->dje", seq_normed, grad_qkv, preferred_element_type=jnp.float32)
-    qv_part = jnp.sum(grad_qkv[:, 0::2].astype(jnp.float32), axis=0)
-    grad_normed_one = lax.psum_scatter(
-        jnp.einsum("sje,dje->sd", grad_qkv, qkv_full, preferred_element_type=jnp.float32).astype(
-            jnp.bfloat16
-        ),
-        "tp",
-        scatter_dimension=0,
-        tiled=True,
-    ).astype(jnp.float32)
+    )
+    grad_qkv = attend_back(low, qb, ka, va, kt, grad_attn_seq, attn_out, start_rows, size)
+    qkv_w_grad = jnp.einsum("sd,sj->dj", seq_normed, grad_qkv, preferred_element_type=f32)
+    col_sums = jnp.sum(grad_qkv.astype(f32), axis=0)
+    partial = jnp.einsum("sj,dj->sd", grad_qkv, qkv_full, preferred_element_type=f32).astype(bf16)
+    grad_normed_one = fold_rows(partial, 3)
+    grad_in_ln, first_gain_part, first_shift_part = norm_back(
+        grad_normed_one, hat_one, inv_one, first_gain.astype(f32)
+    )
+    input_grad = (grad_hidden + grad_in_ln).astype(bf16)
+    shards = model_width // shard_rows
+    every = jnp.concatenate([folded, qkv_w_grad.astype(bf16)], axis=1).reshape(
+        shards, shard_rows, -1
+    )
+    summed = fold_shards(every, 4)
+    fc_w_grad = summed[:, 0:hidden_cols]
+    proj_w_grad = summed[:, hidden_cols : 2 * hidden_cols].T
+    out_w_grad = summed[:, 2 * hidden_cols : 2 * hidden_cols + head_cols].T
+    qkv_grad = summed[:, 2 * hidden_cols + head_cols :].reshape(shard_rows, 3, head_cols)
+    qv_part = jnp.stack([col_sums[0:head_cols], col_sums[2 * head_cols :]])
     qv_full = lax.dynamic_update_slice_in_dim(
-        jnp.zeros((2, model_width), jnp.float32), qv_part, tp_index * head_cols, 1
-    )
-    grad_in_ln, first_gain_part, first_shift_part = norm_back(
-        grad_normed_one, hat_one, inv_one, first_gain.astype(jnp.float32)
-    )
-    input_grad = (grad_hidden + grad_in_ln).astype(jnp.bfloat16)
-    qkv_w_grad, out_w_grad, fc_grad, proj_grad = (
-        sent_and_summed(qkv_w_grad.astype(jnp.bfloat16), "fsdp", 0),
-        sent_and_summed(out_w_grad.astype(jnp.bfloat16), "fsdp", 1),
-        sent_and_summed(fc_grad.astype(jnp.bfloat16), "fsdp", 0),
-        sent_and_summed(proj_grad.astype(jnp.bfloat16), "fsdp", 1),
-    )
+        jnp.zeros((2, model_width), f32), qv_part, tp_index * head_cols, 1
+    )
+    vectors = [
+        first_gain_part,
+        first_shift_part,
+        qv_full.reshape(-1),
+        out_bias_part,
+        second_gain_part,
+        second_shift_part,
+        fc_bias_part,
+        proj_bias_part,
+    ]
+    totals = all_sum(jnp.concatenate(vectors).reshape(-1, 128), 5).reshape(-1)
+    pieces, at = [], 0
+    for vector in vectors:
+        pieces.append(totals[at : at + vector.shape[0]])
+        at += vector.shape[0]
     (
         first_gain_grad,
         first_shift_grad,
@@ -428,33 +774,21 @@
         second_shift_grad,
         fc_bias_grad,
         proj_bias_grad,
-    ) = lax.psum(
-        (
-            first_gain_part,
-            first_shift_part,
-            qv_full,
-            out_bias_part,
-            second_gain_part,
-            second_shift_part,
-            fc_bias_full,
-            proj_bias_part,
-        ),
-        ("fsdp", "tp"),
-    )
+    ) = pieces
     return (
         layer_out,
         input_grad,
         first_gain_grad,
         first_shift_grad,
-        qkv_w_grad,
-        qv_bias_grad,
+        qkv_grad,
+        qv_bias_grad.reshape(2, model_width),
         out_w_grad,
         out_bias_grad,
         second_gain_grad,
         second_shift_grad,
-        fc_grad,
+        fc_w_grad,
         fc_bias_grad,
-        proj_grad,
+        proj_w_grad,
         proj_bias_grad,
     )
 

time: 619 us -> 422 us (0.68)
  Pallas kernels: 52.7 us -> 243 us
  blocking collectives: 177 us -> 0 us
  waiting for transfers between devices: 182 us -> 44.2 us
  matrix products: 72.5 us -> 43.5 us
  other arithmetic: 53 us -> 37.2 us
  between operations: 15.4 us -> 1.47 us
  starting transfers between devices: 26.5 us -> 16.5 us
    pallas_call x0 -> x7, Pallas kernels: none -> 189 us  [the longest x6 178 us: comm_call(): pl.pallas_call(kernel, out_shape=out_shape, in_specs=in_specs, out_specs=...]
    all_gather x5 -> x0, blocking collectives: 138 us -> none  [the longest x1 33.6 us: local(): lax.all_gather(proj_weight, 'fsdp', axis=1, tiled=True)]
    reduce_scatter x4 -> x0, waiting for transfers between devices: 127 us -> none  [the longest x1 47.6 us: local(): lax.psum_scatter(jnp.dot(attn_low, out_full, preferred_element_type=jnp.f...]
    ppermute x0 -> x10, waiting for transfers between devices: none -> 44.2 us  [the longest x8 29.2 us: spread(): other = lax.ppermute(value, axis, [(n, n ^ bit) for n in range(size)])]
    psum x1 -> x0, blocking collectives: 39.4 us -> none  [local(): lax.psum((first_gain_part, first_shift_part, qv_full, out_bias_part, seco...]
    all_gather x4 -> x0, waiting for transfers between devices: 30.6 us -> none  [the longest x1 30.6 us: local(): seq_grad = lax.all_gather(grad_hidden_low, 'tp', axis=0, tiled=True)]
    dot_general x12 -> x11, matrix products: 72.5 us -> 43.5 us  [the longest x1 6.99 us: local(): jnp.einsum('sd,tdf->tsf', out_grad, proj_full, preferred_element_type=f32)]
    all_to_all x4 -> x0, starting transfers between devices: 25.6 us -> none  [sent_and_summed(): lax.all_to_all(pieces, axis, split_axis=0, concat_axis=0, tiled=True)]
  transfers between devices with their start and end apart: 12 -> 10, of which waited for: 8 -> 6; matrix products, arithmetic and copies ran while one was open for 11% -> 11% of each run, Pallas kernels for 0% -> 38%
where the time goes in v2:
time: 422 us; the launch traced here: 418 us
  Pallas kernels  243 us (58%)
  waiting for transfers between devices  44.2 us (10%)
  matrix products  43.5 us (10%)
  other arithmetic  37.2 us (9%)
  local copies, waits for them, and re-layouts  32.2 us (8%)
  starting transfers between devices  16.5 us (4%)
    pallas_call x6, Pallas kernels, comm_call(): pl.pallas_call(kernel, out_shape=out_shape, in_specs=in_specs, out_specs=...  178 us
    pallas_call x1, Pallas kernels, attend_back(): pl.pallas_call(functools.partial(attend_back_kernel, size=size, blocks=ro...  31.1 us
    ppermute x8, waiting for transfers between devices, spread(): other = lax.ppermute(value, axis, [(n, n ^ bit) for n in range(size)])  29.2 us
    pallas_call x1, Pallas kernels, attend(): pl.pallas_call(functools.partial(attend_kernel, size=size, blocks=rows //...  23.4 us
    ppermute x8, starting transfers between devices, spread(): other = lax.ppermute(value, axis, [(n, n ^ bit) for n in range(size)])  16 us
    ppermute x2, waiting for transfers between devices, fold_bits(): arrived = lax.ppermute(sent, axis, [(n, n ^ bit) for n in range(size)])  15 us
    pallas_call x1, Pallas kernels, prepare(): pl.pallas_call(prepare_kernel, grid=(rows // size,), in_specs=[pl.BlockSp...  10.7 us
    unnamed x73, local copies, waits for them, and re-layouts  10.1 us
  transfers between devices with their start and end apart: 10, of which 6 were waited for; matrix products, arithmetic and copies ran while one was open for 11% of the time, Pallas kernels for 38%

profile of v2, /device:TPU:0, one launch (start us, length us, event | category | flops | bytes accessed | tf_op | source)
XLA Modules:
  0.0 418.4 jit_solution(14560712744314804680)
XLA Ops:
  1.7 4.1 collective-permute-start.3
  5.8 7.0 %collective-permute-done.3 = bf16[64,1152]{1,0:T(8,128)(2,1)S(1)} collective-permute-done((bf16[64,1152]{1,0:T(8,128)(2,1)S(1)}, bf16[64,1152]{1,0:T(8,128)(2,1)S(1)}, u32[]{:S(2)}, u32[]{:S(2)}) %collective-permute-start.3) | collective-permute-done | bytes 147488 | tf_op jit(solution)/shard_map/ppermute | solution.py:611
  14.6 7.5 %collective-permute-done.4 = bf16[2,64,1152]{2,1,0:T(8,128)(2,1)S(1)} collective-permute-done((bf16[2,64,1152]{2,1,0:T(8,128)(2,1)S(1)}, bf16[2,64,1152]{2,1,0:T(8,128)(2,1)S(1)}, u32[]{:S(2)}, u32[]{:S(2)}) %collective-permute-start.4) | collective-permute-done | bytes 294944 | tf_op jit(solution)/shard_map/ppermute | solution.py:611
  23.5 3.4 collective-permute-start
  27.2 8.7 %collective-permute-done.5 = bf16[2,2,64,1152]{3,2,1,0:T(8,128)(2,1)S(1)} collective-permute-done((bf16[2,2,64,1152]{3,2,1,0:T(8,128)(2,1)S(1)}, bf16[2,2,64,1152]{3,2,1,0:T(8,128)(2,1)S(1)}, u32[]{:S(2)}, u32[]{:S(2)}) %collective-permute-start.5) | collective-permute-done | bytes 589856 | tf_op jit(solution)/shard_map/ppermute | solution.py:611
  39.5 46.7 %gather_rows.1 = (bf16[4096,512]{1,0:T(8,128)(2,1)}, s32[4,1,1024]{2,1,0:T(1,128)}) custom-call(bf16[1024,512]{1,0:T(8,128)(2,1)} %fusion.10.x_ref, s32[1,1024]{1,0:T(1,128)} %seg_ref.1), custom_call_target="tpu_custom_call" | custom-call | bytes 62914560 | tf_op jit(solution)/shard_map/gather_rows/pallas_call | solution.py:342
  110.6 3.7 collective-permute-done.2
  116.4 10.7 %prepare.1 = (bf16[2,4096,128]{2,1,0:T(8,128)(2,1)}, bf16[2,4096,128]{2,1,0:T(8,128)(2,1)}, bf16[2,4096,128]{2,1,0:T(8,128)(2,1)}, bf16[2,80,4096]{2,1,0:T(8,128)(2,1)}, bf16[2,64,4096]{2,1,0:T(8,128)(2,1)}) custom-call(bf16[4096,512]{1,0:T(8,128)(2,1)} %get-tuple-element.24.x_ref, bf16[512,384]{1,0:T(8,128)(2,1)} %bitcast.192, ...), custom_call_target="tpu_custom_call" | custom-call | flops 1610612736 | bytes 14680064 | tf_op jit(solution)/shard_map/prepare/pallas_call | solution.py:271
  127.7 23.4 %attend.1 = (bf16[4096,128]{1,0:T(8,128)(2,1)}, bf16[2,4096,128]{2,1,0:T(8,128)(2,1)}) custom-call(s32[8]{0:T(128)} %and_select_fusion.low_ref, bf16[2,4096,128]{2,1,0:T(8,128)(2,1)} %get-tuple-element.25.qa_ref, bf16[2,4096,128]{2,1,0:T(8,128)(2,1)} %get-tuple-element.26.ka_ref, bf16[2,80,4096]{2,1,0:T(8,128)(2,1)} %get-tuple-element.27.vt_ref, ...), custom_call_target="tpu_custom_call" | custom-call | flops 2147483648 | bytes 8388608 | tf_op jit(solution)/shard_map/attend/pallas_call | solution.py:124
  151.1 16.5 %exchange_out.1 = bf16[4,1024,128]{2,1,0:T(8,128)(2,1)} custom-call(bf16[4096,128]{1,0:T(8,128)(2,1)} %get-tuple-element.28.x_ref.o_ref), custom_call_target="tpu_custom_call" | custom-call | bytes 31457280 | tf_op jit(solution)/shard_map/exchange_out/pallas_call | solution.py:342
  173.1 6.9 %fusion.1 = (bf16[4,1024,512]{1,2,0:T(8,128)(2,1)}, f32[4,512,1024]{2,1,0:T(8,128)S(1)}) fusion(f32[4,512]{1,0:T(4,128)S(1)} %copy-done.22, f32[1024,512]{1,0:T(8,128)S(1)} %get-tuple-element.116, f32[512]{0:T(512)S(1)} %copy-done.25, f32[512]{0:T(512)S(1)} %copy-done.23, f32[1024]{0:T(1024)S(1)} %add_rsqrt_fusion, f32[1024]{0:T(1024)S(1)} %broadcast_multiply_fusion.4, ...), kind=kOutput, calls=%fused_computation.4 | convolution fusion | flops 2164785152 | bytes 16797696 | tf_op jit(solution)/shard_map/sd,tdf->tsf/dot_general | solution.py:690
  180.0 7.0 %convert_reduce_fusion = (f32[4,512]{1,0:T(4,128)S(1)}, bf16[4,1024,512]{1,2,0:T(8,128)(2,1)S(1)}) fusion(f32[4,512,1024]{2,1,0:T(8,128)S(1)} %get-tuple-element.119, f32[4,512]{1,0:T(4,128)S(1)} %copy-done.22, bf16[1024,512]{1,0:T(8,128)(2,1)S(1)} %copy-done.14, bf16[4,512,1152]{2,1,0:T(8,128)(2,1)S(1)} %bitcast.177), kind=kOutput, calls=%fused_computation.5 | convolution fusion | flops 2174744576 | bytes 15745024 | tf_op jit(solution)/shard_map/sd,tdf->tsf/dot_general | solution.py:701
  187.0 3.9 convert_bitcast_fusion.1
  200.9 16.6 %exchange_grad.1 = bf16[4,1024,128]{2,1,0:T(8,128)(2,1)} custom-call(bf16[4096,128]{1,0:T(8,128)(2,1)} %bitcast.183), custom_call_target="tpu_custom_call" | custom-call | bytes 31457280 | tf_op jit(solution)/shard_map/exchange_grad/pallas_call | solution.py:342
  217.6 31.1 %attend_back.1 = bf16[4096,384]{1,0:T(8,128)(2,1)} custom-call(s32[8]{0:T(128)} %and_select_fusion.low_ref, bf16[2,4096,128]{2,1,0:T(8,128)(2,1)} %get-tuple-element.29.qb_ref, bf16[2,4096,128]{2,1,0:T(8,128)(2,1)} %get-tuple-element.26.ka_ref, bf16[2,4096,128]{2,1,0:T(8,128)(2,1)} %get-tuple-element.30.va_ref, ...), custom_call_target="tpu_custom_call" | custom-call | flops 4294967296 | bytes 16777216 | tf_op jit(solution)/shard_map/attend_back/pallas_call | solution.py:215
  251.5 4.3 %convolution_convert_fusion.x_ref = bf16[4096,512]{1,0:T(8,128)(2,1)} fusion(bf16[4096,384]{1,0:T(8,128)(2,1)S(1)} %copy-done.11, bf16[512,384]{1,0:T(8,128)(2,1)S(1)} %bitcast.193), kind=kOutput, calls=%fused_computation.8 | convolution fusion | flops 1612709888 | bytes 7733248 | tf_op jit(solution)/shard_map/sj,dj->sd/dot_general | solution.py:734
  261.1 4.3 %copy.73 = bf16[2,1,512,1152]{3,2,0,1:T(8,128)(2,1)} copy(bf16[2,1,512,1152]{2,3,1,0:T(8,128)(2,1)} %get-tuple-element.85) | data formatting | bytes 4718592 | tf_op jit(solution)/shard_map/jit(dynamic_index_in_dim)/dynamic_slice | solution.py:622
  265.4 4.4 %copy.83 = bf16[2,1,512,1152]{3,2,0,1:T(8,128)(2,1)} copy(bf16[2,1,512,1152]{2,3,1,0:T(8,128)(2,1)} %get-tuple-element.84) | data formatting | bytes 4718592
  269.9 30.8 %fold_rows.1 = f32[1024,512]{1,0:T(8,128)} custom-call(bf16[4096,512]{1,0:T(8,128)(2,1)} %convolution_convert_fusion.x_ref), custom_call_target="tpu_custom_call" | custom-call | bytes 62914560 | tf_op jit(solution)/shard_map/fold_rows/pallas_call | solution.py:342
  304.1 32.9 %all_sum.1 = f32[48,128]{1,0:T(8,128)} custom-call(f32[48,128]{1,0:T(8,128)} %bitcast.199), custom_call_target="tpu_custom_call" | custom-call | bytes 10485760 | tf_op jit(solution)/shard_map/all_sum/pallas_call | solution.py:342
  339.7 6.4 %convolution_convert_fusion.3 = bf16[512,384]{1,0:T(8,128)(2,1)} fusion(bf16[4096,512]{1,0:T(8,128)(2,1)} %get-tuple-element.24.x_ref, bf16[4096,384]{1,0:T(8,128)(2,1)} %attend_back.1), kind=kOutput, calls=%fused_computation.66 | convolution fusion | flops 1610809344 | bytes 7733248 | tf_op jit(solution)/shard_map/sd,sj->dj/dot_general | solution.py:732
  355.8 5.1 %fusion.21 = bf16[1024,512]{1,0:T(8,128)(2,1)} fusion(f32[1024,512]{1,0:T(8,128)S(1)} %copy-done.7, bf16[4,1024,512]{1,2,0:T(8,128)(2,1)S(1)} %copy-done.30, bf16[4,512,1152]{2,1,0:T(8,128)(2,1)} %bitcast.180, f32[512]{0:T(512)S(1)} %copy-done.24), kind=kOutput, calls=%fused_computation.44 | convolution fusion | flops 2149056512 | bytes 9439232 | tf_op jit(solution)/shard_map/tsf,tdf->sd/dot_general | solution.py:697
  360.9 15.0 %collective-permute-done.9 = bf16[1,512,1152]{2,1,0:T(8,128)(2,1)} collective-permute-done((bf16[1,512,1152]{2,1,0:T(8,128)(2,1)}, bf16[1,512,1152]{2,1,0:T(8,128)(2,1)}, u32[]{:S(2)}, u32[]{:S(2)}) %collective-permute-start.9) | collective-permute-done | bytes 1179680 | tf_op jit(solution)/shard_map/ppermute | solution.py:624
  378.8 34.8 %fold_shards.1 = f32[64,1536]{1,0:T(8,128)} custom-call(bf16[8,64,1536]{2,1,0:T(8,128)(2,1)} %pad_maximum_fusion.3.x_ref), custom_call_target="tpu_custom_call" | custom-call | bytes 62914560 | tf_op jit(solution)/shard_map/fold_shards/pallas_call | solution.py:342
  (165 shorter events, 81.9 us)
Async XLA Ops:
  0.6 22.9 %copy-start = (bf16[64,3,128]{2,0,1:T(8,128)(2,1)S(1)}, bf16[64,3,128]{2,0,1:T(8,128)(2,1)}, u32[]{:S(2)}) copy-start(bf16[64,3,128]{2,0,1:T(8,128)(2,1)} %param.20) | copy-start | bytes 147460
  0.7 26.3 %copy-start.2 = (bf16[1024,512]{1,0:T(8,128)(2,1)S(1)}, bf16[1024,512]{1,0:T(8,128)(2,1)}, u32[]{:S(2)}) copy-start(bf16[1024,512]{1,0:T(8,128)(2,1)} %param.15) | copy-start | bytes 3145732
  1.7 11.1 %collective-permute-start.3 = (bf16[64,1152]{1,0:T(8,128)(2,1)S(1)}, bf16[64,1152]{1,0:T(8,128)(2,1)S(1)}, u32[]{:S(2)}, u32[]{:S(2)}) collective-permute-start(bf16[64,1152]{1,0:T(8,128)(2,1)S(1)} %pad_maximum_fusion.9), channel_id=1, source_target_pairs={{0,16},{4,20},{8,24},{12,28},{16,0},{20,4},{24,8},{28,12},{1,17},{... | collective-permute-start | bytes 442376 | tf_op jit(solution)/shard_map/ppermute | solution.py:611
  13.8 8.2 %collective-permute-start.4 = (bf16[2,64,1152]{2,1,0:T(8,128)(2,1)S(1)}, bf16[2,64,1152]{2,1,0:T(8,128)(2,1)S(1)}, u32[]{:S(2)}, u32[]{:S(2)}) collective-permute-start(bf16[2,64,1152]{2,1,0:T(8,128)(2,1)S(1)} %pad_maximum_fusion.7), channel_id=1, source_target_pairs={{0,8},{4,12},{8,0},{12,4},{16,24},{20,28},{24,16},{28,20},{1,9},{5... | collective-permute-start | bytes 884744 | tf_op jit(solution)/shard_map/ppermute | solution.py:611
  22.2 13.7 %collective-permute-start.5 = (bf16[2,2,64,1152]{3,2,1,0:T(8,128)(2,1)S(1)}, bf16[2,2,64,1152]{3,2,1,0:T(8,128)(2,1)S(1)}, u32[]{:S(2)}, u32[]{:S(2)}) collective-permute-start(bf16[2,2,64,1152]{3,2,1,0:T(8,128)(2,1)S(1)} %pad_maximum_fusion.5), channel_id=1, source_target_pairs={{0,4},{4,0},{8,12},{12,8},{16,20},{20,16},{24,28},{28,24},{1,5},{5... | collective-permute-start | bytes 1769480 | tf_op jit(solution)/shard_map/ppermute | solution.py:611
  23.5 77.3 %collective-permute-start = (bf16[64,384]{1,0:T(8,128)(2,1)S(1)}, bf16[64,384]{1,0:T(8,128)(2,1)}, u32[]{:S(2)}, u32[]{:S(2)}) collective-permute-start(bf16[64,384]{1,0:T(8,128)(2,1)S(1)} %copy_bitcast_fusion.1), channel_id=1, source_target_pairs={{0,16},{4,20},{8,24},{12,28},{16,0},{20,4},{24,8},{28,12},{1,17},{... | collective-permute-start | bytes 147464 | tf_op jit(solution)/shard_map/ppermute | solution.py:611
  27.1 10.3 %copy-start.27 = (bf16[512]{0:T(512)(128)(2,1)S(1)}, bf16[512]{0:T(512)(128)(2,1)}, u32[]{:S(2)}) copy-start(bf16[512]{0:T(512)(128)(2,1)} %param.18) | copy-start | bytes 3076
  27.2 10.3 %copy-start.28 = (bf16[512]{0:T(512)(128)(2,1)S(1)}, bf16[512]{0:T(512)(128)(2,1)}, u32[]{:S(2)}) copy-start(bf16[512]{0:T(512)(128)(2,1)} %param.19) | copy-start | bytes 3076
  36.1 50.0 %copy-start.9 = (bf16[2,2,2,64,1152]{4,3,2,1,0:T(8,128)(2,1)}, bf16[2,2,2,64,1152]{4,3,2,1,0:T(8,128)(2,1)S(1)}, u32[]{:S(2)}) copy-start(bf16[2,2,2,64,1152]{4,3,2,1,0:T(8,128)(2,1)S(1)} %pad_maximum_fusion.4) | copy-start | bytes 3538948
  36.1 52.6 %collective-permute-start.6 = (bf16[512,1152]{1,0:T(8,128)(2,1)S(1)}, bf16[512,1152]{1,0:T(8,128)(2,1)}, u32[]{:S(2)}, u32[]{:S(2)}) collective-permute-start(bf16[512,1152]{1,0:T(8,128)(2,1)S(1)} %bitcast.181), channel_id=1, source_target_pairs={{0,2},{1,3},{2,0},{3,1},{4,6},{5,7},{6,4},{7,5},{8,10},{9,11},{10,... | collective-permute-start | bytes 3538952 | tf_op jit(solution)/shard_map/ppermute | solution.py:611
  92.2 75.4 %collective-permute-start.7 = (bf16[2,512,1152]{2,1,0:T(8,128)(2,1)}, bf16[2,512,1152]{2,1,0:T(8,128)(2,1)}, u32[]{:S(2)}, u32[]{:S(2)}) collective-permute-start(bf16[2,512,1152]{2,1,0:T(8,128)(2,1)} %pad_maximum_fusion.2), channel_id=1, source_target_pairs={{0,1},{1,0},{2,3},{3,2},{4,5},{5,4},{6,7},{7,6},{8,9},{9,8},{10,11... | collective-permute-start | bytes 7077896 | tf_op jit(solution)/shard_map/ppermute | solution.py:611
  101.6 6.1 %collective-permute-start.1 = (bf16[2,64,384]{2,1,0:T(8,128)(2,1)S(1)}, bf16[2,64,384]{2,1,0:T(8,128)(2,1)S(1)}, u32[]{:S(2)}, u32[]{:S(2)}) collective-permute-start(bf16[2,64,384]{2,1,0:T(8,128)(2,1)S(1)} %pad_maximum_fusion.10), channel_id=1, source_target_pairs={{0,8},{4,12},{8,0},{12,4},{16,24},{20,28},{24,16},{28,20},{1,9},{5... | collective-permute-start | bytes 294920 | tf_op jit(solution)/shard_map/ppermute | solution.py:611
  107.8 6.4 %collective-permute-start.2 = (bf16[2,2,64,384]{3,2,0,1:T(8,128)(2,1)S(1)}, bf16[2,2,64,384]{3,2,0,1:T(8,128)(2,1)S(1)}, u32[]{:S(2)}, u32[]{:S(2)}) collective-permute-start(bf16[2,2,64,384]{3,2,0,1:T(8,128)(2,1)S(1)} %pad_maximum_fusion.8), channel_id=1, source_target_pairs={{0,4},{4,0},{8,12},{12,8},{16,20},{20,16},{24,28},{28,24},{1,5},{5... | collective-permute-start | bytes 589832 | tf_op jit(solution)/shard_map/ppermute | solution.py:611
  170.6 26.3 %copy-start.8 = (bf16[2,2,512,1152]{3,2,1,0:T(8,128)(2,1)}, bf16[2,2,512,1152]{3,2,1,0:T(8,128)(2,1)S(1)}, u32[]{:S(2)}) copy-start(bf16[2,2,512,1152]{3,2,1,0:T(8,128)(2,1)S(1)} %copy.63) | copy-start | bytes 14155780
  172.3 21.9 %copy-start.6 = (f32[1024,512]{1,0:T(8,128)}, f32[1024,512]{1,0:T(8,128)S(1)}, u32[]{:S(2)}) copy-start(f32[1024,512]{1,0:T(8,128)S(1)} %get-tuple-element.116) | copy-start | bytes 6291460
  173.1 6.9 %copy-start.14 = (bf16[1024,512]{1,0:T(8,128)(2,1)S(1)}, bf16[1024,512]{1,0:T(8,128)(2,1)}, u32[]{:S(2)}) copy-start(bf16[1024,512]{1,0:T(8,128)(2,1)} %param.17) | copy-start | bytes 3145732
  217.5 33.7 %copy-start.18 = (bf16[2,2,2,64,384]{4,3,2,1,0:T(8,128)(2,1)S(1)}, bf16[2,2,2,64,384]{4,3,2,1,0:T(8,128)(2,1)}, u32[]{:S(2)}) copy-start(bf16[2,2,2,64,384]{4,3,2,1,0:T(8,128)(2,1)} %copy.60) | copy-start | bytes 1179652
  251.5 4.3 %copy-start.29 = (bf16[4,1024,512]{1,2,0:T(8,128)(2,1)S(1)}, bf16[4,1024,512]{1,2,0:T(8,128)(2,1)}, u32[]{:S(2)}) copy-start(bf16[4,1024,512]{1,2,0:T(8,128)(2,1)} %get-tuple-element.118) | copy-start | bytes 12582916
  265.4 80.7 %collective-permute-start.8 = (bf16[2,512,1152]{2,1,0:T(8,128)(2,1)}, bf16[2,512,1152]{2,1,0:T(8,128)(2,1)}, u32[]{:S(2)}, u32[]{:S(2)}) collective-permute-start(bf16[2,512,1152]{2,1,0:T(8,128)(2,1)} %bitcast.184), channel_id=1, source_target_pairs={{0,1},{1,0},{2,3},{3,2},{4,5},{5,4},{6,7},{7,6},{8,9},{9,8},{10,11... | collective-permute-start | bytes 7077896 | tf_op jit(solution)/shard_map/ppermute | solution.py:624
  339.7 6.4 %copy-start.3 = (bf16[2,1,512,1152]{3,2,0,1:T(8,128)(2,1)S(1)}, bf16[2,1,512,1152]{3,2,0,1:T(8,128)(2,1)}, u32[]{:S(2)}) copy-start(bf16[2,1,512,1152]{3,2,0,1:T(8,128)(2,1)} %copy.83) | copy-start | bytes 7077892
  350.8 25.1 %collective-permute-start.9 = (bf16[1,512,1152]{2,1,0:T(8,128)(2,1)}, bf16[1,512,1152]{2,1,0:T(8,128)(2,1)}, u32[]{:S(2)}, u32[]{:S(2)}) collective-permute-start(bf16[1,512,1152]{2,1,0:T(8,128)(2,1)} %constant_dynamic-slice_fusion.3), channel_id=1, source_target_pairs={{0,2},{1,3},{2,0},{3,1},{4,6},{5,7},{6,4},{7,5},{8,10},{9,11},{10,... | collective-permute-start | bytes 3538952 | tf_op jit(solution)/shard_map/ppermute | solution.py:624
  355.8 20.1 %copy-start.5 = (bf16[2,512,1152]{2,1,0:T(8,128)(2,1)S(1)}, bf16[2,512,1152]{2,1,0:T(8,128)(2,1)}, u32[]{:S(2)}) copy-start(bf16[2,512,1152]{2,1,0:T(8,128)(2,1)} %copy-done.4) | copy-start | bytes 7077892
  360.9 16.6 %copy-start.17 = (bf16[512,384]{1,0:T(8,128)(2,1)S(1)}, bf16[512,384]{1,0:T(8,128)(2,1)}, u32[]{:S(2)}) copy-start(bf16[512,384]{1,0:T(8,128)(2,1)} %convolution_convert_fusion.3) | copy-start | bytes 1179652
  377.5 40.7 %copy-start.1 = (bf16[64,3,128]{2,0,1:T(8,128)(2,1)S(1)}, bf16[64,3,128]{2,0,1:T(8,128)(2,1)}, u32[]{:S(2)}) copy-start(bf16[64,3,128]{2,0,1:T(8,128)(2,1)} %param.20) | copy-start | bytes 147460
  (18 other events, 40.0 us)

commit v3 on v2

--- a/solution.py
+++ b/solution.py
@@ -137,7 +137,7 @@
         ],
         compiler_params=pltpu.CompilerParams(vmem_limit_bytes=VMEM_LIMIT),
         cost_estimate=pl.CostEstimate(
-            flops=rows * rows * HD * heads, bytes_accessed=8 << 20, transcendentals=rows * rows
+            flops=14 * rows * rows * HD * heads, bytes_accessed=8 << 20, transcendentals=rows * rows
         ),
         name="attend",
     )(low, qa, ka, vt, start)
@@ -229,74 +229,10 @@
         out_shape=jax.ShapeDtypeStruct((rows, 3 * HD * heads), bf16),
         compiler_params=pltpu.CompilerParams(vmem_limit_bytes=VMEM_LIMIT),
         cost_estimate=pl.CostEstimate(
-            flops=2 * rows * rows * HD * heads, bytes_accessed=16 << 20, transcendentals=rows * rows
+            flops=24 * rows * rows * HD * heads, bytes_accessed=16 << 20, transcendentals=rows * rows
         ),
         name="attend_back",
     )(low, qb, ka, va, kt, g, o, start)
-
-
-def prepare_kernel(x_ref, w_ref, bias_ref, seg_ref, qa_ref, ka_ref, va_ref, vt_ref, kt_ref):
-    size = x_ref.shape[0]
-    heads = qa_ref.shape[0]
-    width = HD * heads
-    projected = dot_n(x_ref[...], w_ref[...]) + bias_ref[0:1, :]
-    queries = (projected[:, 0:width].astype(bf16).astype(f32) * HD ** (-0.5)).astype(bf16)
-    keys = projected[:, width : 2 * width].astype(bf16)
-    values = projected[:, 2 * width : 3 * width].astype(bf16)
-    number = lax.broadcasted_iota(jnp.int32, (size, 64), 1).astype(f32)
-    seg = jnp.broadcast_to(seg_ref[0:1, :].astype(f32), (8, size)).T[:, 0:1]
-    same = seg == number
-    other = jnp.where(same | (number > 31), 0.0, -1e30).astype(bf16)
-    lanes = lax.broadcasted_iota(jnp.int32, (size, 64), 1)
-    key_tail = jnp.where((same & (lanes < 32)) | ((lanes >= 32) & (lanes < 35)), 1.0, 0.0).astype(bf16)
-    value_tail = jnp.where(lanes < 3, 1.0, 0.0).astype(bf16)
-    for h in range(heads):
-        cols = slice(HD * h, HD * h + HD)
-        qa_ref[h] = jnp.concatenate([queries[:, cols], other], axis=1)
-        ka_ref[h] = jnp.concatenate([keys[:, cols], key_tail], axis=1)
-        va_ref[h] = jnp.concatenate([values[:, cols], value_tail], axis=1)
-        turned = jnp.concatenate([values[:, cols], keys[:, cols]], axis=1).astype(f32).T.astype(bf16)
-        vt_ref[h, 0:64, :] = turned[0:64, :]
-        vt_ref[h, 64:80, :] = jnp.where(
-            lax.broadcasted_iota(jnp.int32, (16, size), 0) == 0, 1.0, 0.0
-        ).astype(bf16)
-        kt_ref[h] = turned[64:128, :]
-
-
-def prepare(x, w, bias, seg_rows, size):
-    rows, width = x.shape
-    heads = w.shape[1] // (3 * HD)
-    wide = pl.BlockSpec((heads, size, 128), lambda i: (0, i, 0))
-    shape = jax.ShapeDtypeStruct((heads, rows, 128), bf16)
-    return pl.pallas_call(
-        prepare_kernel,
-        grid=(rows // size,),
-        in_specs=[
-            pl.BlockSpec((size, width), lambda i: (i, 0)),
-            pl.BlockSpec(w.shape, lambda i: (0, 0)),
-            pl.BlockSpec(bias.shape, lambda i: (0, 0)),
-            pl.BlockSpec((8, size), lambda i: (0, i)),
-        ],
-        out_specs=[
-            wide,
-            wide,
-            wide,
-            pl.BlockSpec((heads, 80, size), lambda i: (0, 0, i)),
-            pl.BlockSpec((heads, 64, size), lambda i: (0, 0, i)),
-        ],
-        out_shape=[
-            shape,
-            shape,
-            shape,
-            jax.ShapeDtypeStruct((heads, 80, rows), bf16),
-            jax.ShapeDtypeStruct((heads, 64, rows), bf16),
-        ],
-        compiler_params=pltpu.CompilerParams(vmem_limit_bytes=VMEM_LIMIT),
-        cost_estimate=pl.CostEstimate(
-            flops=2 * rows * width * w.shape[1], bytes_accessed=14 << 20, transcendentals=0
-        ),
-        name="prepare",
-    )(x, w, bias, seg_rows)
 
 
 def document_starts(seg_all):
@@ -361,66 +297,229 @@
     return pl.BlockSpec(memory_space=pl.ANY)
 
 
-def gather_kernel(x_ref, seg_ref, all_ref, segs_ref, sy, ry, ss, rs, sf, rf, sg, rg, own, own_seg, *, parts):
+def flipped(axis, mask):
+    me, index, bit = lax.axis_index(axis), lax.axis_index(axis), 1
+    while bit <= mask:
+        if mask & bit:
+            index = index + bit - 2 * bit * lax.rem(me // bit, 2)
+        bit *= 2
+    return index
+
+
+def awaited(ref, send_sem, recv_sem, peer):
+    return pltpu.make_async_remote_copy(ref, ref, send_sem, recv_sem, peer, MESH)
+
+
+def hop_masks(size):
+    hops, bit = [], size // 2
+    while bit >= 1:
+        hops.append((bit, [high + bit for high in range(0, size, 2 * bit)]))
+        bit //= 2
+    return hops
+
+
+def enter_kernel(
+    x_ref, norm_ref, bias_ref, seg_ref, w0, w1, w2, w3,
+    normed_ref, segs_ref, qa_ref, ka_ref, va_ref, vt_ref, kt_ref, f0, f1, f2, f3,
+    x_all, normed_s, qa_s, ka_s, va_s, vt_s, kt_s,
+    sy, ry, ss, rs, sf, rf, sg, rg, sw, rw, own, own_w, outs, *, parts
+):
     me, side, across, far = quad()
     rows = x_ref.shape[0]
     step = rows // parts
-    greet([{"tp": side}, {"tp": across}, {"tp": far}])
+    shards = f0.shape[0]
+    heads = qa_ref.shape[0]
+    width = HD * heads
+    shard = lax.axis_index("fsdp")
+    hops = hop_masks(shards)
+    greet(
+        [{"tp": side}, {"tp": across}, {"tp": far}]
+        + [{"fsdp": flipped("fsdp", bit)} for bit, _ in hops]
+    )
+    sent = []
 
     def rows_of(owner, part):
-        return all_ref.at[pl.ds(owner * rows + part * step, step)]
-
-    sent = []
+        return x_all.at[pl.ds(pl.multiple_of(owner * rows + part * step, step), step)]
+
+    groups = ((w0, f0), (w1, f1), (w2, f2), (w3, f3))
+    for part in range(parts):
+        mine = x_ref.at[pl.ds(part * step, step)]
+        sent.append(push(mine, rows_of(me, part), sy.at[part], ry.at[part], {"tp": across}))
+
+    def send_hop(g, hop):
+        bit, masks = hops[hop]
+        source, full = groups[g]
+        peer = {"fsdp": flipped("fsdp", bit)}
+        if hop > 0:
+            before, arrived = hops[hop - 1]
+            for mask in arrived:
+                block = full.at[flipped("fsdp", mask)]
+                awaited(block, sw.at[g, mask], rw.at[g, mask], {"fsdp": flipped("fsdp", before)}).wait_recv()
+        for mask in masks:
+            if mask == bit:
+                block = source
+            else:
+                block = full.at[flipped("fsdp", mask - bit)]
+            target = full.at[flipped("fsdp", mask - bit)]
+            sent.append(push(block, target, sw.at[g, mask], rw.at[g, mask], peer))
+
+    def end_hops(g):
+        bit, arrived = hops[-1]
+        for mask in arrived:
+            block = groups[g][1].at[flipped("fsdp", mask)]
+            awaited(block, sw.at[g, mask], rw.at[g, mask], {"fsdp": flipped("fsdp", bit)}).wait_recv()
+
+    send_hop(0, 0)
     for k, peer in enumerate((across, far, side)):
         sent.append(push(seg_ref, segs_ref.at[me], sg.at[k], rg.at[k], {"tp": peer}))
     for part in range(parts):
         mine = x_ref.at[pl.ds(part * step, step)]
-        sent.append(push(mine, rows_of(me, part), sy.at[part], ry.at[part], {"tp": across}))
+        sent.append(push(mine, rows_of(me, part), ss.at[part], rs.at[part], {"tp": side}))
+    for g in (1, 2, 3):
+        send_hop(g, 0)
+    kept = [
+        pltpu.make_async_copy(x_ref, x_all.at[pl.ds(pl.multiple_of(me * rows, rows), rows)], own.at[0]),
+        pltpu.make_async_copy(seg_ref, segs_ref.at[me], own.at[1]),
+    ] + [pltpu.make_async_copy(source, full.at[shard], own_w.at[g]) for g, (source, full) in enumerate(groups)]
+    for copy in kept:
+        copy.start()
+
+    def forward(part):
+        here = rows_of(across, part)
+        awaited(here, sy.at[part], ry.at[part], {"tp": across}).wait_recv()
+        return push(here, here, sf.at[part], rf.at[part], {"tp": side})
+
+    waves = sorted(
+        ((hop + g, g, hop) for hop in range(1, len(hops)) for g in range(4)), key=lambda w: (w[0], w[1])
+    )
+    first_last = [n for n, wave in enumerate(waves) if wave[1] == 0][-1]
+    for _, g, hop in waves[: first_last + 1]:
+        send_hop(g, hop)
+    sent.append(forward(0))
+    for k, peer in enumerate((across, far, side)):
+        awaited(segs_ref.at[peer], sg.at[k], rg.at[k], {"tp": peer}).wait_recv()
     for part in range(parts):
-        mine = x_ref.at[pl.ds(part * step, step)]
-        sent.append(push(mine, rows_of(me, part), ss.at[part], rs.at[part], {"tp": side}))
-    keep = pltpu.make_async_copy(x_ref, all_ref.at[pl.ds(me * rows, rows)], own)
-    keep.start()
-    keep_seg = pltpu.make_async_copy(seg_ref, segs_ref.at[me], own_seg)
-    keep_seg.start()
-    for part in range(parts):
-        here = rows_of(across, part)
-        pltpu.make_async_remote_copy(
-            here, here, sy.at[part], ry.at[part], {"tp": across}, MESH
-        ).wait_recv()
-        sent.append(push(here, here, sf.at[part], rf.at[part], {"tp": side}))
-    for part in range(parts):
-        there = rows_of(side, part)
-        pltpu.make_async_remote_copy(there, there, ss.at[part], rs.at[part], {"tp": side}, MESH).wait_recv()
-    for part in range(parts):
-        there = rows_of(far, part)
-        pltpu.make_async_remote_copy(there, there, sf.at[part], rf.at[part], {"tp": side}, MESH).wait_recv()
-    for k, peer in enumerate((across, far, side)):
-        there = segs_ref.at[peer]
-        pltpu.make_async_remote_copy(there, there, sg.at[k], rg.at[k], {"tp": peer}, MESH).wait_recv()
-    keep.wait()
-    keep_seg.wait()
+        awaited(rows_of(side, part), ss.at[part], rs.at[part], {"tp": side}).wait_recv()
+    for copy in kept:
+        copy.wait()
+    later = waves[first_last + 1 :]
+    for _, g, hop in later[: (len(later) + 1) // 2]:
+        send_hop(g, hop)
+    sent.append(forward(1))
+    end_hops(0)
+
+    gain, shift = norm_ref[0:1, :], norm_ref[1:2, :]
+    bias = bias_ref[0:1, :]
+    number = lax.broadcasted_iota(jnp.int32, (step, 64), 1)
+    number_f = number.astype(f32)
+    key_ones = (number >= 32) & (number < 35)
+    value_tail = jnp.where(number < 3, 1.0, 0.0).astype(bf16)
+    ones_row = jnp.where(lax.broadcasted_iota(jnp.int32, (16, step), 0) == 0, 1.0, 0.0).astype(bf16)
+
+    def copies_out(owner, part):
+        row = pl.multiple_of(owner * rows + part * step, step)
+        slot = owner * parts + part
+        span = pl.ds(row, step)
+        pairs = [(normed_s.at[span], normed_ref.at[span])]
+        for a, b in ((qa_s, qa_ref), (ka_s, ka_ref), (va_s, va_ref)):
+            pairs.append((a.at[:, span, :], b.at[:, span, :]))
+        for a, b in ((vt_s, vt_ref), (kt_s, kt_ref)):
+            pairs.append((a.at[:, :, span], b.at[:, :, span]))
+        return [pltpu.make_async_copy(a, b, outs.at[n, slot]) for n, (a, b) in enumerate(pairs)]
+
+    def compute(owner, part):
+        row = pl.multiple_of(owner * rows + part * step, step)
+        span = pl.ds(row, step)
+        x = x_all[span, :].astype(f32)
+        centred = x - jnp.mean(x, axis=-1, keepdims=True)
+        inverse = lax.rsqrt(jnp.mean(centred * centred, axis=-1, keepdims=True) + epsilon)
+        normed = (centred * inverse * gain + shift).astype(bf16)
+        normed_s[span, :] = normed
+        weights = f0[...].reshape(shards * f0.shape[1], 3 * width)
+        projected = dot_n(normed, weights) + bias
+        queries = (projected[:, 0:width].astype(bf16).astype(f32) * HD ** (-0.5)).astype(bf16)
+        keys = projected[:, width : 2 * width].astype(bf16)
+        values = projected[:, 2 * width : 3 * width].astype(bf16)
+        seg = segs_ref[owner, 0:1, pl.ds(pl.multiple_of(part * step, step), step)].astype(f32)
+        seg = jnp.broadcast_to(seg, (8, step)).T[:, 0:1]
+        same = (seg == number_f) & (number < 32)
+        other = jnp.where(same | (number > 31), 0.0, -1e30).astype(bf16)
+        key_tail = jnp.where(same | key_ones, 1.0, 0.0).astype(bf16)
+        for h in range(heads):
+            cols = slice(HD * h, HD * h + HD)
+            qa_s[h, span, :] = jnp.concatenate([queries[:, cols], other], axis=1)
+            ka_s[h, span, :] = jnp.concatenate([keys[:, cols], key_tail], axis=1)
+            va_s[h, span, :] = jnp.concatenate([values[:, cols], value_tail], axis=1)
+            turned = jnp.concatenate([values[:, cols], keys[:, cols]], axis=1).astype(f32).T.astype(bf16)
+            vt_s[h, 0:64, span] = turned[0:64, :]
+            vt_s[h, 64:80, span] = ones_row
+            kt_s[h, :, span] = turned[64:128, :]
+        for copy in copies_out(owner, part):
+            copy.start()
+
+    def near(k, carry):
+        part = lax.rem(k, parts)
+        compute(me + (k // parts) * (side - me), part)
+        return carry
+
+    lax.fori_loop(0, 2 * parts, near, 0)
+    for _, g, hop in later[(len(later) + 1) // 2 :]:
+        send_hop(g, hop)
+
+    def distant(part, carry):
+        compute(across, part)
+        awaited(rows_of(far, part), sf.at[part], rf.at[part], {"tp": side}).wait_recv()
+        compute(far, part)
+        return carry
+
+    for part in range(2, parts):
+        sent.append(forward(part))
+        lax.fori_loop(part - 2, part - 1, distant, 0)
+    lax.fori_loop(parts - 2, parts, distant, 0)
+    for g in (1, 2, 3):
+        end_hops(g)
+
+    def drain(k, carry):
+        for copy in copies_out(k // parts, lax.rem(k, parts)):
+            copy.wait()
+        return carry
+
+    lax.fori_loop(0, 4 * parts, drain, 0)
     for copy in sent:
         copy.wait_send()
 
 
-def gather_rows(x, segments, number, parts=4):
+def enter(x, norm_rows, bias_rows, segments, weights, number, parts=4):
     rows, width = x.shape
+    seq_rows = 4 * rows
+    shards = lax.axis_size("fsdp")
+    heads = weights[0].shape[1] // (3 * HD)
     dma = pltpu.SemaphoreType.DMA
+    wide = (heads, seq_rows, 128)
+    full = [(shards, *w.shape) for w in weights]
+    shapes = [(seq_rows, width), wide, wide, wide, (heads, 80, seq_rows), (heads, 64, seq_rows)]
+    made = [jax.ShapeDtypeStruct(s, bf16) for s in shapes]
     return comm_call(
-        functools.partial(gather_kernel, parts=parts),
-        "gather_rows",
+        functools.partial(enter_kernel, parts=parts),
+        "enter",
         number,
-        [
-            jax.ShapeDtypeStruct((4 * rows, width), x.dtype),
-            jax.ShapeDtypeStruct((4, *segments.shape), segments.dtype),
-        ],
-        [in_vmem(), in_vmem()],
-        [anywhere(), anywhere()],
-        [dma((parts,))] * 6 + [dma((3,))] * 2 + [dma, dma],
+        [made[0], jax.ShapeDtypeStruct((4, *segments.shape), segments.dtype)]
+        + made[1:]
+        + [jax.ShapeDtypeStruct(s, bf16) for s in full],
+        [in_vmem()] * 8,
+        [anywhere(), in_vmem()] + [anywhere()] * 5 + [in_vmem()] + [anywhere()] * 3,
+        [pltpu.VMEM((seq_rows, width), bf16)]
+        + [pltpu.VMEM(s, bf16) for s in shapes]
+        + [dma((parts,))] * 6
+        + [dma((3,))] * 2
+        + [dma((4, shards))] * 2
+        + [dma((2,)), dma((4,)), dma((6, 4 * parts))],
         60 << 20,
         x,
+        norm_rows,
+        bias_rows,
         segments,
+        *weights,
     )
 
 
@@ -649,32 +748,37 @@
     shard_rows = qkv_weight.shape[0]
     head_cols = qkv_weight.shape[2]
     hidden_cols = fc_weight.shape[1]
-    qkv_full = spread(qkv_weight.reshape(shard_rows, 3 * head_cols), "fsdp").reshape(
-        model_width, 3 * head_cols
-    )
-    packed = jnp.concatenate([fc_weight, proj_weight.T, out_weight.T], axis=1)
-    packed = spread(packed, "fsdp").reshape(model_width, packed.shape[1])
-    packed = spread(packed, "tp")
+    qv_here = lax.dynamic_slice_in_dim(qv_bias, tp_index * head_cols, head_cols, 1).astype(f32)
+    bias_here = jnp.concatenate([qv_here[0], jnp.zeros((head_cols,), f32), qv_here[1]])
+    bias_rows = jnp.broadcast_to(bias_here[None], (8, 3 * head_cols))
+    norm_rows = jnp.concatenate(
+        [first_gain[None], first_shift[None], jnp.zeros((6, model_width), bf16)], axis=0
+    ).astype(f32)
+    seq_normed, seg_parts, qa, ka, va, vt, kt, qkv_full, fc_slice, proj_slice, out_slice = enter(
+        inputs,
+        norm_rows,
+        bias_rows,
+        segments,
+        (qkv_weight.reshape(shard_rows, 3 * head_cols), fc_weight, proj_weight.T, out_weight.T),
+        0,
+    )
+    qkv_full = qkv_full.reshape(model_width, 3 * head_cols)
+    packed = jnp.concatenate([fc_slice, proj_slice, out_slice], axis=2)
+    packed = spread(packed.reshape(model_width, packed.shape[2]), "tp")
     fc_full = packed[:, :, 0:hidden_cols]
     proj_full = packed[:, :, hidden_cols : 2 * hidden_cols]
     out_full = packed[:, :, 2 * hidden_cols :]
 
     resid_in = inputs.astype(f32)
-    normed_one, hat_one, inv_one = layer_norm(
+    _, hat_one, inv_one = layer_norm(
         resid_in, first_gain.astype(f32), first_shift.astype(f32)
     )
-    seq_normed, seg_parts = gather_rows(normed_one.astype(bf16), segments, 0)
     seq_rows = seq_normed.shape[0]
     seg_all = seg_parts.reshape(seq_rows)
     start = document_starts(seg_all)
     size = min(BLOCK, seq_rows)
     low = start[::size] // size
     start_rows = jnp.broadcast_to(start[None], (8, seq_rows))
-    seg_rows = jnp.broadcast_to(seg_all[None], (8, seq_rows))
-    qv_here = lax.dynamic_slice_in_dim(qv_bias, tp_index * head_cols, head_cols, 1).astype(f32)
-    bias_here = jnp.concatenate([qv_here[0], jnp.zeros((head_cols,), f32), qv_here[1]])
-    bias_rows = jnp.broadcast_to(bias_here[None], (8, 3 * head_cols))
-    qa, ka, va, vt, kt = prepare(seq_normed, qkv_full, bias_rows, seg_rows, size)
     attn_out, qb = attend(low, qa, ka, vt, start_rows, size)
     attn_here = exchange(attn_out, 1, "exchange_out")
 

time: 422 us -> 382 us (0.905)
  starting transfers between devices: 16.5 us -> 1 us
  other arithmetic: 37.2 us -> 28.8 us
  Pallas kernels: 243 us -> 235 us
  waiting for transfers between devices: 44.2 us -> 39.4 us
    ppermute x8 -> x2, starting transfers between devices: 16 us -> 0.73 us  [spread(): other = lax.ppermute(value, axis, [(n, n ^ bit) for n in range(size)])]
    pallas_call x1 -> x0, Pallas kernels: 10.7 us -> none  [prepare(): pl.pallas_call(prepare_kernel, grid=(rows // size,), in_specs=[pl.BlockSp...]
    ppermute x8 -> x2, waiting for transfers between devices: 29.2 us -> 24.8 us  [spread(): other = lax.ppermute(value, axis, [(n, n ^ bit) for n in range(size)])]
    another operation x16 -> x4, other arithmetic: 8.46 us -> 6.1 us  [spread(): jnp.stack([jnp.where(high, other, value), jnp.where(high, value, other)],...]
    unnamed x73 -> x67, local copies, waits for them, and re-layouts: 10.1 us -> 9.3 us
  transfers between devices with their start and end apart: 10 -> 4, of which waited for: 6 -> 2; matrix products, arithmetic and copies ran while one was open for 11% -> 11% of each run, Pallas kernels for 38% -> 39%
where the time goes in v3:
time: 382 us; the launch traced here: 375 us
  Pallas kernels  235 us (62%)
  matrix products  39.7 us (10%)
  waiting for transfers between devices  39.4 us (10%)
  local copies, waits for them, and re-layouts  29.6 us (8%)
  other arithmetic  28.8 us (8%)
    pallas_call x6, Pallas kernels, comm_call(): pl.pallas_call(kernel, out_shape=out_shape, in_specs=in_specs, out_specs=...  181 us
    pallas_call x1, Pallas kernels, attend_back(): pl.pallas_call(functools.partial(attend_back_kernel, size=size, blocks=ro...  30.8 us
    ppermute x2, waiting for transfers between devices, spread(): other = lax.ppermute(value, axis, [(n, n ^ bit) for n in range(size)])  24.8 us
    pallas_call x1, Pallas kernels, attend(): pl.pallas_call(functools.partial(attend_kernel, size=size, blocks=rows //...  23.4 us
    ppermute x2, waiting for transfers between devices, fold_bits(): arrived = lax.ppermute(sent, axis, [(n, n ^ bit) for n in range(size)])  14.6 us
    unnamed x67, local copies, waits for them, and re-layouts  9.3 us
  transfers between devices with their start and end apart: 4, of which 2 were waited for; matrix products, arithmetic and copies ran while one was open for 11% of the time, Pallas kernels for 39%

profile of v3, /device:TPU:0, one launch (start us, length us, event | category | flops | bytes accessed | tf_op | source)
XLA Modules:
  0.0 375.4 jit_solution(15717193040190120129)
XLA Ops:
  4.8 53.4 %enter.1 = (bf16[4096,512]{1,0:T(8,128)(2,1)}, s32[4,1,1024]{2,1,0:T(1,128)}, bf16[2,4096,128]{2,1,0:T(8,128)(2,1)}, bf16[2,4096,128]{2,1,0:T(8,128)(2,1)}, bf16...) custom-call(bf16[1024,512]{1,0:T(8,128)(2,1)} %x_ref.1, ...), custom_call_target="tpu_custom_call" | custom-call | bytes 62914560 | tf_op jit(solution)/shard_map/enter/pallas_call | solution.py:278
  61.9 24.8 %collective-permute-done = bf16[512,1152]{1,0:T(8,128)(2,1)} collective-permute-done((bf16[512,1152]{1,0:T(8,128)(2,1)S(1)}, bf16[512,1152]{1,0:T(8,128)(2,1)}, u32[]{:S(2)}, u32[]{:S(2)}) %collective-permute-start) | collective-permute-done | bytes 1179680 | tf_op jit(solution)/shard_map/ppermute | solution.py:710
  90.8 23.4 %attend.1 = (bf16[4096,128]{1,0:T(8,128)(2,1)}, bf16[2,4096,128]{2,1,0:T(8,128)(2,1)}) custom-call(s32[8]{0:T(128)} %and_select_fusion.low_ref, bf16[2,4096,128]{2,1,0:T(8,128)(2,1)} %get-tuple-element.28.qa_ref, bf16[2,4096,128]{2,1,0:T(8,128)(2,1)} %get-tuple-element.29.ka_ref, bf16[2,80,4096]{2,1,0:T(8,128)(2,1)} %get-tuple-element.30.vt_ref, ...), custom_call_target="tpu_custom_call" | custom-call | flops 30064771072 | bytes 8388608 | tf_op jit(solution)/shard_map/attend/pallas_call | solution.py:124
  114.3 16.7 %exchange_out.1 = bf16[4,1024,128]{2,1,0:T(8,128)(2,1)} custom-call(bf16[4096,128]{1,0:T(8,128)(2,1)} %get-tuple-element.31.x_ref.o_ref), custom_call_target="tpu_custom_call" | custom-call | bytes 31457280 | tf_op jit(solution)/shard_map/exchange_out/pallas_call | solution.py:278
  137.7 4.9 %fusion.1 = (bf16[4,1024,512]{1,2,0:T(8,128)(2,1)S(1)}, f32[4,512,1024]{2,1,0:T(8,128)S(1)}) fusion(f32[4,512]{1,0:T(4,128)S(1)} %reshape.179, f32[1024,512]{1,0:T(8,128)S(1)} %get-tuple-element.112, f32[512]{0:T(512)S(1)} %convert_element_type.126, f32[512]{0:T(512)S(1)} %convert_element_type.125, f32[1024]{0:T(1024)S(1)} %add_rsqrt_fusion.1, ...), kind=kOutput, calls=%fused_computation.4 | convolution fusion | flops 2164785152 | bytes 16797696 | tf_op jit(solution)/shard_map/sd,tdf->tsf/dot_general | solution.py:794
  142.6 7.0 %convert_reduce_fusion = (f32[4,512]{1,0:T(4,128)S(1)}, bf16[4,1024,512]{1,2,0:T(8,128)(2,1)S(1)}) fusion(f32[4,512,1024]{2,1,0:T(8,128)S(1)} %get-tuple-element.115, f32[4,512]{1,0:T(4,128)S(1)} %reshape.179, bf16[1024,512]{1,0:T(8,128)(2,1)S(1)} %copy-done.12, bf16[4,512,1152]{2,1,0:T(8,128)(2,1)S(1)} %bitcast.143), kind=kOutput, calls=%fused_computation.5 | convolution fusion | flops 2174744576 | bytes 15745024 | tf_op jit(solution)/shard_map/sd,tdf->tsf/dot_general | solution.py:805
  149.6 2.6 convert_bitcast_fusion.1
  152.2 3.3 fusion.16
  160.1 2.5 constant_dynamic-slice_fusion.1
  162.6 4.3 %copy.66 = bf16[2,1,512,1152]{3,2,0,1:T(8,128)(2,1)} copy(bf16[2,1,512,1152]{2,3,1,0:T(8,128)(2,1)} %get-tuple-element.93) | data formatting | bytes 4718592 | tf_op jit(solution)/shard_map/jit(dynamic_index_in_dim)/dynamic_slice | solution.py:721
  166.9 4.4 %copy.76 = bf16[2,1,512,1152]{3,2,0,1:T(8,128)(2,1)} copy(bf16[2,1,512,1152]{2,3,1,0:T(8,128)(2,1)} %get-tuple-element.92) | data formatting | bytes 4718592
  171.3 2.8 fusion.28
  176.3 16.6 %exchange_grad.1 = bf16[4,1024,128]{2,1,0:T(8,128)(2,1)} custom-call(bf16[4096,128]{1,0:T(8,128)(2,1)} %bitcast.149), custom_call_target="tpu_custom_call" | custom-call | bytes 31457280 | tf_op jit(solution)/shard_map/exchange_grad/pallas_call | solution.py:278
  193.0 30.8 %attend_back.1 = bf16[4096,384]{1,0:T(8,128)(2,1)} custom-call(s32[8]{0:T(128)} %and_select_fusion.low_ref, bf16[2,4096,128]{2,1,0:T(8,128)(2,1)} %get-tuple-element.35.qb_ref, bf16[2,4096,128]{2,1,0:T(8,128)(2,1)} %get-tuple-element.29.ka_ref, bf16[2,4096,128]{2,1,0:T(8,128)(2,1)} %get-tuple-element.36.va_ref, ...), custom_call_target="tpu_custom_call" | custom-call | flops 51539607552 | bytes 16777216 | tf_op jit(solution)/shard_map/attend_back/pallas_call | solution.py:215
  223.8 2.6 convert_reduce_fusion.1
  226.6 4.4 %convolution_convert_fusion.x_ref = bf16[4096,512]{1,0:T(8,128)(2,1)} fusion(bf16[4096,384]{1,0:T(8,128)(2,1)S(1)} %copy-done.11, bf16[512,384]{1,0:T(8,128)(2,1)S(1)} %bitcast.164), kind=kOutput, calls=%fused_computation.8 | convolution fusion | flops 1612709888 | bytes 7733248 | tf_op jit(solution)/shard_map/sj,dj->sd/dot_general | solution.py:838
  231.1 29.6 %fold_rows.1 = f32[1024,512]{1,0:T(8,128)} custom-call(bf16[4096,512]{1,0:T(8,128)(2,1)} %convolution_convert_fusion.x_ref), custom_call_target="tpu_custom_call" | custom-call | bytes 62914560 | tf_op jit(solution)/shard_map/fold_rows/pallas_call | solution.py:278
  260.8 2.7 fusion.13
  264.2 30.1 %all_sum.1 = f32[48,128]{1,0:T(8,128)} custom-call(f32[48,128]{1,0:T(8,128)} %bitcast.159), custom_call_target="tpu_custom_call" | custom-call | bytes 10485760 | tf_op jit(solution)/shard_map/all_sum/pallas_call | solution.py:278
  297.6 5.7 %convolution_convert_fusion.3 = bf16[512,384]{1,0:T(8,128)(2,1)S(1)} fusion(bf16[4096,512]{1,0:T(8,128)(2,1)} %get-tuple-element.39, bf16[4096,384]{1,0:T(8,128)(2,1)} %attend_back.1), kind=kOutput, calls=%fused_computation.63 | convolution fusion | flops 1610809344 | bytes 7733248 | tf_op jit(solution)/shard_map/sd,sj->dj/dot_general | solution.py:836
  309.5 3.7 fusion.12
  313.4 5.1 %fusion.18 = bf16[1024,512]{1,0:T(8,128)(2,1)} fusion(f32[1024,512]{1,0:T(8,128)S(1)} %copy-done.7, bf16[4,1024,512]{1,2,0:T(8,128)(2,1)S(1)} %copy-done.27, bf16[4,512,1152]{2,1,0:T(8,128)(2,1)} %bitcast.146, f32[512]{0:T(512)S(1)} %copy-done.20), kind=kOutput, calls=%fused_computation.41 | convolution fusion | flops 2149056512 | bytes 9439232 | tf_op jit(solution)/shard_map/tsf,tdf->sd/dot_general | solution.py:801
  318.5 14.6 %collective-permute-done.3 = bf16[1,512,1152]{2,1,0:T(8,128)(2,1)} collective-permute-done((bf16[1,512,1152]{2,1,0:T(8,128)(2,1)}, bf16[1,512,1152]{2,1,0:T(8,128)(2,1)}, u32[]{:S(2)}, u32[]{:S(2)}) %collective-permute-start.3) | collective-permute-done | bytes 1179680 | tf_op jit(solution)/shard_map/ppermute | solution.py:723
  336.0 34.3 %fold_shards.1 = f32[64,1536]{1,0:T(8,128)} custom-call(bf16[8,64,1536]{2,1,0:T(8,128)(2,1)} %pad_maximum_fusion.3.x_ref), custom_call_target="tpu_custom_call" | custom-call | bytes 62914560 | tf_op jit(solution)/shard_map/fold_shards/pallas_call | solution.py:278
  (135 shorter events, 43.3 us)
Async XLA Ops:
  0.7 59.7 %copy-start.19 = (bf16[512]{0:T(512)(128)(2,1)S(1)}, bf16[512]{0:T(512)(128)(2,1)}, u32[]{:S(2)}) copy-start(bf16[512]{0:T(512)(128)(2,1)} %param.18) | copy-start | bytes 3076
  59.6 27.1 %collective-permute-start = (bf16[512,1152]{1,0:T(8,128)(2,1)S(1)}, bf16[512,1152]{1,0:T(8,128)(2,1)}, u32[]{:S(2)}, u32[]{:S(2)}) collective-permute-start(bf16[512,1152]{1,0:T(8,128)(2,1)S(1)} %bitcast.147), channel_id=1, source_target_pairs={{0,2},{1,3},{2,0},{3,1},{4,6},{5,7},{6,4},{7,5},{8,10},{9,11},{10,... | collective-permute-start | bytes 3538952 | tf_op jit(solution)/shard_map/ppermute | solution.py:710
  90.2 42.3 %collective-permute-start.1 = (bf16[2,512,1152]{2,1,0:T(8,128)(2,1)}, bf16[2,512,1152]{2,1,0:T(8,128)(2,1)}, u32[]{:S(2)}, u32[]{:S(2)}) collective-permute-start(bf16[2,512,1152]{2,1,0:T(8,128)(2,1)} %pad_maximum_fusion.2), channel_id=1, source_target_pairs={{0,1},{1,0},{2,3},{3,2},{4,5},{5,4},{6,7},{7,6},{8,9},{9,8},{10,11... | collective-permute-start | bytes 7077896 | tf_op jit(solution)/shard_map/ppermute | solution.py:710
  114.2 16.8 %copy-start.21 = (bf16[512]{0:T(512)(128)(2,1)S(1)}, bf16[512]{0:T(512)(128)(2,1)}, u32[]{:S(2)}) copy-start(bf16[512]{0:T(512)(128)(2,1)} %param.23) | copy-start | bytes 3076
  114.2 16.8 %copy-start.22 = (bf16[512]{0:T(512)(128)(2,1)S(1)}, bf16[512]{0:T(512)(128)(2,1)}, u32[]{:S(2)}) copy-start(bf16[512]{0:T(512)(128)(2,1)} %param.24) | copy-start | bytes 3076
  114.2 16.8 %copy-start.18 = (bf16[2048]{0:T(1024)(128)(2,1)S(1)}, bf16[2048]{0:T(1024)(128)(2,1)}, u32[]{:S(2)}) copy-start(bf16[2048]{0:T(1024)(128)(2,1)} %param.27) | copy-start | bytes 12292
  114.2 16.9 %copy-start.23 = (bf16[512]{0:T(512)(128)(2,1)S(1)}, bf16[512]{0:T(512)(128)(2,1)}, u32[]{:S(2)}) copy-start(bf16[512]{0:T(512)(128)(2,1)} %param.25) | copy-start | bytes 3076
  114.2 16.9 %copy-start.24 = (bf16[512]{0:T(512)(128)(2,1)S(1)}, bf16[512]{0:T(512)(128)(2,1)}, u32[]{:S(2)}) copy-start(bf16[512]{0:T(512)(128)(2,1)} %param.29) | copy-start | bytes 3076
  114.3 17.4 %copy-start.17 = (s32[1,1024]{1,0:T(1,128)S(1)}, s32[1,1024]{1,0:T(1,128)}, u32[]{:S(2)}) copy-start(s32[1,1024]{1,0:T(1,128)} %seg_ref.1) | copy-start | bytes 12292
  114.3 17.5 %copy-start.2 = (bf16[1024,512]{1,0:T(8,128)(2,1)S(1)}, bf16[1024,512]{1,0:T(8,128)(2,1)}, u32[]{:S(2)}) copy-start(bf16[1024,512]{1,0:T(8,128)(2,1)} %x_ref.1) | copy-start | bytes 3145732
  135.5 16.6 %copy-start.8 = (bf16[2,2,512,1152]{3,2,1,0:T(8,128)(2,1)}, bf16[2,2,512,1152]{3,2,1,0:T(8,128)(2,1)S(1)}, u32[]{:S(2)}) copy-start(bf16[2,2,512,1152]{3,2,1,0:T(8,128)(2,1)S(1)} %copy.56) | copy-start | bytes 14155780
  137.2 18.3 %copy-start.6 = (f32[1024,512]{1,0:T(8,128)}, f32[1024,512]{1,0:T(8,128)S(1)}, u32[]{:S(2)}) copy-start(f32[1024,512]{1,0:T(8,128)S(1)} %get-tuple-element.112) | copy-start | bytes 6291460
  137.7 4.9 %copy-start.12 = (bf16[1024,512]{1,0:T(8,128)(2,1)S(1)}, bf16[1024,512]{1,0:T(8,128)(2,1)}, u32[]{:S(2)}) copy-start(bf16[1024,512]{1,0:T(8,128)(2,1)} %param.17) | copy-start | bytes 3145732
  142.5 14.8 %copy-start.26 = (bf16[4,1024,512]{1,2,0:T(8,128)(2,1)}, bf16[4,1024,512]{1,2,0:T(8,128)(2,1)S(1)}, u32[]{:S(2)}) copy-start(bf16[4,1024,512]{1,2,0:T(8,128)(2,1)S(1)} %get-tuple-element.114) | copy-start | bytes 12582916
  166.9 136.3 %collective-permute-start.2 = (bf16[2,512,1152]{2,1,0:T(8,128)(2,1)}, bf16[2,512,1152]{2,1,0:T(8,128)(2,1)}, u32[]{:S(2)}, u32[]{:S(2)}) collective-permute-start(bf16[2,512,1152]{2,1,0:T(8,128)(2,1)} %bitcast.150), channel_id=1, source_target_pairs={{0,1},{1,0},{2,3},{3,2},{4,5},{5,4},{6,7},{7,6},{8,9},{9,8},{10,11... | collective-permute-start | bytes 7077896 | tf_op jit(solution)/shard_map/ppermute | solution.py:723
  193.0 33.5 %copy-start.25 = (bf16[8,64,384]{2,1,0:T(8,128)(2,1)S(1)}, bf16[8,64,384]{2,1,0:T(8,128)(2,1)}, u32[]{:S(2)}) copy-start(bf16[8,64,384]{2,1,0:T(8,128)(2,1)} %get-tuple-element.38) | copy-start | bytes 1179652
  231.1 29.7 %copy-start.16 = (f32[512]{0:T(512)S(1)}, f32[512]{0:T(512)}, u32[]{:S(2)}) copy-start(f32[512]{0:T(512)} %convert_element_type.138) | copy-start | bytes 6148
  297.6 5.7 %copy-start.3 = (bf16[2,1,512,1152]{3,2,0,1:T(8,128)(2,1)S(1)}, bf16[2,1,512,1152]{3,2,0,1:T(8,128)(2,1)}, u32[]{:S(2)}) copy-start(bf16[2,1,512,1152]{3,2,0,1:T(8,128)(2,1)} %copy.76) | copy-start | bytes 7077892
  308.0 25.1 %collective-permute-start.3 = (bf16[1,512,1152]{2,1,0:T(8,128)(2,1)}, bf16[1,512,1152]{2,1,0:T(8,128)(2,1)}, u32[]{:S(2)}, u32[]{:S(2)}) collective-permute-start(bf16[1,512,1152]{2,1,0:T(8,128)(2,1)} %constant_dynamic-slice_fusion.2), channel_id=1, source_target_pairs={{0,2},{1,3},{2,0},{3,1},{4,6},{5,7},{6,4},{7,5},{8,10},{9,11},{10,... | collective-permute-start | bytes 3538952 | tf_op jit(solution)/shard_map/ppermute | solution.py:723
  309.5 3.7 copy-start.7
  309.5 3.7 copy-start.20
  309.5 3.9 %copy-start.27 = (bf16[4,1024,512]{1,2,0:T(8,128)(2,1)S(1)}, bf16[4,1024,512]{1,2,0:T(8,128)(2,1)}, u32[]{:S(2)}) copy-start(bf16[4,1024,512]{1,2,0:T(8,128)(2,1)} %copy-done.26) | copy-start | bytes 12582916
  313.4 19.7 %copy-start.5 = (bf16[2,512,1152]{2,1,0:T(8,128)(2,1)S(1)}, bf16[2,512,1152]{2,1,0:T(8,128)(2,1)}, u32[]{:S(2)}) copy-start(bf16[2,512,1152]{2,1,0:T(8,128)(2,1)} %copy-done.4) | copy-start | bytes 7077892
  334.7 40.3 %copy-start.1 = (bf16[64,3,128]{2,0,1:T(8,128)(2,1)S(1)}, bf16[64,3,128]{2,0,1:T(8,128)(2,1)}, u32[]{:S(2)}) copy-start(bf16[64,3,128]{2,0,1:T(8,128)(2,1)} %param.20) | copy-start | bytes 147460
  (9 other events, 16.7 us)

commit v4 on v3

--- a/solution.py
+++ b/solution.py
@@ -523,96 +523,292 @@
     )
 
 
-def exchange_kernel(x_ref, out_ref, sems, rems, own):
+def exchange_out_kernel(x_ref, o0, o1, o2, c0, c1, c2, out_ref, g0, g1, g2, sems, rems, ws, wr, own):
     me, side, across, far = quad()
     rows = x_ref.shape[0] // 4
     greet([{"tp": side}, {"tp": across}, {"tp": far}])
-    sent = []
-    for k, peer in enumerate((far, across, side)):
-        mine = x_ref.at[pl.ds(peer * rows, rows)]
-        sent.append(push(mine, out_ref.at[me], sems.at[k], rems.at[k], {"tp": peer}))
-    keep = pltpu.make_async_copy(x_ref.at[pl.ds(me * rows, rows)], out_ref.at[me], own)
-    keep.start()
-    for k, peer in enumerate((far, across, side)):
-        there = out_ref.at[peer]
-        pltpu.make_async_remote_copy(there, there, sems.at[k], rems.at[k], {"tp": peer}, MESH).wait_recv()
-    keep.wait()
+    peers = {1: side, 2: across, 3: far}
+
+    def mine(owner):
+        return x_ref.at[pl.ds(pl.multiple_of(owner * rows, rows), rows)]
+
+    weights = ((o0, c0, g0), (o1, c1, g1), (o2, c2, g2))
+    sent = [push(mine(peers[k]), out_ref.at[k], sems.at[k], rems.at[k], {"tp": peers[k]}) for k in (3, 2, 1)]
+    for n, (here, over, full) in enumerate(weights):
+        sent.append(push(here, full.at[1], ws.at[0, n], wr.at[0, n], {"tp": side}))
+        sent.append(push(over, full.at[3], ws.at[1, n], wr.at[1, n], {"tp": side}))
+    kept = [pltpu.make_async_copy(mine(me), out_ref.at[0], own.at[0])]
+    for n, (here, over, full) in enumerate(weights):
+        kept.append(pltpu.make_async_copy(here, full.at[0], own.at[2 * n + 1]))
+        kept.append(pltpu.make_async_copy(over, full.at[2], own.at[2 * n + 2]))
+    for copy in kept:
+        copy.start()
+    for copy in kept:
+        copy.wait()
     for copy in sent:
-        copy.wait_send()
-
-
-def exchange(x, number, name):
+        copy.wait()
+
+
+def exchange_out(x, own, over, number):
     rows, width = x.shape
     dma = pltpu.SemaphoreType.DMA
     return comm_call(
-        exchange_kernel,
-        name,
+        exchange_out_kernel,
+        "exchange_out",
         number,
-        jax.ShapeDtypeStruct((4, rows // 4, width), x.dtype),
-        [in_vmem()],
-        in_vmem(),
-        [dma((3,)), dma((3,)), dma],
-        30 << 20,
+        [jax.ShapeDtypeStruct((4, rows // 4, width), x.dtype)]
+        + [jax.ShapeDtypeStruct((4, *w.shape), w.dtype) for w in own],
+        [in_vmem()] * 7,
+        [in_vmem()] * 4,
+        [dma((4,)), dma((4,)), dma((2, 3)), dma((2, 3)), dma((7,))],
+        60 << 20,
         x,
-    )
-
-
-def fold_kernel(x_ref, out_ref, sum_buf, sa, ra, sb, rb, sy, ry, side_far, side_own, over, *, parts):
+        *own,
+        *over,
+    )
+
+
+def exchange_grad_kernel(
+    x_ref, g0, g1, g2, out_ref, k0, k1, k2, a0, a1, a2, sems, rems, ws, wr, own, *boxes
+):
     me, side, across, far = quad()
-    rows = out_ref.shape[0]
-    step = rows // parts
-    greet([{"tp": side}, {"tp": across}])
-
-    def piece(owner, part):
-        return pl.ds(owner * rows + part * step, step)
-
-    sent = []
-    for part in range(parts):
-        here = pl.ds(part * step, step)
-        sent.append(
-            push(x_ref.at[piece(far, part)], side_far.at[here], sa.at[part], ra.at[part], {"tp": side})
-        )
-    for part in range(parts):
-        here = pl.ds(part * step, step)
-        sent.append(
-            push(x_ref.at[piece(side, part)], side_own.at[here], sb.at[part], rb.at[part], {"tp": side})
-        )
-    for part in range(parts):
-        here = pl.ds(part * step, step)
-        block = side_far.at[here]
-        pltpu.make_async_remote_copy(block, block, sa.at[part], ra.at[part], {"tp": side}, MESH).wait_recv()
-        total = x_ref[piece(across, part), :].astype(f32) + side_far[here, :].astype(f32)
-        sum_buf[here, :] = total.astype(sum_buf.dtype)
-        sent.append(push(sum_buf.at[here], over.at[here], sy.at[part], ry.at[part], {"tp": across}))
-    for part in range(parts):
-        here = pl.ds(part * step, step)
-        block = side_own.at[here]
-        pltpu.make_async_remote_copy(block, block, sb.at[part], rb.at[part], {"tp": side}, MESH).wait_recv()
-        out_ref[here, :] = x_ref[piece(me, part), :].astype(f32) + side_own[here, :].astype(f32)
-    for part in range(parts):
-        here = pl.ds(part * step, step)
-        block = over.at[here]
-        pltpu.make_async_remote_copy(block, block, sy.at[part], ry.at[part], {"tp": across}, MESH).wait_recv()
-        out_ref[here, :] += over[here, :].astype(f32)
+    greet([{"tp": side}, {"tp": across}, {"tp": far}])
+    peers = {1: side, 2: across, 3: far}
+    rows = x_ref.shape[1]
+
+    def slot(owner):
+        return out_ref.at[pl.ds(pl.multiple_of(owner * rows, rows), rows)]
+
+    sent = [push(x_ref.at[k], slot(me), sems.at[k], rems.at[k], {"tp": peers[k]}) for k in (3, 2)]
+    grads = ((g0, k0, a0), (g1, k1, a1), (g2, k2, a2))
+    folded = []
+    for n, (grad, _, _) in enumerate(grads):
+        folded.append(push(grad.at[3], boxes[2 * n + 1], ws.at[1, n], wr.at[1, n], {"tp": side}))
+        folded.append(push(grad.at[1], boxes[2 * n], ws.at[0, n], wr.at[0, n], {"tp": side}))
+    sent.append(push(x_ref.at[1], slot(me), sems.at[1], rems.at[1], {"tp": side}))
+    keep = pltpu.make_async_copy(x_ref.at[0], slot(me), own)
+    keep.start()
+    for n, (grad, kept, over) in enumerate(grads):
+        folded[2 * n].wait()
+        over[...] = (grad[2].astype(f32) + boxes[2 * n + 1][...].astype(f32)).astype(bf16)
+        folded[2 * n + 1].wait()
+        kept[...] = (grad[0].astype(f32) + boxes[2 * n][...].astype(f32)).astype(bf16)
+    keep.wait()
+    for k, peer in ((3, far), (2, across), (1, side)):
+        awaited(slot(peer), sems.at[k], rems.at[k], {"tp": peer}).wait_recv()
     for copy in sent:
         copy.wait_send()
 
 
-def fold_rows(x, number, parts=4):
-    rows, width = x.shape[0] // 4, x.shape[1]
+def exchange_grad(x, grads, number):
+    _, rows, width = x.shape
     dma = pltpu.SemaphoreType.DMA
+    pieces = [jax.ShapeDtypeStruct(g.shape[1:], g.dtype) for g in grads]
+    boxes = []
+    for g in grads:
+        boxes += [pltpu.VMEM(g.shape[1:], g.dtype)] * 2
     return comm_call(
-        functools.partial(fold_kernel, parts=parts),
-        "fold_rows",
+        exchange_grad_kernel,
+        "exchange_grad",
         number,
-        jax.ShapeDtypeStruct((rows, width), f32),
-        [in_vmem()],
-        in_vmem(),
-        [pltpu.VMEM((rows, width), x.dtype)]
-        + [dma((parts,))] * 6
-        + [pltpu.VMEM((rows, width), x.dtype)] * 3,
+        [jax.ShapeDtypeStruct((4 * rows, width), x.dtype)] + pieces + pieces,
+        [in_vmem()] * 4,
+        [in_vmem()] * 7,
+        [dma((4,)), dma((4,)), dma((2, 3)), dma((2, 3)), dma] + boxes,
         60 << 20,
         x,
+        *grads,
+    )
+
+
+def leave_kernel(
+    grad_ref, normed_ref, w_ref, k0, k1, k2, a0, a1, a2, early_ref,
+    rows_ref, s0, s1, s2, s3, cols_ref, early_out,
+    far_out, own_out, sum_buf, side_far, side_own, over, dw_acc, early_box,
+    sa, ra, sb, rb, sy, ry, sw, rw, se, re, *bufs, parts, hops, all_hops
+):
+    me, side, across, far = quad()
+    rows = rows_ref.shape[0]
+    step = rows // parts
+    greet([{"tp": side}, {"tp": across}] + [{axis: flip(axis, bit)} for axis, bit in hops])
+    count = len(hops)
+    outs = (s0, s1, s2, s3)
+    mlp = ((k0, a0), (k1, a1), (k2, a2))
+    current = bufs[0:4]
+    boxes = [bufs[4 + g * count : 4 + (g + 1) * count] for g in range(4)]
+    keeps = [bufs[4 + 4 * count + g * (count - 1) : 4 + 4 * count + (g + 1) * (count - 1)] for g in range(4)]
+    sent = []
+
+    def begin(g):
+        kept, arrived = mlp[g]
+        current[g][...] = (kept[...].astype(f32) + arrived[...].astype(f32)).astype(bf16)
+
+    def hop_parts(g, k):
+        axis, bit = hops[k]
+        source = current[g] if k == 0 else keeps[g][k - 1]
+        half = lax.rem(lax.axis_index(axis) // bit, 2)
+        return {axis: flip(axis, bit)}, source, half, boxes[g][k]
+
+    def hop_send(g, k):
+        peer, source, half, box = hop_parts(g, k)
+        sent.append(push(source.at[:, 1 - half], box, sw.at[g, k], rw.at[g, k], peer))
+
+    def hop_add(g, k):
+        peer, source, half, box = hop_parts(g, k)
+        awaited(box, sw.at[g, k], rw.at[g, k], peer).wait_recv()
+        if k == count - 1:
+            outs[g][...] = source[0, half].astype(f32) + box[0].astype(f32)
+        else:
+            target = keeps[g][k]
+            for n in range(box.shape[0]):
+                total = source[n, half].astype(f32) + box[n].astype(f32)
+                target[n // 2, n % 2] = total.astype(bf16)
+            hop_send(g, k + 1)
+
+    def early_send(k):
+        axis, bit = all_hops[k]
+        sent.append(push(early_out.at[k], early_box.at[k], se.at[k], re.at[k], {axis: flip(axis, bit)}))
+
+    def early_add(k):
+        axis, bit = all_hops[k]
+        awaited(early_box.at[k], se.at[k], re.at[k], {axis: flip(axis, bit)}).wait_recv()
+        early_out[k + 1] = early_out[k] + early_box[k]
+        if k + 1 < len(all_hops):
+            early_send(k + 1)
+
+    def span(owner, part):
+        return pl.ds(pl.multiple_of(owner * rows + part * step, step), step)
+
+    def piece(part):
+        return pl.ds(pl.multiple_of(part * step, step), step)
+
+    def partial(owner, part):
+        return dot_t(grad_ref[span(owner, part), :], w_ref[...])
+
+    def give_far(part, carry):
+        here = piece(part)
+        far_out[here, :] = partial(far, part).astype(bf16)
+        push(far_out.at[here], side_far.at[here], sa.at[part], ra.at[part], {"tp": side})
+        return carry
+
+    def give_over(part, carry):
+        here = piece(part)
+        mine = partial(across, part)
+        awaited(side_far.at[here], sa.at[part], ra.at[part], {"tp": side}).wait_recv()
+        sum_buf[here, :] = (mine + side_far[here, :].astype(f32)).astype(bf16)
+        push(sum_buf.at[here], over.at[here], sy.at[part], ry.at[part], {"tp": across})
+        return carry
+
+    def give_own(part, carry):
+        here = piece(part)
+        own_out[here, :] = partial(side, part).astype(bf16)
+        push(own_out.at[here], side_own.at[here], sb.at[part], rb.at[part], {"tp": side})
+        return carry
+
+    def take_own(part, carry):
+        here = piece(part)
+        mine = partial(me, part)
+        awaited(side_own.at[here], sb.at[part], rb.at[part], {"tp": side}).wait_recv()
+        rows_ref[here, :] = mine + side_own[here, :].astype(f32)
+        return carry
+
+    def take_over(part, carry):
+        here = piece(part)
+        awaited(over.at[here], sy.at[part], ry.at[part], {"tp": across}).wait_recv()
+        rows_ref[here, :] += over[here, :].astype(f32)
+        return carry
+
+    def drain(part, carry):
+        here = piece(part)
+        awaited(far_out.at[here], sa.at[part], ra.at[part], {"tp": side}).wait_send()
+        awaited(own_out.at[here], sb.at[part], rb.at[part], {"tp": side}).wait_send()
+        awaited(sum_buf.at[here], sy.at[part], ry.at[part], {"tp": across}).wait_send()
+        return carry
+
+    lax.fori_loop(0, parts, give_far, 0)
+    begin(0)
+    hop_send(0, 0)
+    early_out[0] = early_ref[...]
+    early_send(0)
+    lax.fori_loop(0, parts, give_over, 0)
+    for g in (1, 2):
+        begin(g)
+        hop_send(g, 0)
+    chunk = 512
+    dw_acc[...] = jnp.zeros_like(dw_acc)
+    cols_ref[...] = jnp.zeros_like(cols_ref)
+    ones = jnp.ones((8, chunk), bf16)
+
+    def weight_grad(n, carry):
+        at = pl.ds(pl.multiple_of(n * chunk, chunk), chunk)
+        g = grad_ref[at, :]
+        dw_acc[...] += lax.dot_general(
+            normed_ref[at, :], g, (((0,), (0,)), ((), ())), preferred_element_type=f32
+        )
+        cols_ref[...] += dot_n(ones, g)
+        return carry
+
+    lax.fori_loop(0, grad_ref.shape[0] // chunk, weight_grad, 0)
+    current[3][...] = dw_acc[...].astype(bf16).reshape(current[3].shape)
+    hop_send(3, 0)
+    lax.fori_loop(0, parts, give_own, 0)
+    early_add(0)
+    order = sorted(((k + g, g, k) for g in range(4) for k in range(count)), key=lambda w: (w[0], w[1]))
+    later = list(range(1, len(all_hops)))
+    for n, (_, g, k) in enumerate(order):
+        hop_add(g, k)
+        if n % 2 == 1 and later:
+            early_add(later.pop(0))
+        if n == len(order) // 2:
+            lax.fori_loop(0, parts, take_own, 0)
+    for k in later:
+        early_add(k)
+    lax.fori_loop(0, parts, take_over, 0)
+    lax.fori_loop(0, parts, drain, 0)
+    for copy in sent:
+        copy.wait_send()
+
+
+def leave(grad, normed, w, kept, came, early, number, parts=4):
+    rows, width = grad.shape[0] // 4, w.shape[0]
+    dma = pltpu.SemaphoreType.DMA
+    hops = bits_of("fsdp")
+    all_hops = bits_of("tp") + hops
+    count = len(hops)
+    shards = lax.axis_size("fsdp")
+    shard = width // shards
+    widths = [k.shape[1] for k in kept] + [grad.shape[1]]
+    split = (shards // 2, 2, shard)
+    current = [pltpu.VMEM((*split, n), bf16) for n in widths]
+    boxes = [pltpu.VMEM((shards >> (k + 1), shard, n), bf16) for n in widths for k in range(count)]
+    keeps = [pltpu.VMEM((shards >> (k + 2), 2, shard, n), bf16) for n in widths for k in range(count - 1)]
+    pieces = [x.reshape(*split, x.shape[1]) for x in (*kept, *came)]
+    return comm_call(
+        functools.partial(leave_kernel, parts=parts, hops=hops, all_hops=all_hops),
+        "leave",
+        number,
+        [jax.ShapeDtypeStruct((rows, width), f32)]
+        + [jax.ShapeDtypeStruct((shard, n), f32) for n in widths]
+        + [
+            jax.ShapeDtypeStruct((8, grad.shape[1]), f32),
+            jax.ShapeDtypeStruct((len(all_hops) + 1, *early.shape), f32),
+        ],
+        [in_vmem()] * 10,
+        [in_vmem()] * 7,
+        [pltpu.VMEM((rows, width), bf16)] * 6
+        + [pltpu.VMEM((width, grad.shape[1]), f32), pltpu.VMEM((len(all_hops), *early.shape), f32)]
+        + [dma((parts,))] * 6
+        + [dma((4, count))] * 2
+        + [dma((len(all_hops),))] * 2
+        + current
+        + boxes
+        + keeps,
+        60 << 20,
+        grad,
+        normed,
+        w,
+        *pieces,
+        early,
     )
 
 
@@ -656,73 +852,16 @@
     )
 
 
-def fold_shards_kernel(x_ref, out_ref, sems, rems, *bufs, hops):
-    greet([{axis: flip(axis, bit)} for axis, bit in hops])
-    blocks = x_ref.shape[0]
-    count = len(hops)
-    current = x_ref
-    for k, (axis, bit) in enumerate(hops):
-        peer = flip(axis, bit)
-        mine = lax.rem(lax.axis_index(axis) // bit, 2)
-        half = current.shape[0] // 2
-        stage, inbox = bufs[2 * k], bufs[2 * k + 1]
-        for n in range(half):
-            stage[n] = current[2 * n + 1 - mine]
-        copy = push(stage, inbox, sems.at[k], rems.at[k], {axis: peer})
-        copy.wait()
-        if k == count - 1:
-            out_ref[...] = current[mine].astype(f32) + inbox[0].astype(f32)
-        else:
-            keep = bufs[2 * count + k]
-            for n in range(half):
-                keep[n] = (current[2 * n + mine].astype(f32) + inbox[n].astype(f32)).astype(keep.dtype)
-            current = keep
-
-
-def fold_shards(x, number):
-    hops = bits_of("fsdp")
-    count = len(hops)
-    blocks, rows, width = x.shape
-    dma = pltpu.SemaphoreType.DMA
-    halves = [blocks >> (k + 1) for k in range(count)]
-    bufs = []
-    for half in halves:
-        bufs += [pltpu.VMEM((half, rows, width), x.dtype)] * 2
-    bufs += [pltpu.VMEM((half, rows, width), x.dtype) for half in halves[:-1]]
-    return comm_call(
-        functools.partial(fold_shards_kernel, hops=hops),
-        "fold_shards",
-        number,
-        jax.ShapeDtypeStruct((rows, width), f32),
-        [in_vmem()],
-        in_vmem(),
-        [dma((count,)), dma((count,))] + bufs,
-        60 << 20,
-        x,
-    )
-
-
-def spread(value, axis):
-    bits = bits_of(axis)[::-1]
-    size = lax.axis_size(axis)
-    me = lax.axis_index(axis)
-    for k, (_, bit) in enumerate(bits):
-        other = lax.ppermute(value, axis, [(n, n ^ bit) for n in range(size)])
-        high = lax.rem(me // bit, 2) == 1
-        value = jnp.stack([jnp.where(high, other, value), jnp.where(high, value, other)], axis=k)
-    return value.reshape(size, *value.shape[len(bits) :])
-
-
-def fold_bits(value, axis):
-    size = lax.axis_size(axis)
-    for _, bit in bits_of(axis):
-        own = lax.rem(lax.axis_index(axis) // bit, 2)
-        pairs = value.reshape(value.shape[0] // 2, 2, *value.shape[1:])
-        sent = lax.dynamic_index_in_dim(pairs, 1 - own, 1, keepdims=False)
-        kept = lax.dynamic_index_in_dim(pairs, own, 1, keepdims=False)
-        arrived = lax.ppermute(sent, axis, [(n, n ^ bit) for n in range(size)])
-        value = (kept.astype(f32) + arrived.astype(f32)).astype(bf16)
-    return value[0]
+def relative(value):
+    me = lax.axis_index("tp")
+    pairs = value.reshape(2, 2, *value.shape[1:])
+    pairs = jnp.where(lax.rem(me, 2) == 1, pairs[:, ::-1], pairs)
+    pairs = jnp.where(me // 2 == 1, pairs[::-1], pairs)
+    return pairs.reshape(value.shape)
+
+
+def across(value):
+    return lax.ppermute(value, "tp", [(n, n ^ 2) for n in range(4)])
 
 
 def local(
@@ -763,11 +902,8 @@
         0,
     )
     qkv_full = qkv_full.reshape(model_width, 3 * head_cols)
-    packed = jnp.concatenate([fc_slice, proj_slice, out_slice], axis=2)
-    packed = spread(packed.reshape(model_width, packed.shape[2]), "tp")
-    fc_full = packed[:, :, 0:hidden_cols]
-    proj_full = packed[:, :, hidden_cols : 2 * hidden_cols]
-    out_full = packed[:, :, 2 * hidden_cols :]
+    own = [w.reshape(model_width, w.shape[2]) for w in (fc_slice, proj_slice, out_slice)]
+    over = [across(w) for w in own]
 
     resid_in = inputs.astype(f32)
     _, hat_one, inv_one = layer_norm(
@@ -780,7 +916,7 @@
     low = start[::size] // size
     start_rows = jnp.broadcast_to(start[None], (8, seq_rows))
     attn_out, qb = attend(low, qa, ka, vt, start_rows, size)
-    attn_here = exchange(attn_out, 1, "exchange_out")
+    attn_here, fc_full, proj_full, out_full = exchange_out(attn_out, own, over, 1)
 
     hidden = (
         resid_in
@@ -791,9 +927,9 @@
         hidden, second_gain.astype(f32), second_shift.astype(f32)
     )
     mlp_in = normed_two.astype(bf16)
-    pre_act = jnp.einsum("sd,tdf->tsf", mlp_in, fc_full, preferred_element_type=f32) + fc_bias.astype(
-        f32
-    ).reshape(slices, 1, hidden_cols)
+    pre_act = jnp.einsum("sd,tdf->tsf", mlp_in, fc_full, preferred_element_type=f32) + relative(
+        fc_bias.astype(f32).reshape(slices, 1, hidden_cols)
+    )
     sigmoid_pre = jax.nn.sigmoid(gelu_slope * pre_act)
     act_low = (pre_act * sigmoid_pre).astype(bf16)
     layer_out = (
@@ -806,7 +942,7 @@
     grad_pre = grad_act * (sigmoid_pre + gelu_slope * pre_act * sigmoid_pre * (1.0 - sigmoid_pre))
     grad_pre_low = grad_pre.astype(bf16)
     fc_grad = jnp.einsum("sd,tsf->tdf", mlp_in, grad_pre_low, preferred_element_type=f32)
-    fc_bias_part = jnp.sum(grad_pre_low.astype(f32), axis=1).reshape(-1)
+    fc_bias_part = relative(jnp.sum(grad_pre_low.astype(f32), axis=1)).reshape(-1)
     grad_normed_two = jnp.einsum("tsf,tdf->sd", grad_pre_low, fc_full, preferred_element_type=f32)
     resid_grad = out_grad.astype(f32)
     grad_hidden_ln, second_gain_part, second_shift_part = norm_back(
@@ -823,62 +959,41 @@
     grad_attn = jnp.einsum("sd,pdc->psc", grad_hidden_low, out_full, preferred_element_type=f32).astype(
         bf16
     ) * live_here[None, :, None]
-    grad_attn_seq = exchange(
-        grad_attn.reshape(slices * rows_here, head_cols), 2, "exchange_grad"
-    ).reshape(seq_rows, head_cols)
-    folded = fold_bits(
-        jnp.concatenate(
-            [fc_grad.astype(bf16), proj_grad.astype(bf16), out_grad_part.astype(bf16)], axis=2
-        ),
-        "tp",
-    )
+    grad_attn_seq, *halves = exchange_grad(
+        grad_attn, (fc_grad.astype(bf16), proj_grad.astype(bf16), out_grad_part.astype(bf16)), 2
+    )
+    kept, came = halves[0:3], [across(half) for half in halves[3:6]]
     grad_qkv = attend_back(low, qb, ka, va, kt, grad_attn_seq, attn_out, start_rows, size)
-    qkv_w_grad = jnp.einsum("sd,sj->dj", seq_normed, grad_qkv, preferred_element_type=f32)
-    col_sums = jnp.sum(grad_qkv.astype(f32), axis=0)
-    partial = jnp.einsum("sj,dj->sd", grad_qkv, qkv_full, preferred_element_type=f32).astype(bf16)
-    grad_normed_one = fold_rows(partial, 3)
+    early = [out_bias_part, second_gain_part, second_shift_part, fc_bias_part, proj_bias_part]
+    grad_normed_one, fc_w_grad, proj_w_grad, out_w_grad, qkv_grad, col_sums, early_sums = leave(
+        grad_qkv, seq_normed, qkv_full, kept, came, jnp.concatenate(early).reshape(-1, 128), 3
+    )
     grad_in_ln, first_gain_part, first_shift_part = norm_back(
         grad_normed_one, hat_one, inv_one, first_gain.astype(f32)
     )
     input_grad = (grad_hidden + grad_in_ln).astype(bf16)
-    shards = model_width // shard_rows
-    every = jnp.concatenate([folded, qkv_w_grad.astype(bf16)], axis=1).reshape(
-        shards, shard_rows, -1
-    )
-    summed = fold_shards(every, 4)
-    fc_w_grad = summed[:, 0:hidden_cols]
-    proj_w_grad = summed[:, hidden_cols : 2 * hidden_cols].T
-    out_w_grad = summed[:, 2 * hidden_cols : 2 * hidden_cols + head_cols].T
-    qkv_grad = summed[:, 2 * hidden_cols + head_cols :].reshape(shard_rows, 3, head_cols)
+    proj_w_grad = proj_w_grad.T
+    out_w_grad = out_w_grad.T
+    qkv_grad = qkv_grad.reshape(shard_rows, 3, head_cols)
+    col_sums = col_sums[0]
     qv_part = jnp.stack([col_sums[0:head_cols], col_sums[2 * head_cols :]])
     qv_full = lax.dynamic_update_slice_in_dim(
         jnp.zeros((2, model_width), f32), qv_part, tp_index * head_cols, 1
     )
-    vectors = [
-        first_gain_part,
-        first_shift_part,
-        qv_full.reshape(-1),
-        out_bias_part,
-        second_gain_part,
-        second_shift_part,
-        fc_bias_part,
-        proj_bias_part,
-    ]
-    totals = all_sum(jnp.concatenate(vectors).reshape(-1, 128), 5).reshape(-1)
-    pieces, at = [], 0
-    for vector in vectors:
-        pieces.append(totals[at : at + vector.shape[0]])
-        at += vector.shape[0]
-    (
-        first_gain_grad,
-        first_shift_grad,
-        qv_bias_grad,
-        out_bias_grad,
-        second_gain_grad,
-        second_shift_grad,
-        fc_bias_grad,
-        proj_bias_grad,
-    ) = pieces
+    late = [first_gain_part, first_shift_part, qv_full.reshape(-1)]
+    late_sums = all_sum(jnp.concatenate(late).reshape(-1, 128), 4)
+
+    def pieces(totals, vectors):
+        totals, found, at = totals.reshape(-1), [], 0
+        for vector in vectors:
+            found.append(totals[at : at + vector.shape[0]])
+            at += vector.shape[0]
+        return found
+
+    first_gain_grad, first_shift_grad, qv_bias_grad = pieces(late_sums, late)
+    out_bias_grad, second_gain_grad, second_shift_grad, fc_bias_grad, proj_bias_grad = pieces(
+        early_sums[-1], early
+    )
     return (
         layer_out,
         input_grad,

time: 382 us -> 313 us (0.82)
  waiting for transfers between devices: 39.4 us -> 0.02 us
  local copies, waits for them, and re-layouts: 29.6 us -> 16.2 us
  other arithmetic: 28.8 us -> 15.8 us
  starting transfers between devices: 1 us -> 6.21 us
    ppermute x4 -> x6, waiting for transfers between devices: 39.4 us -> 0.02 us  [across(): return lax.ppermute(value, 'tp', [(n, n ^ 2) for n in range(4)])]
    dot_general x2 -> x0, matrix products: 10.1 us -> none  [the longest x1 5.66 us: local(): jnp.einsum('sd,sj->dj', seq_normed, grad_qkv, preferred_element_type=f32)]
    dynamic_slice x2 -> x0, local copies, waits for them, and re-layouts: 6.82 us -> none  [the longest x1 4.32 us: fold_bits(): sent = lax.dynamic_index_in_dim(pairs, 1 - own, 1, keepdims=False)]
    another operation x4 -> x0, other arithmetic: 6.1 us -> none  [spread(): jnp.stack([jnp.where(high, other, value), jnp.where(high, value, other)],...]
    ppermute x4 -> x6, starting transfers between devices: 1 us -> 6.21 us  [across(): return lax.ppermute(value, 'tp', [(n, n ^ 2) for n in range(4)])]
    unnamed x67 -> x66, local copies, waits for them, and re-layouts: 9.3 us -> 6.38 us
    pallas_call x6 -> x5, Pallas kernels: 181 us -> 178 us  [comm_call(): pl.pallas_call(kernel, out_shape=out_shape, in_specs=in_specs, out_specs=...]
  transfers between devices with their start and end apart: 4 -> 6, of which waited for: 2 -> 0; matrix products, arithmetic and copies ran while one was open for 11% -> 4% of each run, Pallas kernels for 39% -> 17%
where the time goes in v4:
time: 313 us; the launch traced here: 310 us
  Pallas kernels  232 us (74%)
  matrix products  37.9 us (12%)
  local copies, waits for them, and re-layouts  16.2 us (5%)
  other arithmetic  15.8 us (5%)
  starting transfers between devices  6.21 us (2%)
    pallas_call x5, Pallas kernels, comm_call(): pl.pallas_call(kernel, out_shape=out_shape, in_specs=in_specs, out_specs=...  178 us
    pallas_call x1, Pallas kernels, attend_back(): pl.pallas_call(functools.partial(attend_back_kernel, size=size, blocks=ro...  30.5 us
    pallas_call x1, Pallas kernels, attend(): pl.pallas_call(functools.partial(attend_kernel, size=size, blocks=rows //...  23.5 us
    dot_general x1, matrix products, local(): jnp.einsum('tsf,tdf->sd', act_low, proj_full, preferred_element_type=f32)  6.8 us
    dot_general x1, matrix products, local(): jnp.einsum('sd,tdf->tsf', mlp_in, fc_full, preferred_element_type=f32)  6.76 us
    dot_general x1, matrix products, local(): jnp.einsum('sd,tdf->tsf', out_grad, proj_full, preferred_element_type=f32)  6.65 us
    unnamed x66, local copies, waits for them, and re-layouts  6.38 us
  transfers between devices with their start and end apart: 6, of which 0 were waited for; matrix products, arithmetic and copies ran while one was open for 4% of the time, Pallas kernels for 17%

profile of v4, /device:TPU:0, one launch (start us, length us, event | category | flops | bytes accessed | tf_op | source)
XLA Modules:
  0.0 309.8 jit_solution(13490147314235787069)
XLA Ops:
  4.8 53.4 %enter.1 = (bf16[4096,512]{1,0:T(8,128)(2,1)}, s32[4,1,1024]{2,1,0:T(1,128)}, bf16[2,4096,128]{2,1,0:T(8,128)(2,1)}, bf16[2,4096,128]{2,1,0:T(8,128)(2,1)}, bf16...) custom-call(bf16[1024,512]{1,0:T(8,128)(2,1)} %x_ref.1, ...), custom_call_target="tpu_custom_call" | custom-call | bytes 62914560 | tf_op jit(solution)/shard_map/enter/pallas_call | solution.py:278
  58.9 1.4 collective-permute-start.1
  65.9 23.5 %attend.1 = (bf16[4096,128]{1,0:T(8,128)(2,1)}, bf16[2,4096,128]{2,1,0:T(8,128)(2,1)}) custom-call(s32[8]{0:T(128)} %and_select_fusion.low_ref, bf16[2,4096,128]{2,1,0:T(8,128)(2,1)} %get-tuple-element.46.qa_ref, bf16[2,4096,128]{2,1,0:T(8,128)(2,1)} %get-tuple-element.47.ka_ref, bf16[2,80,4096]{2,1,0:T(8,128)(2,1)} %get-tuple-element.48.vt_ref, ...), custom_call_target="tpu_custom_call" | custom-call | flops 30064771072 | bytes 8388608 | tf_op jit(solution)/shard_map/attend/pallas_call | solution.py:124
  91.2 18.9 %exchange_out.1 = (bf16[4,1024,128]{2,1,0:T(8,128)(2,1)}, bf16[4,512,512]{2,1,0:T(8,128)(2,1)}, bf16[4,512,512]{2,1,0:T(8,128)(2,1)}, bf16[4,512,128]{2,1,0:T(8,128)(2,1)}) custom-call(bf16[4096,128]{1,0:T(8,128)(2,1)} %get-tuple-element.49.x_ref.o_ref, bf16[512,512]{1,0:T(8,128)(2,1)} %bitcast.133, bf16[512,512]{1,0:T(8,128)(2,1)} %bitcast.135, ...), custom_call_target="tpu_custom_call" | custom-call | bytes 62914560 | tf_op jit(solution)/shard_map/exchange_out/pallas_call | solution.py:278
  110.1 2.2 fusion.36
  112.7 1.9 copy-done.25
  114.6 6.8 %fusion.1 = (bf16[4,1024,512]{1,2,0:T(8,128)(2,1)}, f32[4,512,1024]{2,1,0:T(8,128)S(1)}) fusion(f32[4,512]{1,0:T(4,128)S(1)} %add.84, bf16[4,512,512]{2,1,0:T(8,128)(2,1)S(1)} %copy-done.25, f32[1024,512]{1,0:T(8,128)S(1)} %get-tuple-element.140, f32[512]{0:T(512)S(1)} %convert_element_type.91, f32[512]{0:T(512)S(1)} %convert_element_type.90, ...), kind=kOutput, calls=%fused_computation.4 | convolution fusion | flops 2164785152 | bytes 16797696 | tf_op jit(solution)/shard_map/sd,tdf->tsf/dot_general | solution.py:930
  121.4 6.6 %convert_reduce_fusion = (f32[4,512]{1,0:T(4,128)S(1)}, bf16[4,1024,512]{1,2,0:T(8,128)(2,1)S(1)}) fusion(f32[4,512,1024]{2,1,0:T(8,128)S(1)} %get-tuple-element.143, f32[4,512]{1,0:T(4,128)S(1)} %add.84, bf16[4,512,512]{2,1,0:T(8,128)(2,1)S(1)} %copy-done.24, bf16[1024,512]{1,0:T(8,128)(2,1)S(1)} %copy-done.5), kind=kOutput, calls=%fused_computation.5 | convolution fusion | flops 2174744576 | bytes 15745024 | tf_op jit(solution)/shard_map/sd,tdf->tsf/dot_general | solution.py:941
  128.0 4.4 %fusion.15 = (f32[512]{0:T(512)S(1)}, f32[1024]{0:T(1024)S(1)}, f32[1024]{0:T(1024)S(1)}, f32[512]{0:T(512)S(1)}, f32[1024,512,1]{1,0,2:T(8,128)}) fusion(f32[1024,512]{1,0:T(8,128)S(1)} %get-tuple-element.140, f32[1024]{0:T(1024)S(1)} %add_rsqrt_fusion.1, f32[1024]{0:T(1024)S(1)} %broadcast_multiply_fusion.5, f32[512]{0:T(512)S(1)} %convert_element_type.90, ...), kind=kOutput, calls=%fused_computation.28 | convolution fusion | flops 2152199168 | bytes 10508288 | tf_op jit(solution)/shard_map/tsf,tdf->sd/dot_general | solution.py:946
  132.5 4.0 %convert_bitcast_fusion.1.g0 = bf16[4,512,512]{2,1,0:T(8,128)(2,1)} fusion(bf16[4,1024,512]{1,2,0:T(8,128)(2,1)S(1)} %get-tuple-element.145, f32[1024,512]{1,0:T(8,128)S(1)} %get-tuple-element.140, f32[512]{0:T(512)S(1)} %convert_element_type.91, f32[512]{0:T(512)S(1)} %convert_element_type.90, f32[1024]{0:T(1024)S(1)} %add_rsqrt_fusion.1, ...), kind=kOutput, calls=%fused_computation.34 | convolution fusion | flops 2151153664 | bytes 8400896 | tf_op jit(solution)/shard_map/sd,tsf->tdf/dot_general | solution.py:944
  136.7 3.1 convert_reduce_fusion.3
  139.8 1.6 fusion.21.g2
  141.4 1.7 fusion.20.x_ref
  143.1 3.8 %convert_bitcast_fusion.g1 = bf16[4,512,512]{2,1,0:T(8,128)(2,1)} fusion(bf16[4,1024,512]{1,2,0:T(8,128)(2,1)S(1)} %copy-done.27, bf16[1024,512]{1,0:T(8,128)(2,1)S(1)} %copy-done.6), kind=kOutput, calls=%fused_computation.33 | convolution fusion | flops 2148532224 | bytes 7340032 | tf_op jit(solution)/shard_map/sd,tsf->tdf/dot_general | solution.py:940
  146.9 18.8 %exchange_grad.1 = (bf16[4096,128]{1,0:T(8,128)(2,1)}, bf16[512,512]{1,0:T(8,128)(2,1)}, bf16[512,512]{1,0:T(8,128)(2,1)}, bf16[512,128]{1,0:T(8,128)(2,1)}, bf1...) custom-call(bf16[4,1024,128]{2,1,0:T(8,128)(2,1)} %fusion.20.x_ref, ...), custom_call_target="tpu_custom_call" | custom-call | bytes 62914560 | tf_op jit(solution)/shard_map/exchange_grad/pallas_call | solution.py:278
  165.7 1.5 collective-permute-start.3
  167.8 1.4 collective-permute-start.5
  169.2 6.8 %fusion.17 = bf16[1024,512]{1,0:T(8,128)(2,1)} fusion(f32[1024,512]{1,0:T(8,128)} %copy-done.3, bf16[4,1024,512]{1,2,0:T(8,128)(2,1)} %get-tuple-element.142, bf16[4,512,512]{2,1,0:T(8,128)(2,1)} %get-tuple-element.56, f32[512]{0:T(512)S(1)} %convert_element_type.94), kind=kOutput, calls=%fused_computation.31 | convolution fusion | flops 2149056512 | bytes 9439232 | tf_op jit(solution)/shard_map/tsf,tdf->sd/dot_general | solution.py:937
  176.0 30.5 %attend_back.1.grad_ref = bf16[4096,384]{1,0:T(8,128)(2,1)} custom-call(s32[8]{0:T(128)} %and_select_fusion.low_ref, bf16[2,4096,128]{2,1,0:T(8,128)(2,1)} %get-tuple-element.57.qb_ref, bf16[2,4096,128]{2,1,0:T(8,128)(2,1)} %get-tuple-element.47.ka_ref, bf16[2,4096,128]{2,1,0:T(8,128)(2,1)} %get-tuple-element.58.va_ref, ...), custom_call_target="tpu_custom_call" | custom-call | flops 51539607552 | bytes 16777216 | tf_op jit(solution)/shard_map/attend_back/pallas_call | solution.py:215
  207.4 72.0 %leave.1 = (f32[1024,512]{1,0:T(8,128)}, f32[64,512]{1,0:T(8,128)}, f32[64,512]{1,0:T(8,128)}, f32[64,128]{1,0:T(8,128)}, f32[64,384]{1,0:T(8,128)}, /*index=5*/f32[8,384]{1,0:T(8,128)}, f32[6,32,128]{2,1,0:T(8,128)}) custom-call(bf16[4096,384]{1,0:T(8,128)(2,1)} %attend_back.1.grad_ref, bf16[4096,512]{1,0:T(8,128)(2,1)} %get-tuple-element.61.normed_ref, ...), custom_call_target="tpu_custom_call" | custom-call | bytes 62914560 | tf_op jit(solution)/shard_map/leave/pallas_call | solution.py:278
  280.2 2.7 fusion.12
  283.5 14.9 %all_sum.1 = f32[16,128]{1,0:T(8,128)} custom-call(f32[16,128]{1,0:T(8,128)} %maximum_bitcast_fusion.x_ref), custom_call_target="tpu_custom_call" | custom-call | bytes 10485760 | tf_op jit(solution)/shard_map/all_sum/pallas_call | solution.py:278
  300.5 1.4 slice_bitcast_fusion.1
  304.4 3.0 fusion.11
  (127 shorter events, 21.9 us)
Async XLA Ops:
  0.7 60.3 %copy-start.2 = (bf16[1024,512]{1,0:T(8,128)(2,1)S(1)}, bf16[1024,512]{1,0:T(8,128)(2,1)}, u32[]{:S(2)}) copy-start(bf16[1024,512]{1,0:T(8,128)(2,1)} %x_ref.1) | copy-start | bytes 3145732
  0.7 64.3 %copy-start.18 = (bf16[2048]{0:T(1024)(128)(2,1)S(1)}, bf16[2048]{0:T(1024)(128)(2,1)}, u32[]{:S(2)}) copy-start(bf16[2048]{0:T(1024)(128)(2,1)} %param.27) | copy-start | bytes 12292
  58.2 31.9 %collective-permute-start = (bf16[512,512]{1,0:T(8,128)(2,1)}, bf16[512,512]{1,0:T(8,128)(2,1)S(1)}, u32[]{:S(2)}, u32[]{:S(2)}) collective-permute-start(bf16[512,512]{1,0:T(8,128)(2,1)} %bitcast.132), channel_id=1, source_target_pairs={{0,2},{1,3},{2,0},{3,1},{4,6},{5,7},{6,4},{7,5},{8,10},{9,11},{10,... | collective-permute-start | bytes 1572872 | tf_op jit(solution)/shard_map/ppermute | solution.py:864
  58.9 31.3 %collective-permute-start.1 = (bf16[512,512]{1,0:T(8,128)(2,1)}, bf16[512,512]{1,0:T(8,128)(2,1)S(1)}, u32[]{:S(2)}, u32[]{:S(2)}) collective-permute-start(bf16[512,512]{1,0:T(8,128)(2,1)} %bitcast.134), channel_id=1, source_target_pairs={{0,2},{1,3},{2,0},{3,1},{4,6},{5,7},{6,4},{7,5},{8,10},{9,11},{10,... | collective-permute-start | bytes 1572872 | tf_op jit(solution)/shard_map/ppermute | solution.py:864
  60.3 29.8 %collective-permute-start.2 = (bf16[512,128]{1,0:T(8,128)(2,1)}, bf16[512,128]{1,0:T(8,128)(2,1)S(1)}, u32[]{:S(2)}, u32[]{:S(2)}) collective-permute-start(bf16[512,128]{1,0:T(8,128)(2,1)} %bitcast.144), channel_id=1, source_target_pairs={{0,2},{1,3},{2,0},{3,1},{4,6},{5,7},{6,4},{7,5},{8,10},{9,11},{10,... | collective-permute-start | bytes 393224 | tf_op jit(solution)/shard_map/ppermute | solution.py:864
  65.9 24.1 %copy-start.19 = (bf16[512]{0:T(512)(128)(2,1)S(1)}, bf16[512]{0:T(512)(128)(2,1)}, u32[]{:S(2)}) copy-start(bf16[512]{0:T(512)(128)(2,1)} %param.18) | copy-start | bytes 3076
  65.9 24.1 %copy-start.20 = (bf16[512]{0:T(512)(128)(2,1)S(1)}, bf16[512]{0:T(512)(128)(2,1)}, u32[]{:S(2)}) copy-start(bf16[512]{0:T(512)(128)(2,1)} %param.23) | copy-start | bytes 3076
  65.9 24.2 %copy-start.21 = (bf16[512]{0:T(512)(128)(2,1)S(1)}, bf16[512]{0:T(512)(128)(2,1)}, u32[]{:S(2)}) copy-start(bf16[512]{0:T(512)(128)(2,1)} %param.24) | copy-start | bytes 3076
  65.9 24.2 %copy-start.22 = (bf16[512]{0:T(512)(128)(2,1)S(1)}, bf16[512]{0:T(512)(128)(2,1)}, u32[]{:S(2)}) copy-start(bf16[512]{0:T(512)(128)(2,1)} %param.25) | copy-start | bytes 3076
  65.9 24.2 %copy-start.23 = (bf16[512]{0:T(512)(128)(2,1)S(1)}, bf16[512]{0:T(512)(128)(2,1)}, u32[]{:S(2)}) copy-start(bf16[512]{0:T(512)(128)(2,1)} %param.29) | copy-start | bytes 3076
  65.9 24.2 %copy-start.17 = (s32[1,1024]{1,0:T(1,128)S(1)}, s32[1,1024]{1,0:T(1,128)}, u32[]{:S(2)}) copy-start(s32[1,1024]{1,0:T(1,128)} %seg_ref.1) | copy-start | bytes 12292
  112.3 20.2 %copy-start.3 = (f32[1024,512]{1,0:T(8,128)}, f32[1024,512]{1,0:T(8,128)S(1)}, u32[]{:S(2)}) copy-start(f32[1024,512]{1,0:T(8,128)S(1)} %get-tuple-element.140) | copy-start | bytes 6291460
  114.6 6.8 %copy-start.5 = (bf16[1024,512]{1,0:T(8,128)(2,1)S(1)}, bf16[1024,512]{1,0:T(8,128)(2,1)}, u32[]{:S(2)}) copy-start(bf16[1024,512]{1,0:T(8,128)(2,1)} %param.17) | copy-start | bytes 3145732
  114.6 6.8 %copy-start.24 = (bf16[4,512,512]{2,1,0:T(8,128)(2,1)S(1)}, bf16[4,512,512]{2,1,0:T(8,128)(2,1)}, u32[]{:S(2)}) copy-start(bf16[4,512,512]{2,1,0:T(8,128)(2,1)} %get-tuple-element.56) | copy-start | bytes 6291460
  136.7 3.1 copy-start.4
  139.8 3.3 %copy-start.27 = (bf16[4,1024,512]{1,2,0:T(8,128)(2,1)S(1)}, bf16[4,1024,512]{1,2,0:T(8,128)(2,1)}, u32[]{:S(2)}) copy-start(bf16[4,1024,512]{1,2,0:T(8,128)(2,1)} %get-tuple-element.142) | copy-start | bytes 12582916
  165.7 40.9 %collective-permute-start.3 = (bf16[512,512]{1,0:T(8,128)(2,1)}, bf16[512,512]{1,0:T(8,128)(2,1)S(1)}, u32[]{:S(2)}, u32[]{:S(2)}) collective-permute-start(bf16[512,512]{1,0:T(8,128)(2,1)} %get-tuple-element.66), channel_id=1, source_target_pairs={{0,2},{1,3},{2,0},{3,1},{4,6},{5,7},{6,4},{7,5},{8,10},{9,11},{10,... | collective-permute-start | bytes 1572872 | tf_op jit(solution)/shard_map/ppermute | solution.py:864
  167.2 39.5 %collective-permute-start.4 = (bf16[512,512]{1,0:T(8,128)(2,1)}, bf16[512,512]{1,0:T(8,128)(2,1)}, u32[]{:S(2)}, u32[]{:S(2)}) collective-permute-start(bf16[512,512]{1,0:T(8,128)(2,1)} %get-tuple-element.67), channel_id=1, source_target_pairs={{0,2},{1,3},{2,0},{3,1},{4,6},{5,7},{6,4},{7,5},{8,10},{9,11},{10,... | collective-permute-start | bytes 1572872 | tf_op jit(solution)/shard_map/ppermute | solution.py:864
  167.8 38.8 %collective-permute-start.5 = (bf16[512,128]{1,0:T(8,128)(2,1)}, bf16[512,128]{1,0:T(8,128)(2,1)S(1)}, u32[]{:S(2)}, u32[]{:S(2)}) collective-permute-start(bf16[512,128]{1,0:T(8,128)(2,1)} %get-tuple-element.68), channel_id=1, source_target_pairs={{0,2},{1,3},{2,0},{3,1},{4,6},{5,7},{6,4},{7,5},{8,10},{9,11},{10,... | collective-permute-start | bytes 393224 | tf_op jit(solution)/shard_map/ppermute | solution.py:864
  279.5 24.3 %copy-start.14 = (f32[64,384]{1,0:T(8,128)S(1)}, f32[64,384]{1,0:T(8,128)}, u32[]{:S(2)}) copy-start(f32[64,384]{1,0:T(8,128)} %get-tuple-element.71) | copy-start | bytes 294916
  304.4 4.9 %copy-start.1 = (bf16[64,3,128]{2,0,1:T(8,128)(2,1)S(1)}, bf16[64,3,128]{2,0,1:T(8,128)(2,1)}, u32[]{:S(2)}) copy-start(bf16[64,3,128]{2,0,1:T(8,128)(2,1)} %param.20) | copy-start | bytes 147460
  304.4 3.0 copy-start.15
  304.4 3.6 %copy-start.12 = (f32[64,512]{1,0:T(8,128)S(1)}, f32[64,512]{1,0:T(8,128)}, u32[]{:S(2)}) copy-start(f32[64,512]{1,0:T(8,128)} %get-tuple-element.172) | copy-start | bytes 393220
  304.4 4.3 %copy-start.11 = (f32[64,512]{1,0:T(8,128)S(1)}, f32[64,512]{1,0:T(8,128)}, u32[]{:S(2)}) copy-start(f32[64,512]{1,0:T(8,128)} %get-tuple-element.75) | copy-start | bytes 393220
  (10 other events, 11.0 us)

commit v5 on v4

--- a/solution.py
+++ b/solution.py
@@ -53,10 +53,12 @@
     return top, mid, (rest - mid.astype(f32)).astype(bf16)
 
 
-def diagonal_mask(start_ref, row_at, size):
+def diagonal_mask(seg_ref, row_at, size):
     key_pos = lax.broadcasted_iota(jnp.int32, (size, 1), 0)
     query_pos = lax.broadcasted_iota(jnp.int32, (1, size), 1)
-    first = start_ref[0:1, pl.ds(row_at, size)] - row_at
+    here = seg_ref.shape[2]
+    seg = seg_ref[row_at // here, 0:1, pl.ds(pl.multiple_of(lax.rem(row_at, here), size), size)]
+    first = jnp.where(seg == 0, query_pos, 0)
     return (key_pos >= first) & (key_pos <= query_pos)
 
 
@@ -235,12 +237,11 @@
     )(low, qb, ka, va, kt, g, o, start)
 
 
-def document_starts(seg_all):
-    positions = jnp.arange(seg_all.shape[0], dtype=jnp.int32)
-    number = jnp.arange(32, dtype=jnp.int32)[:, None]
-    before = jnp.sum(((seg_all > 0) & (seg_all < number)).astype(jnp.int32), axis=1)
-    own = jnp.sum(jnp.where(seg_all == number, before[:, None], 0), axis=0)
-    return jnp.where(seg_all == 0, positions, own)
+def first_blocks(seg_all, size):
+    firsts = seg_all[::size]
+    before = jnp.sum(((seg_all > 0) & (seg_all < firsts[:, None])).astype(jnp.int32), axis=1)
+    own = jnp.arange(firsts.shape[0], dtype=jnp.int32)
+    return jnp.where(firsts == 0, own, before // size)
 
 
 MESH = pl.DeviceIdType.MESH
@@ -319,8 +320,8 @@
 
 
 def enter_kernel(
-    x_ref, norm_ref, bias_ref, seg_ref, w0, w1, w2, w3,
-    normed_ref, segs_ref, qa_ref, ka_ref, va_ref, vt_ref, kt_ref, f0, f1, f2, f3,
+    x_ref, gain_ref, shift_ref, bias_ref, seg_ref, w0, w1, w2, w3,
+    normed_ref, segs_ref, qa_ref, ka_ref, va_ref, vt_ref, kt_ref, f0, f1,
     x_all, normed_s, qa_s, ka_s, va_s, vt_s, kt_s,
     sy, ry, ss, rs, sf, rf, sg, rg, sw, rw, own, own_w, outs, *, parts
 ):
@@ -341,75 +342,67 @@
     def rows_of(owner, part):
         return x_all.at[pl.ds(pl.multiple_of(owner * rows + part * step, step), step)]
 
-    groups = ((w0, f0), (w1, f1), (w2, f2), (w3, f3))
-    for part in range(parts):
-        mine = x_ref.at[pl.ds(part * step, step)]
-        sent.append(push(mine, rows_of(me, part), sy.at[part], ry.at[part], {"tp": across}))
+    sources = (w0, w1, w2, w3)
+
+    def block_of(g, index):
+        if g == 0:
+            return f0.at[index]
+        at = sum(w.shape[1] for w in sources[1:g])
+        return f1.at[index, :, pl.ds(at, sources[g].shape[1])]
 
     def send_hop(g, hop):
         bit, masks = hops[hop]
-        source, full = groups[g]
         peer = {"fsdp": flipped("fsdp", bit)}
         if hop > 0:
             before, arrived = hops[hop - 1]
             for mask in arrived:
-                block = full.at[flipped("fsdp", mask)]
+                block = block_of(g, flipped("fsdp", mask))
                 awaited(block, sw.at[g, mask], rw.at[g, mask], {"fsdp": flipped("fsdp", before)}).wait_recv()
         for mask in masks:
-            if mask == bit:
-                block = source
-            else:
-                block = full.at[flipped("fsdp", mask - bit)]
-            target = full.at[flipped("fsdp", mask - bit)]
+            target = block_of(g, flipped("fsdp", mask - bit))
+            block = sources[g] if mask == bit else target
             sent.append(push(block, target, sw.at[g, mask], rw.at[g, mask], peer))
 
     def end_hops(g):
         bit, arrived = hops[-1]
         for mask in arrived:
-            block = groups[g][1].at[flipped("fsdp", mask)]
+            block = block_of(g, flipped("fsdp", mask))
             awaited(block, sw.at[g, mask], rw.at[g, mask], {"fsdp": flipped("fsdp", bit)}).wait_recv()
 
-    send_hop(0, 0)
     for k, peer in enumerate((across, far, side)):
         sent.append(push(seg_ref, segs_ref.at[me], sg.at[k], rg.at[k], {"tp": peer}))
+    send_hop(0, 0)
+    for part in range(parts):
+        mine = x_ref.at[pl.ds(part * step, step)]
+        sent.append(push(mine, rows_of(me, part), sy.at[part], ry.at[part], {"tp": across}))
+    for g in (1, 2, 3):
+        send_hop(g, 0)
     for part in range(parts):
         mine = x_ref.at[pl.ds(part * step, step)]
         sent.append(push(mine, rows_of(me, part), ss.at[part], rs.at[part], {"tp": side}))
-    for g in (1, 2, 3):
-        send_hop(g, 0)
     kept = [
         pltpu.make_async_copy(x_ref, x_all.at[pl.ds(pl.multiple_of(me * rows, rows), rows)], own.at[0]),
         pltpu.make_async_copy(seg_ref, segs_ref.at[me], own.at[1]),
-    ] + [pltpu.make_async_copy(source, full.at[shard], own_w.at[g]) for g, (source, full) in enumerate(groups)]
+    ] + [pltpu.make_async_copy(source, block_of(g, shard), own_w.at[g]) for g, source in enumerate(sources)]
     for copy in kept:
         copy.start()
-
-    def forward(part):
-        here = rows_of(across, part)
-        awaited(here, sy.at[part], ry.at[part], {"tp": across}).wait_recv()
-        return push(here, here, sf.at[part], rf.at[part], {"tp": side})
-
     waves = sorted(
         ((hop + g, g, hop) for hop in range(1, len(hops)) for g in range(4)), key=lambda w: (w[0], w[1])
     )
-    first_last = [n for n, wave in enumerate(waves) if wave[1] == 0][-1]
-    for _, g, hop in waves[: first_last + 1]:
+    for _, g, hop in waves:
         send_hop(g, hop)
-    sent.append(forward(0))
     for k, peer in enumerate((across, far, side)):
         awaited(segs_ref.at[peer], sg.at[k], rg.at[k], {"tp": peer}).wait_recv()
     for part in range(parts):
         awaited(rows_of(side, part), ss.at[part], rs.at[part], {"tp": side}).wait_recv()
     for copy in kept:
         copy.wait()
-    later = waves[first_last + 1 :]
-    for _, g, hop in later[: (len(later) + 1) // 2]:
-        send_hop(g, hop)
-    sent.append(forward(1))
     end_hops(0)
 
-    gain, shift = norm_ref[0:1, :], norm_ref[1:2, :]
-    bias = bias_ref[0:1, :]
+    gain, shift = gain_ref[...].astype(f32), shift_ref[...].astype(f32)
+    bias_at = pl.ds(pl.multiple_of(me * width, width), width)
+    query_bias = bias_ref[0:1, bias_at].astype(f32)
+    value_bias = bias_ref[1:2, bias_at].astype(f32)
     number = lax.broadcasted_iota(jnp.int32, (step, 64), 1)
     number_f = number.astype(f32)
     key_ones = (number >= 32) & (number < 35)
@@ -436,10 +429,10 @@
         normed = (centred * inverse * gain + shift).astype(bf16)
         normed_s[span, :] = normed
         weights = f0[...].reshape(shards * f0.shape[1], 3 * width)
-        projected = dot_n(normed, weights) + bias
-        queries = (projected[:, 0:width].astype(bf16).astype(f32) * HD ** (-0.5)).astype(bf16)
+        projected = dot_n(normed, weights)
+        queries = ((projected[:, 0:width] + query_bias).astype(bf16).astype(f32) * HD ** (-0.5)).astype(bf16)
         keys = projected[:, width : 2 * width].astype(bf16)
-        values = projected[:, 2 * width : 3 * width].astype(bf16)
+        values = (projected[:, 2 * width : 3 * width] + value_bias).astype(bf16)
         seg = segs_ref[owner, 0:1, pl.ds(pl.multiple_of(part * step, step), step)].astype(f32)
         seg = jnp.broadcast_to(seg, (8, step)).T[:, 0:1]
         same = (seg == number_f) & (number < 32)
@@ -457,25 +450,26 @@
         for copy in copies_out(owner, part):
             copy.start()
 
-    def near(k, carry):
-        part = lax.rem(k, parts)
-        compute(me + (k // parts) * (side - me), part)
-        return carry
-
-    lax.fori_loop(0, 2 * parts, near, 0)
-    for _, g, hop in later[(len(later) + 1) // 2 :]:
-        send_hop(g, hop)
-
-    def distant(part, carry):
-        compute(across, part)
-        awaited(rows_of(far, part), sf.at[part], rf.at[part], {"tp": side}).wait_recv()
-        compute(far, part)
-        return carry
-
-    for part in range(2, parts):
-        sent.append(forward(part))
-        lax.fori_loop(part - 2, part - 1, distant, 0)
-    lax.fori_loop(parts - 2, parts, distant, 0)
+    def work(k, carry):
+        distant = k // (2 * parts)
+        part = lax.rem(k // 2, parts)
+        second = lax.rem(k, 2)
+
+        @pl.when((distant == 0) & (second == 0))
+        def _():
+            here = rows_of(across, part)
+            awaited(here, sy.at[part], ry.at[part], {"tp": across}).wait_recv()
+            push(here, here, sf.at[part], rf.at[part], {"tp": side})
+
+        @pl.when((distant == 1) & (second == 1))
+        def _():
+            awaited(rows_of(far, part), sf.at[part], rf.at[part], {"tp": side}).wait_recv()
+
+        first = me + distant * (across - me)
+        compute(first + second * (side - me + distant * (far - across - side + me)), part)
+        return carry
+
+    lax.fori_loop(0, 4 * parts, work, 0)
     for g in (1, 2, 3):
         end_hops(g)
 
@@ -485,18 +479,21 @@
         return carry
 
     lax.fori_loop(0, 4 * parts, drain, 0)
+    for part in range(parts):
+        awaited(rows_of(across, part), sf.at[part], rf.at[part], {"tp": side}).wait_send()
     for copy in sent:
         copy.wait_send()
 
 
-def enter(x, norm_rows, bias_rows, segments, weights, number, parts=4):
+def enter(x, gain, shift, bias, segments, weights, number, parts=4):
     rows, width = x.shape
     seq_rows = 4 * rows
     shards = lax.axis_size("fsdp")
     heads = weights[0].shape[1] // (3 * HD)
     dma = pltpu.SemaphoreType.DMA
     wide = (heads, seq_rows, 128)
-    full = [(shards, *w.shape) for w in weights]
+    shard_rows = weights[0].shape[0]
+    full = [(shards, *weights[0].shape), (shards, shard_rows, sum(w.shape[1] for w in weights[1:]))]
     shapes = [(seq_rows, width), wide, wide, wide, (heads, 80, seq_rows), (heads, 64, seq_rows)]
     made = [jax.ShapeDtypeStruct(s, bf16) for s in shapes]
     return comm_call(
@@ -506,8 +503,8 @@
         [made[0], jax.ShapeDtypeStruct((4, *segments.shape), segments.dtype)]
         + made[1:]
         + [jax.ShapeDtypeStruct(s, bf16) for s in full],
-        [in_vmem()] * 8,
-        [anywhere(), in_vmem()] + [anywhere()] * 5 + [in_vmem()] + [anywhere()] * 3,
+        [in_vmem()] * 9,
+        [anywhere(), in_vmem()] + [anywhere()] * 5 + [in_vmem(), anywhere()],
         [pltpu.VMEM((seq_rows, width), bf16)]
         + [pltpu.VMEM(s, bf16) for s in shapes]
         + [dma((parts,))] * 6
@@ -516,14 +513,15 @@
         + [dma((2,)), dma((4,)), dma((6, 4 * parts))],
         60 << 20,
         x,
-        norm_rows,
-        bias_rows,
+        gain,
+        shift,
+        bias,
         segments,
         *weights,
     )
 
 
-def exchange_out_kernel(x_ref, o0, o1, o2, c0, c1, c2, out_ref, g0, g1, g2, sems, rems, ws, wr, own):
+def exchange_out_kernel(x_ref, o_ref, c_ref, out_ref, g0, g1, g2, sems, rems, ws, wr, own):
     me, side, across, far = quad()
     rows = x_ref.shape[0] // 4
     greet([{"tp": side}, {"tp": across}, {"tp": far}])
@@ -532,7 +530,11 @@
     def mine(owner):
         return x_ref.at[pl.ds(pl.multiple_of(owner * rows, rows), rows)]
 
-    weights = ((o0, c0, g0), (o1, c1, g1), (o2, c2, g2))
+    weights, at = [], 0
+    for full in (g0, g1, g2):
+        cols = pl.ds(at, full.shape[2])
+        weights.append((o_ref.at[:, cols], c_ref.at[:, cols], full))
+        at += full.shape[2]
     sent = [push(mine(peers[k]), out_ref.at[k], sems.at[k], rems.at[k], {"tp": peers[k]}) for k in (3, 2, 1)]
     for n, (here, over, full) in enumerate(weights):
         sent.append(push(here, full.at[1], ws.at[0, n], wr.at[0, n], {"tp": side}))
@@ -549,7 +551,7 @@
         copy.wait()
 
 
-def exchange_out(x, own, over, number):
+def exchange_out(x, own, over, widths, number):
     rows, width = x.shape
     dma = pltpu.SemaphoreType.DMA
     return comm_call(
@@ -557,19 +559,19 @@
         "exchange_out",
         number,
         [jax.ShapeDtypeStruct((4, rows // 4, width), x.dtype)]
-        + [jax.ShapeDtypeStruct((4, *w.shape), w.dtype) for w in own],
-        [in_vmem()] * 7,
+        + [jax.ShapeDtypeStruct((4, own.shape[0], w), own.dtype) for w in widths],
+        [in_vmem()] * 3,
         [in_vmem()] * 4,
         [dma((4,)), dma((4,)), dma((2, 3)), dma((2, 3)), dma((7,))],
         60 << 20,
         x,
-        *own,
-        *over,
+        own,
+        over,
     )
 
 
 def exchange_grad_kernel(
-    x_ref, g0, g1, g2, out_ref, k0, k1, k2, a0, a1, a2, sems, rems, ws, wr, own, *boxes
+    x_ref, g0, g1, g2, out_ref, kept_ref, over_ref, sems, rems, ws, wr, own, *boxes
 ):
     me, side, across, far = quad()
     greet([{"tp": side}, {"tp": across}, {"tp": far}])
@@ -580,19 +582,22 @@
         return out_ref.at[pl.ds(pl.multiple_of(owner * rows, rows), rows)]
 
     sent = [push(x_ref.at[k], slot(me), sems.at[k], rems.at[k], {"tp": peers[k]}) for k in (3, 2)]
-    grads = ((g0, k0, a0), (g1, k1, a1), (g2, k2, a2))
+    grads = (g0, g1, g2)
     folded = []
-    for n, (grad, _, _) in enumerate(grads):
+    for n, grad in enumerate(grads):
         folded.append(push(grad.at[3], boxes[2 * n + 1], ws.at[1, n], wr.at[1, n], {"tp": side}))
         folded.append(push(grad.at[1], boxes[2 * n], ws.at[0, n], wr.at[0, n], {"tp": side}))
     sent.append(push(x_ref.at[1], slot(me), sems.at[1], rems.at[1], {"tp": side}))
     keep = pltpu.make_async_copy(x_ref.at[0], slot(me), own)
     keep.start()
-    for n, (grad, kept, over) in enumerate(grads):
+    at = 0
+    for n, grad in enumerate(grads):
+        cols = slice(at, at + grad.shape[2])
+        at += grad.shape[2]
         folded[2 * n].wait()
-        over[...] = (grad[2].astype(f32) + boxes[2 * n + 1][...].astype(f32)).astype(bf16)
+        over_ref[:, cols] = (grad[2].astype(f32) + boxes[2 * n + 1][...].astype(f32)).astype(bf16)
         folded[2 * n + 1].wait()
-        kept[...] = (grad[0].astype(f32) + boxes[2 * n][...].astype(f32)).astype(bf16)
+        kept_ref[:, cols] = (grad[0].astype(f32) + boxes[2 * n][...].astype(f32)).astype(bf16)
     keep.wait()
     for k, peer in ((3, far), (2, across), (1, side)):
         awaited(slot(peer), sems.at[k], rems.at[k], {"tp": peer}).wait_recv()
@@ -603,7 +608,7 @@
 def exchange_grad(x, grads, number):
     _, rows, width = x.shape
     dma = pltpu.SemaphoreType.DMA
-    pieces = [jax.ShapeDtypeStruct(g.shape[1:], g.dtype) for g in grads]
+    piece = jax.ShapeDtypeStruct((grads[0].shape[1], sum(g.shape[2] for g in grads)), x.dtype)
     boxes = []
     for g in grads:
         boxes += [pltpu.VMEM(g.shape[1:], g.dtype)] * 2
@@ -611,9 +616,9 @@
         exchange_grad_kernel,
         "exchange_grad",
         number,
-        [jax.ShapeDtypeStruct((4 * rows, width), x.dtype)] + pieces + pieces,
+        [jax.ShapeDtypeStruct((4 * rows, width), x.dtype), piece, piece],
         [in_vmem()] * 4,
-        [in_vmem()] * 7,
+        [in_vmem()] * 3,
         [dma((4,)), dma((4,)), dma((2, 3)), dma((2, 3)), dma] + boxes,
         60 << 20,
         x,
@@ -622,26 +627,41 @@
 
 
 def leave_kernel(
-    grad_ref, normed_ref, w_ref, k0, k1, k2, a0, a1, a2, early_ref,
-    rows_ref, s0, s1, s2, s3, cols_ref, early_out,
-    far_out, own_out, sum_buf, side_far, side_own, over, dw_acc, early_box,
-    sa, ra, sb, rb, sy, ry, sw, rw, se, re, *bufs, parts, hops, all_hops
+    grad_ref, normed_ref, w_ref, kept_ref, came_ref, early_ref, x_ref, gain_ref, resid_ref,
+    input_ref, s0, s1, s2, s3, early_out, late_out,
+    rows_ref, far_out, own_out, sum_buf, side_far, side_own, over, dw_acc, cols_ref,
+    late_ref, early_mid, late_mid, early_one, early_two, late_one, late_two,
+    sa, ra, sb, rb, sy, ry, sw, rw, se, re, sl, rl, se2, re2, sl2, rl2, *bufs, parts, hops
 ):
     me, side, across, far = quad()
     rows = rows_ref.shape[0]
     step = rows // parts
-    greet([{"tp": side}, {"tp": across}] + [{axis: flip(axis, bit)} for axis, bit in hops])
+    shard, shards = lax.axis_index("fsdp"), early_two.shape[0]
+    barrier = pltpu.get_barrier_semaphore()
+    for peer in (side, across, far):
+        pl.semaphore_signal(barrier, inc=1, device_id={"tp": peer}, device_id_type=MESH)
+
+    def other(k):
+        return {"fsdp": lax.rem(shard + k, shards)}
+
+    def signal(k, carry):
+        pl.semaphore_signal(barrier, inc=1, device_id=other(k), device_id_type=MESH)
+        return carry
+
+    lax.fori_loop(1, shards, signal, 0)
+    pl.semaphore_wait(barrier, 3 + shards - 1)
     count = len(hops)
     outs = (s0, s1, s2, s3)
-    mlp = ((k0, a0), (k1, a1), (k2, a2))
     current = bufs[0:4]
     boxes = [bufs[4 + g * count : 4 + (g + 1) * count] for g in range(4)]
     keeps = [bufs[4 + 4 * count + g * (count - 1) : 4 + 4 * count + (g + 1) * (count - 1)] for g in range(4)]
     sent = []
 
     def begin(g):
-        kept, arrived = mlp[g]
-        current[g][...] = (kept[...].astype(f32) + arrived[...].astype(f32)).astype(bf16)
+        at = sum(c.shape[3] for c in current[0:g])
+        cols = slice(at, at + current[g].shape[3])
+        total = kept_ref[:, :, :, cols].astype(f32) + came_ref[:, :, :, cols].astype(f32)
+        current[g][...] = total.astype(bf16)
 
     def hop_parts(g, k):
         axis, bit = hops[k]
@@ -665,16 +685,35 @@
                 target[n // 2, n % 2] = total.astype(bf16)
             hop_send(g, k + 1)
 
-    def early_send(k):
-        axis, bit = all_hops[k]
-        sent.append(push(early_out.at[k], early_box.at[k], se.at[k], re.at[k], {axis: flip(axis, bit)}))
-
-    def early_add(k):
-        axis, bit = all_hops[k]
-        awaited(early_box.at[k], se.at[k], re.at[k], {axis: flip(axis, bit)}).wait_recv()
-        early_out[k + 1] = early_out[k] + early_box[k]
-        if k + 1 < len(all_hops):
-            early_send(k + 1)
+    def tp_send(value, box, send, recv):
+        box[me] = value[...]
+        for k, peer in enumerate((side, across, far)):
+            sent.append(push(value, box.at[me], send.at[k], recv.at[me], {"tp": peer}))
+
+    def tp_sum(value, box, send, recv):
+        for k, peer in enumerate((side, across, far)):
+            awaited(box.at[peer], send.at[k], recv.at[peer], {"tp": peer}).wait_recv()
+        value[...] = box[0] + box[1] + box[2] + box[3]
+
+    def fsdp_send(value, box, send, recv):
+        box[shard] = value[...]
+
+        def give(k, carry):
+            push(value, box.at[shard], send.at[k], recv.at[shard], other(k))
+            return carry
+
+        lax.fori_loop(1, shards, give, 0)
+
+    def fsdp_sum(value, target, box, send, recv):
+        def take(k, carry):
+            peer = lax.rem(shard + k, shards)
+            copy = awaited(box.at[peer], send.at[k], recv.at[peer], other(k))
+            copy.wait_recv()
+            copy.wait_send()
+            return carry
+
+        lax.fori_loop(1, shards, take, 0)
+        target[...] = lax.fori_loop(1, shards, lambda n, total: total + box[n], box[0])
 
     def span(owner, part):
         return pl.ds(pl.multiple_of(owner * rows + part * step, step), step)
@@ -712,10 +751,20 @@
         rows_ref[here, :] = mine + side_own[here, :].astype(f32)
         return carry
 
+    gain = gain_ref[...].astype(f32)
+
     def take_over(part, carry):
         here = piece(part)
+        x = x_ref[here, :].astype(f32)
+        centred = x - jnp.mean(x, axis=-1, keepdims=True)
+        inverse = lax.rsqrt(jnp.mean(centred * centred, axis=-1, keepdims=True) + epsilon)
+        normed = centred * inverse
         awaited(over.at[here], sy.at[part], ry.at[part], {"tp": across}).wait_recv()
-        rows_ref[here, :] += over[here, :].astype(f32)
+        grad = rows_ref[here, :] + over[here, :].astype(f32)
+        grad_in, gain_part, shift_part = norm_back(grad, normed, inverse, gain)
+        input_ref[here, :] = (resid_ref[here, :] + grad_in).astype(bf16)
+        late_ref[0:1, :] += gain_part[None]
+        late_ref[1:2, :] += shift_part[None]
         return carry
 
     def drain(part, carry):
@@ -725,11 +774,12 @@
         awaited(sum_buf.at[here], sy.at[part], ry.at[part], {"tp": across}).wait_send()
         return carry
 
+    tp_send(early_ref, early_one, se, re)
     lax.fori_loop(0, parts, give_far, 0)
     begin(0)
     hop_send(0, 0)
-    early_out[0] = early_ref[...]
-    early_send(0)
+    tp_sum(early_mid, early_one, se, re)
+    fsdp_send(early_mid, early_two, se2, re2)
     lax.fori_loop(0, parts, give_over, 0)
     for g in (1, 2):
         begin(g)
@@ -751,55 +801,59 @@
     lax.fori_loop(0, grad_ref.shape[0] // chunk, weight_grad, 0)
     current[3][...] = dw_acc[...].astype(bf16).reshape(current[3].shape)
     hop_send(3, 0)
+    late_ref[...] = jnp.zeros_like(late_ref)
+    wide = cols_ref.shape[1] // 3
+    qv_at = pl.ds(pl.multiple_of(me * wide, wide), wide)
+    late_ref[2:3, qv_at] = cols_ref[0:1, 0:wide]
+    late_ref[3:4, qv_at] = cols_ref[0:1, 2 * wide : 3 * wide]
     lax.fori_loop(0, parts, give_own, 0)
-    early_add(0)
     order = sorted(((k + g, g, k) for g in range(4) for k in range(count)), key=lambda w: (w[0], w[1]))
-    later = list(range(1, len(all_hops)))
     for n, (_, g, k) in enumerate(order):
         hop_add(g, k)
-        if n % 2 == 1 and later:
-            early_add(later.pop(0))
         if n == len(order) // 2:
             lax.fori_loop(0, parts, take_own, 0)
-    for k in later:
-        early_add(k)
     lax.fori_loop(0, parts, take_over, 0)
+    tp_send(late_ref, late_one, sl, rl)
+    fsdp_sum(early_mid, early_out, early_two, se2, re2)
+    tp_sum(late_mid, late_one, sl, rl)
+    fsdp_send(late_mid, late_two, sl2, rl2)
     lax.fori_loop(0, parts, drain, 0)
+    fsdp_sum(late_mid, late_out, late_two, sl2, rl2)
     for copy in sent:
         copy.wait_send()
 
 
-def leave(grad, normed, w, kept, came, early, number, parts=4):
+def leave(grad, normed, w, kept, came, widths, early, x, gain, resid, number, parts=4):
     rows, width = grad.shape[0] // 4, w.shape[0]
     dma = pltpu.SemaphoreType.DMA
     hops = bits_of("fsdp")
-    all_hops = bits_of("tp") + hops
     count = len(hops)
     shards = lax.axis_size("fsdp")
     shard = width // shards
-    widths = [k.shape[1] for k in kept] + [grad.shape[1]]
+    widths = [*widths, grad.shape[1]]
     split = (shards // 2, 2, shard)
     current = [pltpu.VMEM((*split, n), bf16) for n in widths]
     boxes = [pltpu.VMEM((shards >> (k + 1), shard, n), bf16) for n in widths for k in range(count)]
     keeps = [pltpu.VMEM((shards >> (k + 2), 2, shard, n), bf16) for n in widths for k in range(count - 1)]
-    pieces = [x.reshape(*split, x.shape[1]) for x in (*kept, *came)]
+    late = (4, width)
     return comm_call(
-        functools.partial(leave_kernel, parts=parts, hops=hops, all_hops=all_hops),
+        functools.partial(leave_kernel, parts=parts, hops=hops),
         "leave",
         number,
-        [jax.ShapeDtypeStruct((rows, width), f32)]
+        [jax.ShapeDtypeStruct((rows, width), bf16)]
         + [jax.ShapeDtypeStruct((shard, n), f32) for n in widths]
-        + [
-            jax.ShapeDtypeStruct((8, grad.shape[1]), f32),
-            jax.ShapeDtypeStruct((len(all_hops) + 1, *early.shape), f32),
-        ],
-        [in_vmem()] * 10,
+        + [jax.ShapeDtypeStruct(early.shape, f32), jax.ShapeDtypeStruct(late, f32)],
+        [in_vmem()] * 9,
         [in_vmem()] * 7,
-        [pltpu.VMEM((rows, width), bf16)] * 6
-        + [pltpu.VMEM((width, grad.shape[1]), f32), pltpu.VMEM((len(all_hops), *early.shape), f32)]
+        [pltpu.VMEM((rows, width), f32)]
+        + [pltpu.VMEM((rows, width), bf16)] * 6
+        + [pltpu.VMEM((width, grad.shape[1]), f32), pltpu.VMEM((8, grad.shape[1]), f32)]
+        + [pltpu.VMEM(late, f32), pltpu.VMEM(early.shape, f32), pltpu.VMEM(late, f32)]
+        + [pltpu.VMEM((n, *shape), f32) for shape in (early.shape, late) for n in (4, shards)]
         + [dma((parts,))] * 6
         + [dma((4, count))] * 2
-        + [dma((len(all_hops),))] * 2
+        + [dma((3,)), dma((4,))] * 2
+        + [dma((shards,))] * 4
         + current
         + boxes
         + keeps,
@@ -807,19 +861,13 @@
         grad,
         normed,
         w,
-        *pieces,
+        kept.reshape(*split, kept.shape[1]),
+        came.reshape(*split, came.shape[1]),
         early,
-    )
-
-
-def all_sum_kernel(x_ref, out_ref, sems, rems, inbox, *, hops):
-    greet([{axis: flip(axis, bit)} for axis, bit in hops])
-    out_ref[...] = x_ref[...]
-    for k, (axis, bit) in enumerate(hops):
-        peer = {axis: flip(axis, bit)}
-        copy = push(out_ref, inbox.at[k], sems.at[k], rems.at[k], peer)
-        copy.wait()
-        out_ref[...] = out_ref[...] + inbox[k]
+        x,
+        gain,
+        resid,
+    )
 
 
 def flip(axis, bit):
@@ -833,23 +881,6 @@
         bits.append((axis, bit))
         bit *= 2
     return bits
-
-
-def all_sum(x, number):
-    hops = bits_of("tp") + bits_of("fsdp")
-    dma = pltpu.SemaphoreType.DMA
-    count = len(hops)
-    return comm_call(
-        functools.partial(all_sum_kernel, hops=hops),
-        "all_sum",
-        number,
-        jax.ShapeDtypeStruct(x.shape, f32),
-        [in_vmem()],
-        in_vmem(),
-        [dma((count,)), dma((count,)), pltpu.VMEM((count, *x.shape), f32)],
-        10 << 20,
-        x,
-    )
 
 
 def relative(value):
@@ -881,42 +912,32 @@
     proj_weight,
     proj_bias,
 ):
-    tp_index = lax.axis_index("tp")
     slices = lax.axis_size("tp")
     rows_here, model_width = inputs.shape
     shard_rows = qkv_weight.shape[0]
     head_cols = qkv_weight.shape[2]
     hidden_cols = fc_weight.shape[1]
-    qv_here = lax.dynamic_slice_in_dim(qv_bias, tp_index * head_cols, head_cols, 1).astype(f32)
-    bias_here = jnp.concatenate([qv_here[0], jnp.zeros((head_cols,), f32), qv_here[1]])
-    bias_rows = jnp.broadcast_to(bias_here[None], (8, 3 * head_cols))
-    norm_rows = jnp.concatenate(
-        [first_gain[None], first_shift[None], jnp.zeros((6, model_width), bf16)], axis=0
-    ).astype(f32)
-    seq_normed, seg_parts, qa, ka, va, vt, kt, qkv_full, fc_slice, proj_slice, out_slice = enter(
+    seq_normed, seg_parts, qa, ka, va, vt, kt, qkv_full, own = enter(
         inputs,
-        norm_rows,
-        bias_rows,
+        first_gain[None],
+        first_shift[None],
+        qv_bias,
         segments,
         (qkv_weight.reshape(shard_rows, 3 * head_cols), fc_weight, proj_weight.T, out_weight.T),
         0,
     )
     qkv_full = qkv_full.reshape(model_width, 3 * head_cols)
-    own = [w.reshape(model_width, w.shape[2]) for w in (fc_slice, proj_slice, out_slice)]
-    over = [across(w) for w in own]
+    own = own.reshape(model_width, own.shape[2])
+    over = across(own)
+    widths = (hidden_cols, hidden_cols, head_cols)
 
     resid_in = inputs.astype(f32)
-    _, hat_one, inv_one = layer_norm(
-        resid_in, first_gain.astype(f32), first_shift.astype(f32)
-    )
     seq_rows = seq_normed.shape[0]
     seg_all = seg_parts.reshape(seq_rows)
-    start = document_starts(seg_all)
-    size = min(BLOCK, seq_rows)
-    low = start[::size] // size
-    start_rows = jnp.broadcast_to(start[None], (8, seq_rows))
-    attn_out, qb = attend(low, qa, ka, vt, start_rows, size)
-    attn_here, fc_full, proj_full, out_full = exchange_out(attn_out, own, over, 1)
+    size = min(BLOCK, rows_here)
+    low = first_blocks(seg_all, size)
+    attn_out, qb = attend(low, qa, ka, vt, seg_parts, size)
+    attn_here, fc_full, proj_full, out_full = exchange_out(attn_out, own, over, widths, 1)
 
     hidden = (
         resid_in
@@ -959,48 +980,43 @@
     grad_attn = jnp.einsum("sd,pdc->psc", grad_hidden_low, out_full, preferred_element_type=f32).astype(
         bf16
     ) * live_here[None, :, None]
-    grad_attn_seq, *halves = exchange_grad(
+    grad_attn_seq, kept, passed = exchange_grad(
         grad_attn, (fc_grad.astype(bf16), proj_grad.astype(bf16), out_grad_part.astype(bf16)), 2
     )
-    kept, came = halves[0:3], [across(half) for half in halves[3:6]]
-    grad_qkv = attend_back(low, qb, ka, va, kt, grad_attn_seq, attn_out, start_rows, size)
+    came = across(passed)
+    grad_qkv = attend_back(low, qb, ka, va, kt, grad_attn_seq, attn_out, seg_parts, size)
     early = [out_bias_part, second_gain_part, second_shift_part, fc_bias_part, proj_bias_part]
-    grad_normed_one, fc_w_grad, proj_w_grad, out_w_grad, qkv_grad, col_sums, early_sums = leave(
-        grad_qkv, seq_normed, qkv_full, kept, came, jnp.concatenate(early).reshape(-1, 128), 3
-    )
-    grad_in_ln, first_gain_part, first_shift_part = norm_back(
-        grad_normed_one, hat_one, inv_one, first_gain.astype(f32)
-    )
-    input_grad = (grad_hidden + grad_in_ln).astype(bf16)
+    input_grad, fc_w_grad, proj_w_grad, out_w_grad, qkv_grad, early_sums, late_sums = leave(
+        grad_qkv,
+        seq_normed,
+        qkv_full,
+        kept,
+        came,
+        widths,
+        jnp.concatenate(early).reshape(-1, 128),
+        inputs,
+        first_gain[None],
+        grad_hidden,
+        3,
+    )
     proj_w_grad = proj_w_grad.T
     out_w_grad = out_w_grad.T
     qkv_grad = qkv_grad.reshape(shard_rows, 3, head_cols)
-    col_sums = col_sums[0]
-    qv_part = jnp.stack([col_sums[0:head_cols], col_sums[2 * head_cols :]])
-    qv_full = lax.dynamic_update_slice_in_dim(
-        jnp.zeros((2, model_width), f32), qv_part, tp_index * head_cols, 1
-    )
-    late = [first_gain_part, first_shift_part, qv_full.reshape(-1)]
-    late_sums = all_sum(jnp.concatenate(late).reshape(-1, 128), 4)
-
-    def pieces(totals, vectors):
-        totals, found, at = totals.reshape(-1), [], 0
-        for vector in vectors:
-            found.append(totals[at : at + vector.shape[0]])
-            at += vector.shape[0]
-        return found
-
-    first_gain_grad, first_shift_grad, qv_bias_grad = pieces(late_sums, late)
-    out_bias_grad, second_gain_grad, second_shift_grad, fc_bias_grad, proj_bias_grad = pieces(
-        early_sums[-1], early
-    )
+    totals, found, at = early_sums.reshape(-1), [], 0
+    for vector in early:
+        found.append(totals[at : at + vector.shape[0]])
+        at += vector.shape[0]
+    out_bias_grad, second_gain_grad, second_shift_grad, fc_bias_grad, proj_bias_grad = found
+    first_gain_grad, first_shift_grad = late_sums[0], late_sums[1]
+    qv_bias_grad = late_sums[2:4]
+
     return (
         layer_out,
         input_grad,
         first_gain_grad,
         first_shift_grad,
         qkv_grad,
-        qv_bias_grad.reshape(2, model_width),
+        qv_bias_grad,
         out_w_grad,
         out_bias_grad,
         second_gain_grad,

time: 313 us -> 269 us (0.86)
  Pallas kernels: 232 us -> 203 us
  other arithmetic: 15.8 us -> 5.2 us
  starting transfers between devices: 6.21 us -> 1.76 us
  local copies, waits for them, and re-layouts: 16.2 us -> 19.6 us
    pallas_call x5 -> x4, Pallas kernels: 178 us -> 145 us  [comm_call(): pl.pallas_call(kernel, out_shape=out_shape, in_specs=in_specs, out_specs=...]
    ppermute x6 -> x2, starting transfers between devices: 6.21 us -> 1.76 us  [across(): return lax.ppermute(value, 'tp', [(n, n ^ 2) for n in range(4)])]
    convert_element_type x4 -> x0, other arithmetic: 4.42 us -> none  [the longest x1 2.99 us: local(): input_grad = (grad_hidden + grad_in_ln).astype(bf16)]
    reduce_sum x4 -> x1, other arithmetic: 4.69 us -> 0.93 us  [first_blocks(): jnp.sum(((seg_all > 0) & (seg_all < firsts[:, None])).astype(jnp.int32),...]
    unnamed x66 -> x54, local copies, waits for them, and re-layouts: 6.38 us -> 9.96 us
  transfers between devices with their start and end apart: 6 -> 2, of which waited for: 0 -> 0; matrix products, arithmetic and copies ran while one was open for 4% -> 4% of each run, Pallas kernels for 17% -> 22%
where the time goes in v5:
time: 269 us; the launch traced here: 268 us
  Pallas kernels  203 us (75%)
  matrix products  37.2 us (14%)
  local copies, waits for them, and re-layouts  19.6 us (7%)
  other arithmetic  5.2 us (2%)
    pallas_call x4, Pallas kernels, comm_call(): pl.pallas_call(kernel, out_shape=out_shape, in_specs=in_specs, out_specs=...  145 us
    pallas_call x1, Pallas kernels, attend_back(): pl.pallas_call(functools.partial(attend_back_kernel, size=size, blocks=ro...  33.4 us
    pallas_call x1, Pallas kernels, attend(): pl.pallas_call(functools.partial(attend_kernel, size=size, blocks=rows //...  25.1 us
    unnamed x54, local copies, waits for them, and re-layouts  9.96 us
    dot_general x1, matrix products, local(): jnp.einsum('sd,tdf->tsf', mlp_in, fc_full, preferred_element_type=f32)  6.73 us
    dot_general x1, matrix products, local(): jnp.einsum('sd,tdf->tsf', out_grad, proj_full, preferred_element_type=f32)  6.43 us
    dot_general x1, matrix products, local(): jnp.einsum('tsf,tdf->sd', act_low, proj_full, preferred_element_type=f32)  6.22 us
  transfers between devices with their start and end apart: 2, of which 0 were waited for; matrix products, arithmetic and copies ran while one was open for 4% of the time, Pallas kernels for 22%

profile of v5, /device:TPU:0, one launch (start us, length us, event | category | flops | bytes accessed | tf_op | source)
XLA Modules:
  0.0 268.0 jit_solution(1736524386835340515)
XLA Ops:
  0.7 1.3 broadcast_in_dim.4.gain_ref
  3.8 46.1 %enter.1 = (bf16[4096,512]{1,0:T(8,128)(2,1)}, s32[4,1,1024]{2,1,0:T(1,128)}, bf16[2,4096,128]{2,1,0:T(8,128)(2,1)}, bf16[2,4096,128]{2,1,0:T(8,128)(2,1)}, bf16...) custom-call(bf16[1024,512]{1,0:T(8,128)(2,1)} %x_ref.3, ...), custom_call_target="tpu_custom_call" | custom-call | bytes 62914560 | tf_op jit(solution)/shard_map/enter/pallas_call | solution.py:279
  53.0 25.1 %attend.1 = (bf16[4096,128]{1,0:T(8,128)(2,1)}, bf16[2,4096,128]{2,1,0:T(8,128)(2,1)}) custom-call(s32[8]{0:T(128)} %compare_select_fusion.low_ref, bf16[2,4096,128]{2,1,0:T(8,128)(2,1)} %get-tuple-element.40.qa_ref, bf16[2,4096,128]{2,1,0:T(8,128)(2,1)} %get-tuple-element.41.ka_ref, bf16[2,80,4096]{2,1,0:T(8,128)(2,1)} %get-tuple-element.42.vt_ref, ...), custom_call_target="tpu_custom_call" | custom-call | flops 30064771072 | bytes 8388608 | tf_op jit(solution)/shard_map/attend/pallas_call | solution.py:126
  79.6 19.3 %exchange_out.1 = (bf16[4,1024,128]{2,1,0:T(8,128)(2,1)}, bf16[4,512,512]{2,1,0:T(8,128)(2,1)}, bf16[4,512,512]{2,1,0:T(8,128)(2,1)}, bf16[4,512,128]{2,1,0:T(8,128)(2,1)}) custom-call(bf16[4096,128]{1,0:T(8,128)(2,1)} %get-tuple-element.43.x_ref.o_ref, bf16[512,1152]{1,0:T(8,128)(2,1)} %bitcast.116, bf16[512,1152]{1,0:T(8,128)(2,1)} %copy-done.4), custom_call_target="tpu_custom_call" | custom-call | bytes 62914560 | tf_op jit(solution)/shard_map/exchange_out/pallas_call | solution.py:279
  98.9 2.2 fusion.23
  102.7 6.7 %fusion.1 = (bf16[4,1024,512]{1,2,0:T(8,128)(2,1)}, f32[4,512,1024]{2,1,0:T(8,128)S(1)}) fusion(f32[4,512]{1,0:T(4,128)S(1)} %add.72, bf16[4,512,512]{2,1,0:T(8,128)(2,1)S(1)} %copy-done.19, f32[1024,512]{1,0:T(8,128)S(1)} %get-tuple-element.120, f32[512]{0:T(512)S(1)} %convert_element_type.77, f32[512]{0:T(512)S(1)} %convert_element_type.76, ...), kind=kOutput, calls=%fused_computation.4 | convolution fusion | flops 2164785152 | bytes 16797696 | tf_op jit(solution)/shard_map/sd,tdf->tsf/dot_general | solution.py:951
  109.5 6.4 %convert_reduce_fusion = (f32[4,512]{1,0:T(4,128)S(1)}, bf16[4,1024,512]{1,2,0:T(8,128)(2,1)S(1)}) fusion(f32[4,512,1024]{2,1,0:T(8,128)S(1)} %get-tuple-element.123, f32[4,512]{1,0:T(4,128)S(1)} %add.72, bf16[4,512,512]{2,1,0:T(8,128)(2,1)S(1)} %copy-done.18, bf16[1024,512]{1,0:T(8,128)(2,1)S(1)} %copy-done.7), kind=kOutput, calls=%fused_computation.5 | convolution fusion | flops 2174744576 | bytes 15745024 | tf_op jit(solution)/shard_map/sd,tdf->tsf/dot_general | solution.py:962
  115.9 4.4 %fusion.2 = (f32[512]{0:T(512)S(1)}, f32[1024]{0:T(1024)S(1)}, f32[1024]{0:T(1024)S(1)}, f32[512]{0:T(512)S(1)}, f32[1024,512,1]{1,0,2:T(8,128)}) fusion(f32[1024,512]{1,0:T(8,128)S(1)} %get-tuple-element.120, f32[1024]{0:T(1024)S(1)} %add_rsqrt_fusion, f32[1024]{0:T(1024)S(1)} %broadcast_multiply_fusion.2, f32[512]{0:T(512)S(1)} %convert_element_type.76, ...), kind=kOutput, calls=%fused_computation.12 | convolution fusion | flops 2152199168 | bytes 10508288 | tf_op jit(solution)/shard_map/tsf,tdf->sd/dot_general | solution.py:967
  120.3 4.1 %convert_bitcast_fusion.1.g0 = bf16[4,512,512]{2,1,0:T(8,128)(2,1)} fusion(bf16[4,1024,512]{1,2,0:T(8,128)(2,1)S(1)} %get-tuple-element.125, f32[1024,512]{1,0:T(8,128)S(1)} %get-tuple-element.120, f32[512]{0:T(512)S(1)} %convert_element_type.77, f32[512]{0:T(512)S(1)} %convert_element_type.76, f32[1024]{0:T(1024)S(1)} %add_rsqrt_fusion, ...), kind=kOutput, calls=%fused_computation.20 | convolution fusion | flops 2151153664 | bytes 8400896 | tf_op jit(solution)/shard_map/sd,tsf->tdf/dot_general | solution.py:965
  124.6 2.5 convert_reduce_fusion.2
  127.1 1.6 fusion.9.g2
  128.7 1.7 fusion.8.x_ref
  131.3 3.9 %convert_bitcast_fusion.g1 = bf16[4,512,512]{2,1,0:T(8,128)(2,1)} fusion(bf16[4,1024,512]{1,2,0:T(8,128)(2,1)S(1)} %copy-done.21, bf16[1024,512]{1,0:T(8,128)(2,1)S(1)} %copy-done.7), kind=kOutput, calls=%fused_computation.19 | convolution fusion | flops 2148532224 | bytes 7340032 | tf_op jit(solution)/shard_map/sd,tsf->tdf/dot_general | solution.py:961
  135.2 18.9 %exchange_grad.1 = (bf16[4096,128]{1,0:T(8,128)(2,1)}, bf16[512,1152]{1,0:T(8,128)(2,1)}, bf16[512,1152]{1,0:T(8,128)(2,1)}) custom-call(bf16[4,1024,128]{2,1,0:T(8,128)(2,1)} %fusion.8.x_ref, bf16[4,512,512]{2,1,0:T(8,128)(2,1)} %convert_bitcast_fusion.1.g0, bf16[4,512,512]{2,1,0:T(8,128)(2,1)} %convert_bitcast_fusion.g1, bf16[4,512,128]{2,1,0:T(8,128)(2,1)} %fusion.9.g2), custom_call_target="tpu_custom_call" | custom-call | bytes 62914560 | tf_op jit(solution)/shard_map/exchange_grad/pallas_call | solution.py:279
  154.1 1.7 collective-permute-start.1
  155.8 33.4 %attend_back.1.grad_ref = bf16[4096,384]{1,0:T(8,128)(2,1)} custom-call(s32[8]{0:T(128)} %compare_select_fusion.low_ref, bf16[2,4096,128]{2,1,0:T(8,128)(2,1)} %get-tuple-element.49.qb_ref, bf16[2,4096,128]{2,1,0:T(8,128)(2,1)} %get-tuple-element.41.ka_ref, bf16[2,4096,128]{2,1,0:T(8,128)(2,1)} %get-tuple-element.50.va_ref, ...), custom_call_target="tpu_custom_call" | custom-call | flops 51539607552 | bytes 16777216 | tf_op jit(solution)/shard_map/attend_back/pallas_call | solution.py:217
  189.2 6.2 %fusion.4 = bf16[1024,512]{1,0:T(8,128)(2,1)} fusion(f32[1024,512]{1,0:T(8,128)S(1)} %get-tuple-element.120, bf16[4,1024,512]{1,2,0:T(8,128)(2,1)} %get-tuple-element.122, bf16[4,512,512]{2,1,0:T(8,128)(2,1)} %get-tuple-element.48, f32[512]{0:T(512)S(1)} %convert_element_type.80), kind=kOutput, calls=%fused_computation.15 | convolution fusion | flops 2149056512 | bytes 9439232 | tf_op jit(solution)/shard_map/tsf,tdf->sd/dot_general | solution.py:958
  196.5 60.4 %leave.1 = (bf16[1024,512]{1,0:T(8,128)(2,1)}, f32[64,512]{1,0:T(8,128)}, f32[64,512]{1,0:T(8,128)}, f32[64,128]{1,0:T(8,128)}, f32[64,384]{1,0:T(8,128)}, /*index=5*/f32[32,128]{1,0:T(8,128)}, f32[4,512]{1,0:T(4,128)}) custom-call(bf16[4096,384]{1,0:T(8,128)(2,1)} %attend_back.1.grad_ref, bf16[4096,512]{1,0:T(8,128)(2,1)} %get-tuple-element.53.normed_ref, ...), custom_call_target="tpu_custom_call" | custom-call | bytes 62914560 | tf_op jit(solution)/shard_map/leave/pallas_call | solution.py:279
  256.9 1.3 slice_bitcast_fusion.1
  258.3 1.3 slice_bitcast_fusion
  259.6 1.4 fusion.22
  260.9 1.3 slice.45
  262.2 1.5 copy_bitcast_fusion
  263.8 2.3 copy.94
  (81 shorter events, 11.9 us)
Async XLA Ops:
  0.6 1.3 copy-start
  49.9 28.6 %collective-permute-start = (bf16[512,1152]{1,0:T(8,128)(2,1)}, bf16[512,1152]{1,0:T(8,128)(2,1)S(1)}, u32[]{:S(2)}, u32[]{:S(2)}) collective-permute-start(bf16[512,1152]{1,0:T(8,128)(2,1)} %bitcast.115), channel_id=1, source_target_pairs={{0,2},{1,3},{2,0},{3,1},{4,6},{5,7},{6,4},{7,5},{8,10},{9,11},{10,... | collective-permute-start | bytes 3538952 | tf_op jit(solution)/shard_map/ppermute | solution.py:895
  52.9 25.2 %copy-start.14 = (bf16[512]{0:T(512)(128)(2,1)S(1)}, bf16[512]{0:T(512)(128)(2,1)}, u32[]{:S(2)}) copy-start(bf16[512]{0:T(512)(128)(2,1)} %param.23) | copy-start | bytes 3076
  52.9 25.2 %copy-start.13 = (bf16[2048]{0:T(1024)(128)(2,1)S(1)}, bf16[2048]{0:T(1024)(128)(2,1)}, u32[]{:S(2)}) copy-start(bf16[2048]{0:T(1024)(128)(2,1)} %param.27) | copy-start | bytes 12292
  52.9 25.4 %copy-start.15 = (bf16[512]{0:T(512)(128)(2,1)S(1)}, bf16[512]{0:T(512)(128)(2,1)}, u32[]{:S(2)}) copy-start(bf16[512]{0:T(512)(128)(2,1)} %param.24) | copy-start | bytes 3076
  53.0 25.4 %copy-start.16 = (bf16[512]{0:T(512)(128)(2,1)S(1)}, bf16[512]{0:T(512)(128)(2,1)}, u32[]{:S(2)}) copy-start(bf16[512]{0:T(512)(128)(2,1)} %param.25) | copy-start | bytes 3076
  53.0 25.5 %copy-start.17 = (bf16[512]{0:T(512)(128)(2,1)S(1)}, bf16[512]{0:T(512)(128)(2,1)}, u32[]{:S(2)}) copy-start(bf16[512]{0:T(512)(128)(2,1)} %param.29) | copy-start | bytes 3076
  53.0 25.5 %copy-start.12 = (s32[1,1024]{1,0:T(1,128)S(1)}, s32[1,1024]{1,0:T(1,128)}, u32[]{:S(2)}) copy-start(s32[1,1024]{1,0:T(1,128)} %seg_ref.1) | copy-start | bytes 12292
  78.1 20.8 %copy-start.3 = (bf16[1024,512]{1,0:T(8,128)(2,1)S(1)}, bf16[1024,512]{1,0:T(8,128)(2,1)}, u32[]{:S(2)}) copy-start(bf16[1024,512]{1,0:T(8,128)(2,1)} %x_ref.3) | copy-start | bytes 3145732
  78.5 1.1 copy-start.4
  101.1 1.6 copy-start.19
  102.7 6.7 %copy-start.7 = (bf16[1024,512]{1,0:T(8,128)(2,1)S(1)}, bf16[1024,512]{1,0:T(8,128)(2,1)}, u32[]{:S(2)}) copy-start(bf16[1024,512]{1,0:T(8,128)(2,1)} %param.17) | copy-start | bytes 3145732
  102.7 6.7 %copy-start.18 = (bf16[4,512,512]{2,1,0:T(8,128)(2,1)S(1)}, bf16[4,512,512]{2,1,0:T(8,128)(2,1)}, u32[]{:S(2)}) copy-start(bf16[4,512,512]{2,1,0:T(8,128)(2,1)} %get-tuple-element.48) | copy-start | bytes 6291460
  124.6 2.6 copy-start.6
  127.1 3.3 %copy-start.2 = (f32[1024,512]{1,0:T(8,128)}, f32[1024,512]{1,0:T(8,128)S(1)}, u32[]{:S(2)}) copy-start(f32[1024,512]{1,0:T(8,128)S(1)} %get-tuple-element.111.resid_ref) | copy-start | bytes 6291460
  127.1 1.6 copy-start.20
  128.7 2.6 copy-start.21
  154.1 41.4 %collective-permute-start.1 = (bf16[512,1152]{1,0:T(8,128)(2,1)}, bf16[512,1152]{1,0:T(8,128)(2,1)S(1)}, u32[]{:S(2)}, u32[]{:S(2)}) collective-permute-start(bf16[512,1152]{1,0:T(8,128)(2,1)} %get-tuple-element.56), channel_id=1, source_target_pairs={{0,2},{1,3},{2,0},{3,1},{4,6},{5,7},{6,4},{7,5},{8,10},{9,11},{10,... | collective-permute-start | bytes 3538952 | tf_op jit(solution)/shard_map/ppermute | solution.py:895
  189.2 6.2 %copy-start.11 = (f32[4096]{0:T(1024)}, f32[4096]{0:T(1024)S(1)}, u32[]{:S(2)}) copy-start(f32[4096]{0:T(1024)S(1)} %constant_dynamic-update-slice_fusion) | copy-start | bytes 49156
  195.5 1.0 copy-start.5
  196.5 71.5 %copy-start.1 = (bf16[64,3,128]{2,0,1:T(8,128)(2,1)S(1)}, bf16[64,3,128]{2,0,1:T(8,128)(2,1)}, u32[]{:S(2)}) copy-start(bf16[64,3,128]{2,0,1:T(8,128)(2,1)} %param.20) | copy-start | bytes 147460
  256.9 9.1 %copy-start.10 = (f32[64,128]{1,0:T(8,128)S(1)}, f32[64,128]{1,0:T(8,128)}, u32[]{:S(2)}) copy-start(f32[64,128]{1,0:T(8,128)} %get-tuple-element.60) | copy-start | bytes 98308
  256.9 9.7 %copy-start.9 = (f32[64,512]{1,0:T(8,128)S(1)}, f32[64,512]{1,0:T(8,128)}, u32[]{:S(2)}) copy-start(f32[64,512]{1,0:T(8,128)} %get-tuple-element.152) | copy-start | bytes 393220
  256.9 10.4 %copy-start.8 = (f32[64,512]{1,0:T(8,128)S(1)}, f32[64,512]{1,0:T(8,128)}, u32[]{:S(2)}) copy-start(f32[64,512]{1,0:T(8,128)} %get-tuple-element.63) | copy-start | bytes 393220

commit v6 on v5

--- a/solution.py
+++ b/solution.py
@@ -375,6 +375,7 @@
     for part in range(parts):
         mine = x_ref.at[pl.ds(part * step, step)]
         sent.append(push(mine, rows_of(me, part), sy.at[part], ry.at[part], {"tp": across}))
+    send_hop(0, 1)
     for g in (1, 2, 3):
         send_hop(g, 0)
     for part in range(parts):
@@ -389,7 +390,7 @@
     waves = sorted(
         ((hop + g, g, hop) for hop in range(1, len(hops)) for g in range(4)), key=lambda w: (w[0], w[1])
     )
-    for _, g, hop in waves:
+    for _, g, hop in waves[1:2]:
         send_hop(g, hop)
     for k, peer in enumerate((across, far, side)):
         awaited(segs_ref.at[peer], sg.at[k], rg.at[k], {"tp": peer}).wait_recv()
@@ -397,9 +398,23 @@
         awaited(rows_of(side, part), ss.at[part], rs.at[part], {"tp": side}).wait_recv()
     for copy in kept:
         copy.wait()
+    gain, shift = gain_ref[...].astype(f32), shift_ref[...].astype(f32)
+
+    def norm(owner, part):
+        span = pl.ds(pl.multiple_of(owner * rows + part * step, step), step)
+        x = x_all[span, :].astype(f32)
+        centred = x - jnp.mean(x, axis=-1, keepdims=True)
+        inverse = lax.rsqrt(jnp.mean(centred * centred, axis=-1, keepdims=True) + epsilon)
+        normed_s[span, :] = (centred * inverse * gain + shift).astype(bf16)
+
+    def norm_near(k, carry):
+        norm(me + lax.rem(k, 2) * (side - me), k // 2)
+        return carry
+
+    lax.fori_loop(0, 2 * parts, norm_near, 0)
+    for _, g, hop in waves[2:]:
+        send_hop(g, hop)
     end_hops(0)
-
-    gain, shift = gain_ref[...].astype(f32), shift_ref[...].astype(f32)
     bias_at = pl.ds(pl.multiple_of(me * width, width), width)
     query_bias = bias_ref[0:1, bias_at].astype(f32)
     value_bias = bias_ref[1:2, bias_at].astype(f32)
@@ -423,11 +438,7 @@
     def compute(owner, part):
         row = pl.multiple_of(owner * rows + part * step, step)
         span = pl.ds(row, step)
-        x = x_all[span, :].astype(f32)
-        centred = x - jnp.mean(x, axis=-1, keepdims=True)
-        inverse = lax.rsqrt(jnp.mean(centred * centred, axis=-1, keepdims=True) + epsilon)
-        normed = (centred * inverse * gain + shift).astype(bf16)
-        normed_s[span, :] = normed
+        normed = normed_s[span, :]
         weights = f0[...].reshape(shards * f0.shape[1], 3 * width)
         projected = dot_n(normed, weights)
         queries = ((projected[:, 0:width] + query_bias).astype(bf16).astype(f32) * HD ** (-0.5)).astype(bf16)
@@ -464,6 +475,10 @@
         @pl.when((distant == 1) & (second == 1))
         def _():
             awaited(rows_of(far, part), sf.at[part], rf.at[part], {"tp": side}).wait_recv()
+
+        @pl.when(distant == 1)
+        def _():
+            norm(across + second * (far - across), part)
 
         first = me + distant * (across - me)
         compute(first + second * (side - me + distant * (far - across - side + me)), part)
@@ -561,7 +576,7 @@
         [jax.ShapeDtypeStruct((4, rows // 4, width), x.dtype)]
         + [jax.ShapeDtypeStruct((4, own.shape[0], w), own.dtype) for w in widths],
         [in_vmem()] * 3,
-        [in_vmem()] * 4,
+        [in_vmem()] + [anywhere()] * 3,
         [dma((4,)), dma((4,)), dma((2, 3)), dma((2, 3)), dma((7,))],
         60 << 20,
         x,
@@ -571,7 +586,7 @@
 
 
 def exchange_grad_kernel(
-    x_ref, g0, g1, g2, out_ref, kept_ref, over_ref, sems, rems, ws, wr, own, *boxes
+    x_ref, g0, g1, g2, out_ref, kept_ref, over_ref, sems, rems, ws, wr, own, loads, *boxes
 ):
     me, side, across, far = quad()
     greet([{"tp": side}, {"tp": across}, {"tp": far}])
@@ -581,8 +596,16 @@
     def slot(owner):
         return out_ref.at[pl.ds(pl.multiple_of(owner * rows, rows), rows)]
 
+    grads = (g0, g1, g2)
+    count = len(grads)
+    own_bufs = boxes[2 * count :]
+    loading = []
+    for n, grad in enumerate(grads):
+        for k in (0, 1):
+            loading.append(pltpu.make_async_copy(grad.at[2 * k], own_bufs[2 * n + k], loads.at[n, k]))
+    for copy in loading:
+        copy.start()
     sent = [push(x_ref.at[k], slot(me), sems.at[k], rems.at[k], {"tp": peers[k]}) for k in (3, 2)]
-    grads = (g0, g1, g2)
     folded = []
     for n, grad in enumerate(grads):
         folded.append(push(grad.at[3], boxes[2 * n + 1], ws.at[1, n], wr.at[1, n], {"tp": side}))
@@ -594,10 +617,12 @@
     for n, grad in enumerate(grads):
         cols = slice(at, at + grad.shape[2])
         at += grad.shape[2]
+        loading[2 * n].wait()
+        loading[2 * n + 1].wait()
         folded[2 * n].wait()
-        over_ref[:, cols] = (grad[2].astype(f32) + boxes[2 * n + 1][...].astype(f32)).astype(bf16)
+        over_ref[:, cols] = (own_bufs[2 * n + 1][...].astype(f32) + boxes[2 * n + 1][...].astype(f32)).astype(bf16)
         folded[2 * n + 1].wait()
-        kept_ref[:, cols] = (grad[0].astype(f32) + boxes[2 * n][...].astype(f32)).astype(bf16)
+        kept_ref[:, cols] = (own_bufs[2 * n][...].astype(f32) + boxes[2 * n][...].astype(f32)).astype(bf16)
     keep.wait()
     for k, peer in ((3, far), (2, across), (1, side)):
         awaited(slot(peer), sems.at[k], rems.at[k], {"tp": peer}).wait_recv()
@@ -617,9 +642,9 @@
         "exchange_grad",
         number,
         [jax.ShapeDtypeStruct((4 * rows, width), x.dtype), piece, piece],
-        [in_vmem()] * 4,
+        [in_vmem()] + [anywhere()] * 3,
         [in_vmem()] * 3,
-        [dma((4,)), dma((4,)), dma((2, 3)), dma((2, 3)), dma] + boxes,
+        [dma((4,)), dma((4,)), dma((2, 3)), dma((2, 3)), dma, dma((3, 2))] + boxes * 2,
         60 << 20,
         x,
         *grads,
@@ -627,16 +652,21 @@
 
 
 def leave_kernel(
-    grad_ref, normed_ref, w_ref, kept_ref, came_ref, early_ref, x_ref, gain_ref, resid_ref,
+    grad_ref, normed_in, w_ref, kept_ref, came_ref, early_ref, x_in, gain_ref, resid_in,
     input_ref, s0, s1, s2, s3, early_out, late_out,
     rows_ref, far_out, own_out, sum_buf, side_far, side_own, over, dw_acc, cols_ref,
     late_ref, early_mid, late_mid, early_one, early_two, late_one, late_two,
+    normed_ref, x_ref, resid_ref, loads,
     sa, ra, sb, rb, sy, ry, sw, rw, se, re, sl, rl, se2, re2, sl2, rl2, *bufs, parts, hops
 ):
     me, side, across, far = quad()
     rows = rows_ref.shape[0]
     step = rows // parts
     shard, shards = lax.axis_index("fsdp"), early_two.shape[0]
+    pairs = ((normed_in, normed_ref), (x_in, x_ref), (resid_in, resid_ref))
+    loading = [pltpu.make_async_copy(a, b, loads.at[n]) for n, (a, b) in enumerate(pairs)]
+    for copy in loading:
+        copy.start()
     barrier = pltpu.get_barrier_semaphore()
     for peer in (side, across, far):
         pl.semaphore_signal(barrier, inc=1, device_id={"tp": peer}, device_id_type=MESH)
@@ -774,17 +804,8 @@
         awaited(sum_buf.at[here], sy.at[part], ry.at[part], {"tp": across}).wait_send()
         return carry
 
-    tp_send(early_ref, early_one, se, re)
-    lax.fori_loop(0, parts, give_far, 0)
-    begin(0)
-    hop_send(0, 0)
-    tp_sum(early_mid, early_one, se, re)
-    fsdp_send(early_mid, early_two, se2, re2)
-    lax.fori_loop(0, parts, give_over, 0)
-    for g in (1, 2):
-        begin(g)
-        hop_send(g, 0)
     chunk = 512
+    steps = grad_ref.shape[0] // chunk
     dw_acc[...] = jnp.zeros_like(dw_acc)
     cols_ref[...] = jnp.zeros_like(cols_ref)
     ones = jnp.ones((8, chunk), bf16)
@@ -798,9 +819,24 @@
         cols_ref[...] += dot_n(ones, g)
         return carry
 
-    lax.fori_loop(0, grad_ref.shape[0] // chunk, weight_grad, 0)
+    tp_send(early_ref, early_one, se, re)
+    lax.fori_loop(0, parts, give_far, 0)
+    for g in (0, 1):
+        begin(g)
+        hop_send(g, 0)
+    lax.fori_loop(0, parts, give_over, 0)
+    begin(2)
+    hop_send(2, 0)
+    for copy in loading:
+        copy.wait()
+    lax.fori_loop(0, steps // 2, weight_grad, 0)
+    hop_add(0, 0)
+    lax.fori_loop(steps // 2, steps, weight_grad, 0)
     current[3][...] = dw_acc[...].astype(bf16).reshape(current[3].shape)
     hop_send(3, 0)
+    tp_sum(early_mid, early_one, se, re)
+    fsdp_send(early_mid, early_two, se2, re2)
+    hop_add(1, 0)
     late_ref[...] = jnp.zeros_like(late_ref)
     wide = cols_ref.shape[1] // 3
     qv_at = pl.ds(pl.multiple_of(me * wide, wide), wide)
@@ -808,12 +844,16 @@
     late_ref[3:4, qv_at] = cols_ref[0:1, 2 * wide : 3 * wide]
     lax.fori_loop(0, parts, give_own, 0)
     order = sorted(((k + g, g, k) for g in range(4) for k in range(count)), key=lambda w: (w[0], w[1]))
-    for n, (_, g, k) in enumerate(order):
+    order = [(g, k) for _, g, k in order if (g, k) not in ((0, 0), (1, 0))]
+    lax.fori_loop(0, parts, take_own, 0)
+    taken = {len(order) * share // 10: span for share, span in ((6, (0, 2)), (7, (2, 3)), (9, (3, 4)))}
+    for n, (g, k) in enumerate(order):
+        if n in taken:
+            first, last = taken[n]
+            lax.fori_loop(first * parts // 4, last * parts // 4, take_over, 0)
+        if n == len(order) - 1:
+            tp_send(late_ref, late_one, sl, rl)
         hop_add(g, k)
-        if n == len(order) // 2:
-            lax.fori_loop(0, parts, take_own, 0)
-    lax.fori_loop(0, parts, take_over, 0)
-    tp_send(late_ref, late_one, sl, rl)
     fsdp_sum(early_mid, early_out, early_two, se2, re2)
     tp_sum(late_mid, late_one, sl, rl)
     fsdp_send(late_mid, late_two, sl2, rl2)
@@ -843,13 +883,15 @@
         [jax.ShapeDtypeStruct((rows, width), bf16)]
         + [jax.ShapeDtypeStruct((shard, n), f32) for n in widths]
         + [jax.ShapeDtypeStruct(early.shape, f32), jax.ShapeDtypeStruct(late, f32)],
-        [in_vmem()] * 9,
+        [in_vmem(), anywhere()] + [in_vmem()] * 4 + [anywhere(), in_vmem(), anywhere()],
         [in_vmem()] * 7,
         [pltpu.VMEM((rows, width), f32)]
         + [pltpu.VMEM((rows, width), bf16)] * 6
         + [pltpu.VMEM((width, grad.shape[1]), f32), pltpu.VMEM((8, grad.shape[1]), f32)]
         + [pltpu.VMEM(late, f32), pltpu.VMEM(early.shape, f32), pltpu.VMEM(late, f32)]
         + [pltpu.VMEM((n, *shape), f32) for shape in (early.shape, late) for n in (4, shards)]
+        + [pltpu.VMEM(v.shape, v.dtype) for v in (normed, x, resid)]
+        + [dma((3,))]
         + [dma((parts,))] * 6
         + [dma((4, count))] * 2
         + [dma((3,)), dma((4,))] * 2
@@ -868,6 +910,46 @@
         gain,
         resid,
     )
+
+
+def finish_kernel(
+    rows_in, fc_in, proj_in, out_in, qkv_in, early_in, late_in,
+    rows_ref, fc_ref, proj_ref, out_ref, qkv_ref, qv_ref, *vectors
+):
+    rows_ref[...] = rows_in[...]
+    fc_ref[...] = fc_in[...]
+    proj_ref[...] = proj_in[...]
+    out_ref[...] = out_in[...]
+    width = qkv_ref.shape[2]
+    for n in range(3):
+        qkv_ref[n] = qkv_in[:, n * width : (n + 1) * width]
+    qv_ref[...] = late_in[2:4, :]
+    lanes = early_in.shape[1]
+    for n, ref in enumerate(vectors[0:2]):
+        for row in range(ref.shape[0]):
+            ref[row : row + 1, :] = late_in[n : n + 1, row * lanes : (row + 1) * lanes]
+    at = 0
+    for ref in vectors[2:]:
+        ref[...] = early_in[at : at + ref.shape[0], :]
+        at += ref.shape[0]
+
+
+def finish(rows, fc, proj, out, qkv, early, late, sizes):
+    lanes = early.shape[1]
+    shapes = [rows, fc, proj, out]
+    outs = [jax.ShapeDtypeStruct(v.shape, v.dtype) for v in shapes]
+    outs.append(jax.ShapeDtypeStruct((3, qkv.shape[0], qkv.shape[1] // 3), f32))
+    outs.append(jax.ShapeDtypeStruct((2, late.shape[1]), f32))
+    outs += [jax.ShapeDtypeStruct((n // lanes, lanes), f32) for n in (late.shape[1], late.shape[1], *sizes)]
+    rows, fc, proj, out, qkv, qv, *vectors = pl.pallas_call(
+        finish_kernel,
+        out_shape=outs,
+        in_specs=[in_vmem()] * 7,
+        out_specs=[in_vmem()] * len(outs),
+        cost_estimate=pl.CostEstimate(flops=0, bytes_accessed=3 << 20, transcendentals=0),
+        name="finish",
+    )(rows, fc, proj, out, qkv, early, late)
+    return rows, fc, proj.T, out.T, qkv.transpose(1, 0, 2), qv, [v.reshape(-1) for v in vectors]
 
 
 def flip(axis, bit):
@@ -999,16 +1081,18 @@
         grad_hidden,
         3,
     )
-    proj_w_grad = proj_w_grad.T
-    out_w_grad = out_w_grad.T
-    qkv_grad = qkv_grad.reshape(shard_rows, 3, head_cols)
-    totals, found, at = early_sums.reshape(-1), [], 0
-    for vector in early:
-        found.append(totals[at : at + vector.shape[0]])
-        at += vector.shape[0]
-    out_bias_grad, second_gain_grad, second_shift_grad, fc_bias_grad, proj_bias_grad = found
-    first_gain_grad, first_shift_grad = late_sums[0], late_sums[1]
-    qv_bias_grad = late_sums[2:4]
+    input_grad, fc_w_grad, proj_w_grad, out_w_grad, qkv_grad, qv_bias_grad, vectors = finish(
+        input_grad,
+        fc_w_grad,
+        proj_w_grad,
+        out_w_grad,
+        qkv_grad,
+        early_sums,
+        late_sums,
+        [vector.shape[0] for vector in early],
+    )
+    first_gain_grad, first_shift_grad, out_bias_grad, second_gain_grad, second_shift_grad = vectors[0:5]
+    fc_bias_grad, proj_bias_grad = vectors[5:7]
 
     return (
         layer_out,

time: 269 us -> 254 us (0.944); the launches traced: 268 us -> 249 us
  local copies, waits for them, and re-layouts: 19.6 us -> 8.48 us
  Pallas kernels: 203 us -> 195 us
    pallas_call x4, Pallas kernels: 145 us -> 134 us  [comm_call(): pl.pallas_call(kernel, out_shape=out_shape, in_specs=in_specs, out_specs=...]
    unnamed x54 -> x43, local copies, waits for them, and re-layouts: 9.96 us -> 4.2 us
    slice x4 -> x0, local copies, waits for them, and re-layouts: 5.3 us -> none  [the longest x2 2.65 us: local(): found.append(totals[at:at + vector.shape[0]])]
  transfers between devices with their start and end apart: 2 -> 2, of which waited for: 0 -> 0; matrix products, arithmetic and copies ran while one was open for 4% -> 4% of each run, Pallas kernels for 22% -> 24%
where the time goes in v6:
time: 254 us; the launch traced here: 249 us
  Pallas kernels  195 us (77%)
  matrix products  37.2 us (15%)
  local copies, waits for them, and re-layouts  8.48 us (3%)
  other arithmetic  5.2 us (2%)
    pallas_call x4, Pallas kernels, comm_call(): pl.pallas_call(kernel, out_shape=out_shape, in_specs=in_specs, out_specs=...  134 us
    pallas_call x1, Pallas kernels, attend_back(): pl.pallas_call(functools.partial(attend_back_kernel, size=size, blocks=ro...  33.5 us
    pallas_call x1, Pallas kernels, attend(): pl.pallas_call(functools.partial(attend_kernel, size=size, blocks=rows //...  25.2 us
    dot_general x1, matrix products, local(): jnp.einsum('sd,tdf->tsf', mlp_in, fc_full, preferred_element_type=f32)  6.74 us
    dot_general x1, matrix products, local(): jnp.einsum('sd,tdf->tsf', out_grad, proj_full, preferred_element_type=f32)  6.43 us
    dot_general x1, matrix products, local(): jnp.einsum('tsf,tdf->sd', act_low, proj_full, preferred_element_type=f32)  6.22 us
  transfers between devices with their start and end apart: 2, of which 0 were waited for; matrix products, arithmetic and copies ran while one was open for 4% of the time, Pallas kernels for 24%

profile of v6, /device:TPU:0, one launch (start us, length us, event | category | flops | bytes accessed | tf_op | source)
XLA Modules:
  0.0 249.4 jit_solution(11645173068272441073)
XLA Ops:
  0.7 1.3 broadcast_in_dim.4.gain_ref
  2.6 1.3 broadcast_in_dim.5.shift_ref
  3.8 41.9 %enter.1 = (bf16[4096,512]{1,0:T(8,128)(2,1)}, s32[4,1,1024]{2,1,0:T(1,128)}, bf16[2,4096,128]{2,1,0:T(8,128)(2,1)}, bf16[2,4096,128]{2,1,0:T(8,128)(2,1)}, bf16...) custom-call(bf16[1024,512]{1,0:T(8,128)(2,1)} %x_in.1, ...), custom_call_target="tpu_custom_call" | custom-call | bytes 62914560 | tf_op jit(solution)/shard_map/enter/pallas_call | solution.py:279
  45.7 1.3 collective-permute-start
  48.5 0.9 convert_reduce_fusion.3
  50.0 25.2 %attend.1 = (bf16[4096,128]{1,0:T(8,128)(2,1)}, bf16[2,4096,128]{2,1,0:T(8,128)(2,1)}) custom-call(s32[8]{0:T(128)} %compare_select_fusion.low_ref, bf16[2,4096,128]{2,1,0:T(8,128)(2,1)} %get-tuple-element.53.qa_ref, bf16[2,4096,128]{2,1,0:T(8,128)(2,1)} %get-tuple-element.54.ka_ref, bf16[2,80,4096]{2,1,0:T(8,128)(2,1)} %get-tuple-element.55.vt_ref, ...), custom_call_target="tpu_custom_call" | custom-call | flops 30064771072 | bytes 8388608 | tf_op jit(solution)/shard_map/attend/pallas_call | solution.py:126
  75.6 1.1 copy-done.4
  76.6 17.4 %exchange_out.1 = (bf16[4,1024,128]{2,1,0:T(8,128)(2,1)}, bf16[4,512,512]{2,1,0:T(8,128)(2,1)}, bf16[4,512,512]{2,1,0:T(8,128)(2,1)}, bf16[4,512,128]{2,1,0:T(8,128)(2,1)}) custom-call(bf16[4096,128]{1,0:T(8,128)(2,1)} %get-tuple-element.56.x_ref.o_ref, bf16[512,1152]{1,0:T(8,128)(2,1)} %bitcast.107, bf16[512,1152]{1,0:T(8,128)(2,1)} %copy-done.4), custom_call_target="tpu_custom_call" | custom-call | bytes 62914560 | tf_op jit(solution)/shard_map/exchange_out/pallas_call | solution.py:279
  94.0 2.2 fusion.22
  96.7 1.1 copy-done.16
  97.8 6.7 %fusion.1 = (bf16[4,1024,512]{1,2,0:T(8,128)(2,1)}, f32[4,512,1024]{2,1,0:T(8,128)S(1)}) fusion(f32[4,512]{1,0:T(4,128)S(1)} %add.72, bf16[4,512,512]{2,1,0:T(8,128)(2,1)S(1)} %copy-done.16, f32[1024,512]{1,0:T(8,128)S(1)} %get-tuple-element.98, f32[512]{0:T(512)S(1)} %convert_element_type.77, f32[512]{0:T(512)S(1)} %convert_element_type.76, ...), kind=kOutput, calls=%fused_computation.4 | convolution fusion | flops 2164785152 | bytes 16797696 | tf_op jit(solution)/shard_map/sd,tdf->tsf/dot_general | solution.py:1033
  104.6 6.4 %convert_reduce_fusion = (f32[4,512]{1,0:T(4,128)S(1)}, bf16[4,1024,512]{1,2,0:T(8,128)(2,1)S(1)}) fusion(f32[4,512,1024]{2,1,0:T(8,128)S(1)} %get-tuple-element.100, f32[4,512]{1,0:T(4,128)S(1)} %add.72, bf16[4,512,512]{2,1,0:T(8,128)(2,1)S(1)} %copy-done.15, bf16[1024,512]{1,0:T(8,128)(2,1)S(1)} %copy-done.7), kind=kOutput, calls=%fused_computation.5 | convolution fusion | flops 2174744576 | bytes 15745024 | tf_op jit(solution)/shard_map/sd,tdf->tsf/dot_general | solution.py:1044
  111.0 4.4 %fusion.2 = (f32[512]{0:T(512)S(1)}, f32[1024]{0:T(1024)S(1)}, f32[1024]{0:T(1024)S(1)}, f32[512]{0:T(512)S(1)}, f32[1024,512,1]{1,0,2:T(8,128)}) fusion(f32[1024,512]{1,0:T(8,128)S(1)} %get-tuple-element.98, f32[1024]{0:T(1024)S(1)} %add_rsqrt_fusion, f32[1024]{0:T(1024)S(1)} %broadcast_multiply_fusion.2, f32[512]{0:T(512)S(1)} %convert_element_type.76, ...), kind=kOutput, calls=%fused_computation.12 | convolution fusion | flops 2152199168 | bytes 10508288 | tf_op jit(solution)/shard_map/tsf,tdf->sd/dot_general | solution.py:1049
  115.4 4.1 %convert_bitcast_fusion.1.g0 = bf16[4,512,512]{2,1,0:T(8,128)(2,1)} fusion(bf16[4,1024,512]{1,2,0:T(8,128)(2,1)S(1)} %get-tuple-element.103, f32[1024,512]{1,0:T(8,128)S(1)} %get-tuple-element.98, f32[512]{0:T(512)S(1)} %convert_element_type.77, f32[512]{0:T(512)S(1)} %convert_element_type.76, f32[1024]{0:T(1024)S(1)} %add_rsqrt_fusion, ...), kind=kOutput, calls=%fused_computation.20 | convolution fusion | flops 2151153664 | bytes 8400896 | tf_op jit(solution)/shard_map/sd,tsf->tdf/dot_general | solution.py:1047
  119.7 2.5 %convert_reduce_fusion.2 = (f32[512]{0:T(512)S(1)}, f32[1024,512]{1,0:T(8,128)S(1)}, f32[512]{0:T(512)S(1)}) fusion(f32[1024]{0:T(1024)S(1)} %get-tuple-element.104, f32[1024,512]{1,0:T(8,128)S(1)} %get-tuple-element.98, f32[1024]{0:T(1024)S(1)} %broadcast_multiply_fusion.2, f32[1024]{0:T(1024)S(1)} %get-tuple-element.105, f32[512]{0:T(512)S(1)} %convert_element_type.76, ...), kind=kLoop, calls=%fused_computation.18 | loop fusion | flops 6814720 | bytes 7362560 | tf_op jit(solution)/shard_map/reduce_sum | solution.py:1056
  122.3 1.6 fusion.9.g2
  123.9 1.7 fusion.8.x_ref
  126.5 3.9 %convert_bitcast_fusion.g1 = bf16[4,512,512]{2,1,0:T(8,128)(2,1)} fusion(bf16[4,1024,512]{1,2,0:T(8,128)(2,1)S(1)} %copy-done.18, bf16[1024,512]{1,0:T(8,128)(2,1)S(1)} %copy-done.7), kind=kOutput, calls=%fused_computation.19 | convolution fusion | flops 2148532224 | bytes 7340032 | tf_op jit(solution)/shard_map/sd,tsf->tdf/dot_general | solution.py:1043
  130.3 17.5 %exchange_grad.1 = (bf16[4096,128]{1,0:T(8,128)(2,1)}, bf16[512,1152]{1,0:T(8,128)(2,1)}, bf16[512,1152]{1,0:T(8,128)(2,1)}) custom-call(bf16[4,1024,128]{2,1,0:T(8,128)(2,1)} %fusion.8.x_ref, bf16[4,512,512]{2,1,0:T(8,128)(2,1)} %convert_bitcast_fusion.1.g0, bf16[4,512,512]{2,1,0:T(8,128)(2,1)} %convert_bitcast_fusion.g1, bf16[4,512,128]{2,1,0:T(8,128)(2,1)} %fusion.9.g2), custom_call_target="tpu_custom_call" | custom-call | bytes 62914560 | tf_op jit(solution)/shard_map/exchange_grad/pallas_call | solution.py:279
  148.7 33.5 %attend_back.1.grad_ref = bf16[4096,384]{1,0:T(8,128)(2,1)} custom-call(s32[8]{0:T(128)} %compare_select_fusion.low_ref, bf16[2,4096,128]{2,1,0:T(8,128)(2,1)} %get-tuple-element.62.qb_ref, bf16[2,4096,128]{2,1,0:T(8,128)(2,1)} %get-tuple-element.54.ka_ref, bf16[2,4096,128]{2,1,0:T(8,128)(2,1)} %get-tuple-element.63.va_ref, ...), custom_call_target="tpu_custom_call" | custom-call | flops 51539607552 | bytes 16777216 | tf_op jit(solution)/shard_map/attend_back/pallas_call | solution.py:217
  182.3 6.2 %fusion.4 = bf16[1024,512]{1,0:T(8,128)(2,1)} fusion(f32[1024,512]{1,0:T(8,128)S(1)} %get-tuple-element.98, bf16[4,1024,512]{1,2,0:T(8,128)(2,1)} %get-tuple-element.99, bf16[4,512,512]{2,1,0:T(8,128)(2,1)} %get-tuple-element.61, f32[512]{0:T(512)S(1)} %convert_element_type.80), kind=kOutput, calls=%fused_computation.15 | convolution fusion | flops 2149056512 | bytes 9439232 | tf_op jit(solution)/shard_map/tsf,tdf->sd/dot_general | solution.py:1040
  188.5 1.0 copy-done.5
  189.5 57.2 %leave.1 = (bf16[1024,512]{1,0:T(8,128)(2,1)}, f32[64,512]{1,0:T(8,128)}, f32[64,512]{1,0:T(8,128)}, f32[64,128]{1,0:T(8,128)}, f32[64,384]{1,0:T(8,128)}, /*index=5*/f32[32,128]{1,0:T(8,128)}, f32[4,512]{1,0:T(4,128)}) custom-call(bf16[4096,384]{1,0:T(8,128)(2,1)} %attend_back.1.grad_ref, bf16[4096,512]{1,0:T(8,128)(2,1)} %get-tuple-element.66.normed_in, ...), custom_call_target="tpu_custom_call" | custom-call | bytes 62914560 | tf_op jit(solution)/shard_map/leave/pallas_call | solution.py:279
  246.7 2.5 %finish.1 = (bf16[1024,512]{1,0:T(8,128)(2,1)}, f32[64,512]{1,0:T(8,128)}, f32[64,512]{1,0:T(8,128)}, f32[64,128]{1,0:T(8,128)}, f32[3,64,128]{2,1,0:T(8,128)}, ...) custom-call(bf16[1024,512]{1,0:T(8,128)(2,1)} %get-tuple-element.70., ...), custom_call_target="tpu_custom_call" | custom-call | bytes 3145728 | tf_op jit(solution)/shard_map/finish/pallas_call | solution.py:944
  (67 shorter events, 5.3 us)
Async XLA Ops:
  0.6 1.3 copy-start
  45.7 29.8 %collective-permute-start = (bf16[512,1152]{1,0:T(8,128)(2,1)}, bf16[512,1152]{1,0:T(8,128)(2,1)S(1)}, u32[]{:S(2)}, u32[]{:S(2)}) collective-permute-start(bf16[512,1152]{1,0:T(8,128)(2,1)} %bitcast.106), channel_id=1, source_target_pairs={{0,2},{1,3},{2,0},{3,1},{4,6},{5,7},{6,4},{7,5},{8,10},{9,11},{10,... | collective-permute-start | bytes 3538952 | tf_op jit(solution)/shard_map/ppermute | solution.py:977
  50.0 25.2 %copy-start.11 = (bf16[512]{0:T(512)(128)(2,1)S(1)}, bf16[512]{0:T(512)(128)(2,1)}, u32[]{:S(2)}) copy-start(bf16[512]{0:T(512)(128)(2,1)} %param.23) | copy-start | bytes 3076
  50.0 25.2 %copy-start.10 = (bf16[2048]{0:T(1024)(128)(2,1)S(1)}, bf16[2048]{0:T(1024)(128)(2,1)}, u32[]{:S(2)}) copy-start(bf16[2048]{0:T(1024)(128)(2,1)} %param.27) | copy-start | bytes 12292
  50.0 25.4 %copy-start.12 = (bf16[512]{0:T(512)(128)(2,1)S(1)}, bf16[512]{0:T(512)(128)(2,1)}, u32[]{:S(2)}) copy-start(bf16[512]{0:T(512)(128)(2,1)} %param.24) | copy-start | bytes 3076
  50.0 25.5 %copy-start.13 = (bf16[512]{0:T(512)(128)(2,1)S(1)}, bf16[512]{0:T(512)(128)(2,1)}, u32[]{:S(2)}) copy-start(bf16[512]{0:T(512)(128)(2,1)} %param.25) | copy-start | bytes 3076
  50.0 25.5 %copy-start.14 = (bf16[512]{0:T(512)(128)(2,1)S(1)}, bf16[512]{0:T(512)(128)(2,1)}, u32[]{:S(2)}) copy-start(bf16[512]{0:T(512)(128)(2,1)} %param.29) | copy-start | bytes 3076
  50.0 25.5 %copy-start.9 = (s32[1,1024]{1,0:T(1,128)S(1)}, s32[1,1024]{1,0:T(1,128)}, u32[]{:S(2)}) copy-start(s32[1,1024]{1,0:T(1,128)} %seg_ref.1) | copy-start | bytes 12292
  75.2 18.9 %copy-start.3 = (bf16[1024,512]{1,0:T(8,128)(2,1)S(1)}, bf16[1024,512]{1,0:T(8,128)(2,1)}, u32[]{:S(2)}) copy-start(bf16[1024,512]{1,0:T(8,128)(2,1)} %x_in.1) | copy-start | bytes 3145732
  75.5 1.1 copy-start.4
  96.2 1.6 copy-start.16
  97.8 6.7 %copy-start.7 = (bf16[1024,512]{1,0:T(8,128)(2,1)S(1)}, bf16[1024,512]{1,0:T(8,128)(2,1)}, u32[]{:S(2)}) copy-start(bf16[1024,512]{1,0:T(8,128)(2,1)} %param.17) | copy-start | bytes 3145732
  97.8 6.7 %copy-start.15 = (bf16[4,512,512]{2,1,0:T(8,128)(2,1)S(1)}, bf16[4,512,512]{2,1,0:T(8,128)(2,1)}, u32[]{:S(2)}) copy-start(bf16[4,512,512]{2,1,0:T(8,128)(2,1)} %get-tuple-element.61) | copy-start | bytes 6291460
  119.7 2.6 %copy-start.6 = (bf16[4,1024,128]{2,1,0:T(8,128)(2,1)S(1)}, bf16[4,1024,128]{2,1,0:T(8,128)(2,1)}, u32[]{:S(2)}) copy-start(bf16[4,1024,128]{2,1,0:T(8,128)(2,1)} %get-tuple-element.58) | copy-start | bytes 3145732
  122.3 3.3 %copy-start.2 = (f32[1024,512]{1,0:T(8,128)}, f32[1024,512]{1,0:T(8,128)S(1)}, u32[]{:S(2)}) copy-start(f32[1024,512]{1,0:T(8,128)S(1)} %get-tuple-element.95.resid_in) | copy-start | bytes 6291460
  122.3 1.6 copy-start.17
  123.9 2.6 %copy-start.18 = (bf16[4,1024,512]{1,2,0:T(8,128)(2,1)S(1)}, bf16[4,1024,512]{1,2,0:T(8,128)(2,1)}, u32[]{:S(2)}) copy-start(bf16[4,1024,512]{1,2,0:T(8,128)(2,1)} %get-tuple-element.99) | copy-start | bytes 12582916
  147.9 40.6 %collective-permute-start.1 = (bf16[512,1152]{1,0:T(8,128)(2,1)}, bf16[512,1152]{1,0:T(8,128)(2,1)S(1)}, u32[]{:S(2)}, u32[]{:S(2)}) collective-permute-start(bf16[512,1152]{1,0:T(8,128)(2,1)} %get-tuple-element.69), channel_id=1, source_target_pairs={{0,2},{1,3},{2,0},{3,1},{4,6},{5,7},{6,4},{7,5},{8,10},{9,11},{10,... | collective-permute-start | bytes 3538952 | tf_op jit(solution)/shard_map/ppermute | solution.py:977
  182.2 6.2 %copy-start.8 = (f32[4096]{0:T(1024)}, f32[4096]{0:T(1024)S(1)}, u32[]{:S(2)}) copy-start(f32[4096]{0:T(1024)S(1)} %constant_dynamic-update-slice_fusion) | copy-start | bytes 49156
  188.5 1.0 copy-start.5
  189.5 59.7 %copy-start.1 = (bf16[64,3,128]{2,0,1:T(8,128)(2,1)S(1)}, bf16[64,3,128]{2,0,1:T(8,128)(2,1)}, u32[]{:S(2)}) copy-start(bf16[64,3,128]{2,0,1:T(8,128)(2,1)} %param.20) | copy-start | bytes 147460
